TPU v7x, 256 devices: a whole 4x4x8 slice. The times are simulated.
256 devices in a mesh: seq: 64 (over z, x, core), head: 4 (over y).
Axes of the slice: x: 4, y: 4, z: 8, core: 2. Of those that a mesh axis runs over, the one named last changes fastest.
Arguments:
- query_vectors: bfloat16 [32768, 2048], P('seq', 'head'), may hold values from -6 to 6
- key_vectors: bfloat16 [32768, 2048], P('seq', 'head'), may hold values from -6 to 6
- value_vectors: bfloat16 [32768, 4096], P('seq', 'head'), may hold values from -6 to 6
- query_gain: float32 [16, 32768], P('head', 'seq'), may hold values from 0.25 to 1
- level_gain: float32 [16, 21], P('head'), may hold values from 0.25 to 2
- out_weight: bfloat16 [4096, 2304], P('head'), may hold values from -0.09375 to 0.09375
- out_grad: bfloat16 [32768, 2304], P('seq'), may hold values from -6 to 6
Outputs:
- layer_out: bfloat16 [32768, 2304], P(('seq', 'head'))
- grad_queries: bfloat16 [32768, 2048], P('seq', 'head')
- grad_keys: bfloat16 [32768, 2048], P('seq', 'head')
- grad_values: bfloat16 [32768, 4096], P('seq', 'head')
All inputs are finite; a program needn't handle non-finite values.
Results may differ from a plain program's by a relative error of at most 0.012.
Values may be sent and summed in bfloat16 or wider, within the bound.
No kernel may reach another device: no remote copies, remote signals or barrier semaphores. Data moves between devices by JAX's collectives and lax.ppermute only.
A program may use at most 128 MiB of HBM per device.

v0:
```python
import jax
import jax.numpy as jnp
from jax import lax
from jax.sharding import PartitionSpec as P


def from_partner(value, axis, bit):
    mask = 2**bit
    pairs = [(source, source ^ mask) for source in range(lax.axis_size(axis))]
    return lax.ppermute(value, axis, pairs)


def split_up(array, dim, count):
    shape = array.shape
    pieces = array.reshape(*shape[:dim], count, shape[dim] // count, *shape[dim + 1 :])
    return jnp.moveaxis(pieces, dim, 0)


def sent_and_summed(array, axis, dim):
    pieces = split_up(array, dim, lax.axis_size(axis))
    arrived = lax.all_to_all(pieces, axis, split_axis=0, concat_axis=0, tiled=True)
    return arrived.astype(jnp.float32).sum(axis=0)


def bit_length(numbers):
    powers = jnp.left_shift(jnp.int32(1), jnp.arange(31, dtype=jnp.int32))
    return jnp.sum((numbers[..., None] >= powers).astype(jnp.int32), axis=-1)


def level_weights_of(level_gain):
    levels = jnp.arange(level_gain.shape[1], dtype=jnp.int32)
    decline = jnp.exp2(-0.5 * (levels - 1).astype(jnp.float32))
    factor = jnp.where(levels == 0, jnp.float32(1.0), decline)
    return level_gain * factor[None, :]


def local_table(level_weights, block_rows):
    tokens = jnp.arange(block_rows, dtype=jnp.int32)
    pair_level = bit_length(tokens[:, None] ^ tokens[None, :])
    causal = (tokens[None, :] <= tokens[:, None]).astype(jnp.float32)
    weight_table = jnp.zeros((level_weights.shape[0], block_rows, block_rows), jnp.float32)
    for level_index in range(block_rows.bit_length()):
        weight_table = weight_table + jnp.where(
            pair_level == level_index,
            level_weights[:, level_index][:, None, None],
            jnp.float32(0.0),
        )
    return weight_table * causal


def exchange_levels(key_running_state, query_running_state, level_weights, shift_bits):
    seq_count = lax.axis_size("seq")
    bit_count = seq_count.bit_length() - 1
    seq_index = lax.axis_index("seq")
    key_group = key_running_state
    query_group = query_running_state
    earlier_window_state = jnp.zeros(key_running_state.shape, jnp.float32)
    later_window_state = jnp.zeros(query_running_state.shape, jnp.float32)
    for bit_index in range(bit_count):
        other_key, other_query = from_partner((key_group, query_group), "seq", bit_index)
        upper = (seq_index >> bit_index & 1).astype(jnp.float32)
        level_scale = level_weights[:, shift_bits + 1 + bit_index][:, None, None]
        earlier_window_state = earlier_window_state + upper * level_scale * other_key
        later_window_state = later_window_state + (1.0 - upper) * level_scale * other_query
        key_group = key_group + other_key
        query_group = query_group + other_query
    return (earlier_window_state.astype(jnp.bfloat16), later_window_state.astype(jnp.bfloat16))


def near_terms(
    query_per_head,
    key_per_head,
    value_per_head,
    gradient_per_head,
    query_gain,
    weight_table,
    attention_scale,
):
    pair_weight = query_gain[:, :, None] * weight_table
    scores = (
        jnp.einsum("thk,shk->hts", query_per_head, key_per_head, preferred_element_type=jnp.float32)
        * attention_scale
    )
    near_weights = (pair_weight * scores).astype(jnp.bfloat16)
    level_mixing = jnp.einsum(
        "amc,caj->maj", near_weights, value_per_head, preferred_element_type=jnp.float32
    )
    grad_scores = jnp.einsum(
        "thv,shv->hts", gradient_per_head, value_per_head, preferred_element_type=jnp.float32
    )
    nearby_gradients = (attention_scale * pair_weight * grad_scores).astype(jnp.bfloat16)
    query_gradient = jnp.einsum(
        "xuf,fxl->uxl", nearby_gradients, key_per_head, preferred_element_type=jnp.float32
    )
    key_gradient = jnp.einsum(
        "quw,uqg->wqg", nearby_gradients, query_per_head, preferred_element_type=jnp.float32
    )
    value_gradient = jnp.einsum(
        "fpx,pfj->xfj", near_weights, gradient_per_head, preferred_element_type=jnp.float32
    )
    return (level_mixing, query_gradient, key_gradient, value_gradient)


def state_terms(
    near_parts,
    query_per_head,
    key_per_head,
    value_per_head,
    gradient_per_head,
    query_gain,
    earlier_lower_bits,
    later_lower_bits,
    attention_scale,
):
    level_mixing, query_gradient, key_gradient, value_gradient = near_parts
    level_gain_rows = query_gain.T[:, :, None]
    level_mixing = level_mixing + attention_scale * level_gain_rows * jnp.einsum(
        "sxz,xzg->sxg", query_per_head, earlier_lower_bits, preferred_element_type=jnp.float32
    )
    query_gradient = query_gradient + attention_scale * level_gain_rows * jnp.einsum(
        "gbf,bzf->gbz", gradient_per_head, earlier_lower_bits, preferred_element_type=jnp.float32
    )
    key_gradient = key_gradient + attention_scale * jnp.einsum(
        "xtl,tzl->xtz", value_per_head, later_lower_bits, preferred_element_type=jnp.float32
    )
    value_gradient = value_gradient + attention_scale * jnp.einsum(
        "mwg,wgc->mwc", key_per_head, later_lower_bits, preferred_element_type=jnp.float32
    )
    return (
        level_mixing.astype(jnp.bfloat16),
        query_gradient.astype(jnp.bfloat16),
        key_gradient.astype(jnp.bfloat16),
        value_gradient.astype(jnp.bfloat16),
    )


def on_device(
    query_vectors, key_vectors, value_vectors, query_gain, level_gain, out_weight, out_grad
):
    head_count = query_gain.shape[0]
    block_rows = query_gain.shape[1]
    key_width = query_vectors.shape[1] // head_count
    value_width = value_vectors.shape[1] // head_count
    attention_scale = key_width ** (-0.5)
    level_weights = level_weights_of(level_gain)
    weight_table = local_table(level_weights, block_rows)
    grad_mixture = lax.dot_general(
        out_grad, out_weight, (((1,), (1,)), ((), ())), preferred_element_type=jnp.float32
    ).astype(jnp.bfloat16)
    query_per_head = query_vectors.reshape(block_rows, head_count, key_width)
    key_per_head = key_vectors.reshape(block_rows, head_count, key_width)
    value_per_head = value_vectors.reshape(block_rows, head_count, value_width)
    gradient_per_head = grad_mixture.reshape(block_rows, head_count, value_width)
    key_running_state = jnp.einsum(
        "wdp,wdg->dpg", key_per_head, value_per_head, preferred_element_type=jnp.float32
    )
    scaled_by_gain = (gradient_per_head.astype(jnp.float32) * query_gain.T[:, :, None]).astype(
        jnp.bfloat16
    )
    query_running_state = jnp.einsum(
        "wdp,wdg->dpg", query_per_head, scaled_by_gain, preferred_element_type=jnp.float32
    )
    shift_bits = block_rows.bit_length() - 1
    near_parts = near_terms(
        query_per_head,
        key_per_head,
        value_per_head,
        gradient_per_head,
        query_gain,
        weight_table,
        attention_scale,
    )
    earlier_lower_bits, later_lower_bits = exchange_levels(
        key_running_state, query_running_state, level_weights, shift_bits
    )
    level_mixing, query_gradient, key_gradient, value_gradient = state_terms(
        near_parts,
        query_per_head,
        key_per_head,
        value_per_head,
        gradient_per_head,
        query_gain,
        earlier_lower_bits,
        later_lower_bits,
        attention_scale,
    )
    mixture_rows = level_mixing.reshape(block_rows, head_count * value_width)
    layer_out = sent_and_summed(
        jnp.dot(mixture_rows, out_weight, preferred_element_type=jnp.float32).astype(jnp.bfloat16),
        "head",
        0,
    ).astype(jnp.bfloat16)
    return (
        layer_out,
        query_gradient.reshape(block_rows, head_count * key_width),
        key_gradient.reshape(block_rows, head_count * key_width),
        value_gradient.reshape(block_rows, head_count * value_width),
    )


def solution(mesh):
    return jax.shard_map(
        on_device,
        mesh=mesh,
        in_specs=(
            P("seq", "head"),
            P("seq", "head"),
            P("seq", "head"),
            P("head", "seq"),
            P("head", None),
            P("head", None),
            P("seq", None),
        ),
        out_specs=(P(("seq", "head"), None), P("seq", "head"), P("seq", "head"), P("seq", "head")),
        check_vma=False,
    )
```

profile of v0, /device:TPU:1, one launch (start us, length us, event | category | flops | bytes accessed | tf_op | source)
XLA Modules:
  0.0 186.1 jit_solution(15649092405713684171)
XLA Ops:
  2.1 2.5 %fusion.12 = f32[4,128,256]{2,1,0:T(8,128)} fusion(bf16[512,4,128]{0,2,1:T(8,128)(2,1)S(1)} %bitcast.108, bf16[64,4,8,256]{3,2,1,0:T(8,128)(2,1)} %bitcast.100), kind=kOutput, calls=%fused_computation.26 | convolution fusion | flops 134217728 | bytes 2097152 | tf_op jit(solution)/shard_map/wdp,wdg->dpg/dot_general | solution.py:154
  4.6 3.2 %collective-permute-start = (f32[4,128,256]{2,1,0:T(8,128)}, f32[4,128,256]{2,1,0:T(8,128)}, u32[]{:S(2)}, u32[]{:S(2)}) collective-permute-start(f32[4,128,256]{2,1,0:T(8,128)} %fusion.12), channel_id=1, source_target_pairs={{0,4},{4,0},{8,12},{12,8},{16,20},{20,16},{24,28},{28,24},{32,36},... | collective-permute-start | bytes 1572872 | tf_op jit(solution)/shard_map/ppermute | solution.py:10
  7.8 5.9 %convolution_convert_fusion.1 = bf16[512,1024]{1,0:T(8,128)(2,1)} fusion(bf16[512,2304]{1,0:T(8,128)(2,1)S(1)} %copy-done, bf16[1024,2304]{1,0:T(8,128)(2,1)} %param.12), kind=kOutput, calls=%fused_computation.10 | convolution fusion | flops 2416443392 | bytes 8126464 | tf_op jit(solution)/shard_map/dot_general | solution.py:147
  15.3 2.6 %convolution_bitcast_fusion.3 = f32[4,128,256]{1,2,0:T(8,128)} fusion(bf16[512,4,256]{0,2,1:T(8,128)(2,1)S(1)} %bitcast.104, f32[512,4]{0,1:T(4,128)S(1)} %bitcast.115, bf16[512,512]{1,0:T(8,128)(2,1)} %param.7), kind=kOutput, calls=%fused_computation.21 | convolution fusion | flops 135790592 | bytes 2105344 | tf_op jit(solution)/shard_map/wdp,wdg->dpg/dot_general | solution.py:160
  20.2 3.2 %convert_reduce_fusion = s32[512,512]{1,0:T(8,128)S(1)} fusion(s32[512,512]{1,0:T(8,128)S(1)} %iota_xor_fusion, s32[31]{0:T(128)S(1)} %iota_shift-left_fusion), kind=kLoop, calls=%fused_computation | loop fusion | flops 24117248 | bytes 2097276 | tf_op jit(solution)/shard_map/reduce_sum | solution.py:27
  23.4 9.7 %collective-permute-done.1 = f32[4,128,256]{2,1,0:T(8,128)S(1)} collective-permute-done((f32[4,128,256]{2,1,0:T(8,128)S(1)}, f32[4,128,256]{2,1,0:T(8,128)S(1)}, u32[]{:S(2)}, u32[]{:S(2)}) %collective-permute-start.1) | collective-permute-done | bytes 524320 | tf_op jit(solution)/shard_map/ppermute | solution.py:10
  37.8 9.3 %collective-permute-done.2 = f32[4,128,256]{2,1,0:T(8,128)S(1)} collective-permute-done((f32[4,128,256]{2,1,0:T(8,128)S(1)}, f32[4,128,256]{2,1,0:T(8,128)S(1)}, u32[]{:S(2)}, u32[]{:S(2)}) %collective-permute-start.2) | collective-permute-done | bytes 524320 | tf_op jit(solution)/shard_map/ppermute | solution.py:10
  47.4 7.4 %multiply_convert_fusion = bf16[4,512,512]{2,1,0:T(8,128)(2,1)} fusion(bf16[512,4,256]{0,2,1:T(8,128)(2,1)S(1)} %bitcast.105, bf16[64,4,8,256]{3,2,1,0:T(8,128)(2,1)S(1)} %bitcast.101, f32[512,512]{1,0:T(8,128)S(1)} %get-tuple-element.44, f32[4]{0:T(128)S(1)} %get-tuple-element.21, pred[512,512]{1,0:T(8,128)(4,1)S(1)} %get-tuple-element.35, ...), kind=kOutput, calls=%fused_computation.2 | convolution fusion | flops 562036736 | bytes 7872672 | tf_op jit(solution)/shard_map/thv,shv->hts/dot_general | solution.py:88
  56.7 2.9 %collective-permute-start.8 = (f32[4,128,256]{1,2,0:T(8,128)S(1)}, f32[4,128,256]{1,2,0:T(8,128)S(1)}, u32[]{:S(2)}, u32[]{:S(2)}) collective-permute-start(f32[4,128,256]{1,2,0:T(8,128)S(1)} %add.128), channel_id=1, source_target_pairs={{0,16},{4,20},{8,24},{12,28},{16,0},{20,4},{24,8},{28,12},{32,48},... | collective-permute-start | bytes 1572872 | tf_op jit(solution)/shard_map/ppermute | solution.py:10
  61.7 5.9 %multiply_convert_fusion.1 = bf16[4,512,512]{2,1,0:T(8,128)(2,1)S(1)} fusion(f32[512,512]{1,0:T(8,128)S(1)} %get-tuple-element.44, f32[4]{0:T(128)S(1)} %get-tuple-element.21, pred[512,512]{1,0:T(8,128)(4,1)S(1)} %get-tuple-element.35, f32[4]{0:T(128)S(1)} %get-tuple-element.25, pred[512,512]{1,0:T(8,128)(4,1)S(1)} %get-tuple-element.36, ...), kind=kOutput, calls=%fused_computation.3 | convolution fusion | flops 293601280 | bytes 6824096 | tf_op jit(solution)/shard_map/thk,shk->hts/dot_general | solution.py:81
  67.6 2.1 %fusion.35 = f32[4,256,512]{2,1,0:T(8,128)} fusion(bf16[512,4,256]{0,2,1:T(8,128)(2,1)S(1)} %bitcast.106, bf16[4,512,512]{2,1,0:T(8,128)(2,1)S(1)} %multiply_convert_fusion.1), kind=kOutput, calls=%fused_computation.90 | convolution fusion | flops 536870912 | bytes 5242880 | tf_op jit(solution)/shard_map/fpx,pfj->xfj/dot_general | solution.py:98
  71.5 13.3 %collective-permute-done.4 = f32[4,128,256]{2,1,0:T(8,128)S(1)} collective-permute-done((f32[4,128,256]{2,1,0:T(8,128)S(1)}, f32[4,128,256]{2,1,0:T(8,128)S(1)}, u32[]{:S(2)}, u32[]{:S(2)}) %collective-permute-start.4) | collective-permute-done | bytes 524320 | tf_op jit(solution)/shard_map/ppermute | solution.py:10
  84.9 6.4 %collective-permute-start.5 = (f32[4,128,256]{2,1,0:T(8,128)S(1)}, f32[4,128,256]{2,1,0:T(8,128)S(1)}, u32[]{:S(2)}, u32[]{:S(2)}) collective-permute-start(f32[4,128,256]{2,1,0:T(8,128)S(1)} %add.122), channel_id=1, source_target_pairs={{0,128},{4,132},{8,136},{12,140},{16,144},{20,148},{24,152},{28,15... | collective-permute-start | bytes 1572872 | tf_op jit(solution)/shard_map/ppermute | solution.py:10
  93.0 14.9 %collective-permute-start.10 = (f32[4,128,256]{1,2,0:T(8,128)}, f32[4,128,256]{1,2,0:T(8,128)}, u32[]{:S(2)}, u32[]{:S(2)}) collective-permute-start(f32[4,128,256]{1,2,0:T(8,128)} %add.132), channel_id=1, source_target_pairs={{0,64},{4,68},{8,72},{12,76},{16,80},{20,84},{24,88},{28,92},{32,9... | collective-permute-start | bytes 1572872 | tf_op jit(solution)/shard_map/ppermute | solution.py:10
  110.0 3.8 %convolution_convert_fusion = bf16[512,2304]{1,0:T(8,128)(2,1)} fusion(bf16[512,1024]{0,1:T(8,128)(2,1)S(1)} %bitcast.114, bf16[1024,2304]{1,0:T(8,128)(2,1)S(1)} %bitcast.117), kind=kOutput, calls=%fused_computation.1 | convolution fusion | flops 2417098752 | bytes 8126464 | tf_op jit(solution)/shard_map/dot_general | solution.py:189
  113.9 4.5 %all-to-all-start = ((bf16[4,128,2304]{2,1,0:T(8,128)(2,1)}), bf16[4,128,2304]{2,1,0:T(8,128)(2,1)}, u32[]{:S(2)}, u32[]{:S(2)}) async-start(bf16[4,128,2304]{2,1,0:T(8,128)(2,1)} %bitcast.111), calls=%async_computation | async-start | bytes 4718592 | tf_op jit(solution)/shard_map/all_to_all | solution.py:21
  118.4 2.6 %convolution_bitcast_fusion.1 = f32[512,4,128]{0,2,1:T(8,128)S(1)} fusion(bf16[4,512,512]{2,1,0:T(8,128)(2,1)} %multiply_convert_fusion, bf16[512,4,128]{0,2,1:T(8,128)(2,1)} %bitcast.109), kind=kOutput, calls=%fused_computation.12 | convolution fusion | flops 268435456 | bytes 3670016 | tf_op jit(solution)/shard_map/xuf,fxl->uxl/dot_general | solution.py:92
  121.1 20.6 %collective-permute-done.10 = f32[4,128,256]{1,2,0:T(8,128)} collective-permute-done((f32[4,128,256]{1,2,0:T(8,128)}, f32[4,128,256]{1,2,0:T(8,128)}, u32[]{:S(2)}, u32[]{:S(2)}) %collective-permute-start.10) | collective-permute-done | bytes 524320 | tf_op jit(solution)/shard_map/ppermute | solution.py:10
  143.7 2.8 %collective-permute-start.11 = (f32[4,128,256]{1,2,0:T(8,128)}, f32[4,128,256]{1,2,0:T(8,128)}, u32[]{:S(2)}, u32[]{:S(2)}) collective-permute-start(f32[4,128,256]{1,2,0:T(8,128)} %add.134), channel_id=1, source_target_pairs={{0,128},{4,132},{8,136},{12,140},{16,144},{20,148},{24,152},{28,15... | collective-permute-start | bytes 1572872 | tf_op jit(solution)/shard_map/ppermute | solution.py:10
  151.2 21.6 %collective-permute-done.11 = f32[4,128,256]{1,2,0:T(8,128)} collective-permute-done((f32[4,128,256]{1,2,0:T(8,128)}, f32[4,128,256]{1,2,0:T(8,128)}, u32[]{:S(2)}, u32[]{:S(2)}) %collective-permute-start.11) | collective-permute-done | bytes 524320 | tf_op jit(solution)/shard_map/ppermute | solution.py:10
  172.7 2.1 %add_convert_fusion.1 = bf16[4,128,256]{1,2,0:T(8,128)(2,1)S(1)} fusion(f32[4,128,256]{1,2,0:T(8,128)} %collective-permute-done.11, f32[4,128,256]{1,2,0:T(8,128)} %collective-permute-done.10, f32[4,128,256]{1,2,0:T(8,128)} %copy-done.15, f32[4,128,256]{1,2,0:T(8,128)} %copy-done.14, f32[4,128,256]{1,2,0:T(8,128)} %copy-done.13, ...), kind=kLoop, calls=%fused_computation.42 | loop fusion | flops 1572864 | bytes 3407968 | tf_op jit(solution)/shard_map/convert_element_type | solution.py:67
  174.9 2.6 %fusion.6 = bf16[512,4,128]{0,2,1:T(8,128)(2,1)} fusion(f32[512,4,128]{0,2,1:T(8,128)} %convolution_bitcast_fusion, bf16[4,128,256]{1,2,0:T(8,128)(2,1)S(1)} %add_convert_fusion.1, bf16[64,4,8,256]{3,2,1,0:T(8,128)(2,1)S(1)} %bitcast.103), kind=kOutput, calls=%fused_computation.19 | convolution fusion | flops 135004160 | bytes 2883584 | tf_op jit(solution)/shard_map/xtl,tzl->xtz/dot_general | solution.py:123
  179.5 2.3 %add_convert_fusion = bf16[4,256,512]{2,1,0:T(8,128)(2,1)S(1)} fusion(f32[4,256,512]{2,1,0:T(8,128)} %fusion.35, bf16[4,128,256]{1,2,0:T(8,128)(2,1)} %copy-done.9, bf16[512,512]{1,0:T(8,128)(2,1)} %param.8), kind=kOutput, calls=%fused_computation.8 | convolution fusion | flops 135790592 | bytes 3932160 | tf_op jit(solution)/shard_map/mwg,wgc->mwc/dot_general | solution.py:126
  183.1 3.0 %reduce_sum.22 = bf16[128,2304]{1,0:T(8,128)(2,1)} reduce(bf16[4,128,2304]{2,1,0:T(8,128)(2,1)} %all-to-all-done, bf16[]{:T(256)} %constant.11.clone.1), dimensions={0}, to_apply=%region_1.2 | reduce | flops 884736 | bytes 2949122 | tf_op jit(solution)/shard_map/reduce_sum | solution.py:22
  (84 shorter events, 29.6 us)
Async XLA Ops:
  4.6 14.2 %collective-permute-start = (f32[4,128,256]{2,1,0:T(8,128)}, f32[4,128,256]{2,1,0:T(8,128)}, u32[]{:S(2)}, u32[]{:S(2)}) collective-permute-start(f32[4,128,256]{2,1,0:T(8,128)} %fusion.12), channel_id=1, source_target_pairs={{0,4},{4,0},{8,12},{12,8},{16,20},{20,16},{24,28},{28,24},{32,36},... | collective-permute-start | bytes 1572872 | tf_op jit(solution)/shard_map/ppermute | solution.py:10
  15.2 17.9 %copy-start.2 = (bf16[512,1024]{0,1:T(8,128)(2,1)}, bf16[512,1024]{0,1:T(8,128)(2,1)S(1)}, u32[]{:S(2)}) copy-start(bf16[512,1024]{0,1:T(8,128)(2,1)S(1)} %copy.55) | copy-start | bytes 3145732
  17.9 18.2 %collective-permute-start.6 = (f32[4,128,256]{1,2,0:T(8,128)}, f32[4,128,256]{1,2,0:T(8,128)}, u32[]{:S(2)}, u32[]{:S(2)}) collective-permute-start(f32[4,128,256]{1,2,0:T(8,128)} %convolution_bitcast_fusion.3), channel_id=1, source_target_pairs={{0,4},{4,0},{8,12},{12,8},{16,20},{20,16},{24,28},{28,24},{32,36},... | collective-permute-start | bytes 1572872 | tf_op jit(solution)/shard_map/ppermute | solution.py:10
  20.1 13.1 %collective-permute-start.1 = (f32[4,128,256]{2,1,0:T(8,128)S(1)}, f32[4,128,256]{2,1,0:T(8,128)S(1)}, u32[]{:S(2)}, u32[]{:S(2)}) collective-permute-start(f32[4,128,256]{2,1,0:T(8,128)S(1)} %add.114), channel_id=1, source_target_pairs={{0,8},{4,12},{8,0},{12,4},{16,24},{20,28},{24,16},{28,20},{32,40},... | collective-permute-start | bytes 1572872 | tf_op jit(solution)/shard_map/ppermute | solution.py:10
  33.3 13.7 %collective-permute-start.2 = (f32[4,128,256]{2,1,0:T(8,128)S(1)}, f32[4,128,256]{2,1,0:T(8,128)S(1)}, u32[]{:S(2)}, u32[]{:S(2)}) collective-permute-start(f32[4,128,256]{2,1,0:T(8,128)S(1)} %add.116), channel_id=1, source_target_pairs={{0,16},{4,20},{8,24},{12,28},{16,0},{20,4},{24,8},{28,12},{32,48},... | collective-permute-start | bytes 1572872 | tf_op jit(solution)/shard_map/ppermute | solution.py:10
  37.4 19.3 %collective-permute-start.7 = (f32[4,128,256]{1,2,0:T(8,128)S(1)}, f32[4,128,256]{1,2,0:T(8,128)S(1)}, u32[]{:S(2)}, u32[]{:S(2)}) collective-permute-start(f32[4,128,256]{1,2,0:T(8,128)S(1)} %add.126), channel_id=1, source_target_pairs={{0,8},{4,12},{8,0},{12,4},{16,24},{20,28},{24,16},{28,20},{32,40},... | collective-permute-start | bytes 1572872 | tf_op jit(solution)/shard_map/ppermute | solution.py:10
  47.1 12.5 %collective-permute-start.3 = (f32[4,128,256]{2,1,0:T(8,128)S(1)}, f32[4,128,256]{2,1,0:T(8,128)S(1)}, u32[]{:S(2)}, u32[]{:S(2)}) collective-permute-start(f32[4,128,256]{2,1,0:T(8,128)S(1)} %add.118), channel_id=1, source_target_pairs={{0,32},{4,36},{8,40},{12,44},{16,48},{20,52},{24,56},{28,60},{32,0... | collective-permute-start | bytes 1572872 | tf_op jit(solution)/shard_map/ppermute | solution.py:10
  47.4 14.3 %copy-start.10 = (bf16[512,512]{1,0:T(8,128)(2,1)S(1)}, bf16[512,512]{1,0:T(8,128)(2,1)}, u32[]{:S(2)}) copy-start(bf16[512,512]{1,0:T(8,128)(2,1)} %param.7) | copy-start | bytes 1572868
  47.4 14.2 %copy-start.12 = (bf16[512,512]{1,0:T(8,128)(2,1)S(1)}, bf16[512,512]{1,0:T(8,128)(2,1)}, u32[]{:S(2)}) copy-start(bf16[512,512]{1,0:T(8,128)(2,1)} %param.8) | copy-start | bytes 1572868
  56.7 13.0 %collective-permute-start.8 = (f32[4,128,256]{1,2,0:T(8,128)S(1)}, f32[4,128,256]{1,2,0:T(8,128)S(1)}, u32[]{:S(2)}, u32[]{:S(2)}) collective-permute-start(f32[4,128,256]{1,2,0:T(8,128)S(1)} %add.128), channel_id=1, source_target_pairs={{0,16},{4,20},{8,24},{12,28},{16,0},{20,4},{24,8},{28,12},{32,48},... | collective-permute-start | bytes 1572872 | tf_op jit(solution)/shard_map/ppermute | solution.py:10
  59.6 25.2 %collective-permute-start.4 = (f32[4,128,256]{2,1,0:T(8,128)S(1)}, f32[4,128,256]{2,1,0:T(8,128)S(1)}, u32[]{:S(2)}, u32[]{:S(2)}) collective-permute-start(f32[4,128,256]{2,1,0:T(8,128)S(1)} %add.120), channel_id=1, source_target_pairs={{0,64},{4,68},{8,72},{12,76},{16,80},{20,84},{24,88},{28,92},{32,9... | collective-permute-start | bytes 1572872 | tf_op jit(solution)/shard_map/ppermute | solution.py:10
  69.7 22.4 %copy-start.14 = (f32[4,128,256]{1,2,0:T(8,128)}, f32[4,128,256]{1,2,0:T(8,128)S(1)}, u32[]{:S(2)}) copy-start(f32[4,128,256]{1,2,0:T(8,128)S(1)} %collective-permute-done.8) | copy-start | bytes 1572868
  69.8 22.4 %collective-permute-start.9 = (f32[4,128,256]{1,2,0:T(8,128)S(1)}, f32[4,128,256]{1,2,0:T(8,128)S(1)}, u32[]{:S(2)}, u32[]{:S(2)}) collective-permute-start(f32[4,128,256]{1,2,0:T(8,128)S(1)} %add.130), channel_id=1, source_target_pairs={{0,32},{4,36},{8,40},{12,44},{16,48},{20,52},{24,56},{28,60},{32,0... | collective-permute-start | bytes 1572872 | tf_op jit(solution)/shard_map/ppermute | solution.py:10
  84.8 25.2 %slice-start = ((s8[4718592]{0:T(1024)(128)(4,1)}), s8[4194304]{0:T(1024)(128)(4,1)S(1)}, s32[]{:S(2)}) async-start(s8[4718592]{0:T(1024)(128)(4,1)} %bitcast.116), calls=%async_computation.1 | async-start | bytes 8388608
  84.9 23.0 %collective-permute-start.5 = (f32[4,128,256]{2,1,0:T(8,128)S(1)}, f32[4,128,256]{2,1,0:T(8,128)S(1)}, u32[]{:S(2)}, u32[]{:S(2)}) collective-permute-start(f32[4,128,256]{2,1,0:T(8,128)S(1)} %add.122), channel_id=1, source_target_pairs={{0,128},{4,132},{8,136},{12,140},{16,144},{20,148},{24,152},{28,15... | collective-permute-start | bytes 1572872 | tf_op jit(solution)/shard_map/ppermute | solution.py:10
  92.1 17.9 %slice-start.1 = ((s8[4718592]{0:T(1024)(128)(4,1)}), s8[524288]{0:T(1024)(128)(4,1)S(1)}, s32[]{:S(2)}) async-start(s8[4718592]{0:T(1024)(128)(4,1)} %bitcast.116), calls=%async_computation.2 | async-start | bytes 1048576
  92.1 17.7 %copy-start.15 = (f32[4,128,256]{1,2,0:T(8,128)}, f32[4,128,256]{1,2,0:T(8,128)S(1)}, u32[]{:S(2)}) copy-start(f32[4,128,256]{1,2,0:T(8,128)S(1)} %collective-permute-done.9) | copy-start | bytes 1572868
  93.0 48.7 %collective-permute-start.10 = (f32[4,128,256]{1,2,0:T(8,128)}, f32[4,128,256]{1,2,0:T(8,128)}, u32[]{:S(2)}, u32[]{:S(2)}) collective-permute-start(f32[4,128,256]{1,2,0:T(8,128)} %add.132), channel_id=1, source_target_pairs={{0,64},{4,68},{8,72},{12,76},{16,80},{20,84},{24,88},{28,92},{32,9... | collective-permute-start | bytes 1572872 | tf_op jit(solution)/shard_map/ppermute | solution.py:10
  113.9 69.2 %all-to-all-start = ((bf16[4,128,2304]{2,1,0:T(8,128)(2,1)}), bf16[4,128,2304]{2,1,0:T(8,128)(2,1)}, u32[]{:S(2)}, u32[]{:S(2)}) async-start(bf16[4,128,2304]{2,1,0:T(8,128)(2,1)} %bitcast.111), calls=%async_computation | async-start | bytes 4718592 | tf_op jit(solution)/shard_map/all_to_all | solution.py:21
  118.4 28.2 %copy-start.5 = (bf16[4,512,512]{2,1,0:T(8,128)(2,1)S(1)}, bf16[4,512,512]{2,1,0:T(8,128)(2,1)}, u32[]{:S(2)}) copy-start(bf16[4,512,512]{2,1,0:T(8,128)(2,1)} %multiply_convert_fusion) | copy-start | bytes 6291460
  118.4 28.1 %copy-start.11 = (bf16[512,512]{1,0:T(8,128)(2,1)S(1)}, bf16[512,512]{1,0:T(8,128)(2,1)}, u32[]{:S(2)}) copy-start(bf16[512,512]{1,0:T(8,128)(2,1)} %param.7) | copy-start | bytes 1572868
  118.4 29.6 %copy-start.4 = (bf16[512,1024]{0,1:T(8,128)(2,1)S(1)}, bf16[512,1024]{0,1:T(8,128)(2,1)}, u32[]{:S(2)}) copy-start(bf16[512,1024]{0,1:T(8,128)(2,1)} %copy-done.2) | copy-start | bytes 3145732
  118.4 29.6 %copy-start.8 = (bf16[4,128,256]{2,1,0:T(8,128)(2,1)S(1)}, bf16[4,128,256]{2,1,0:T(8,128)(2,1)}, u32[]{:S(2)}) copy-start(bf16[4,128,256]{2,1,0:T(8,128)(2,1)} %copy-done.7) | copy-start | bytes 786436
  143.7 29.0 %collective-permute-start.11 = (f32[4,128,256]{1,2,0:T(8,128)}, f32[4,128,256]{1,2,0:T(8,128)}, u32[]{:S(2)}, u32[]{:S(2)}) collective-permute-start(f32[4,128,256]{1,2,0:T(8,128)} %add.134), channel_id=1, source_target_pairs={{0,128},{4,132},{8,136},{12,140},{16,144},{20,148},{24,152},{28,15... | collective-permute-start | bytes 1572872 | tf_op jit(solution)/shard_map/ppermute | solution.py:10
  (9 other events, 70.3 us)
where the time goes:
time: 187 us; the launch traced here: 186 us
  waiting for transfers between devices  76.3 us (41%)
  matrix products  41.7 us (22%)
  starting transfers between devices  40.4 us (22%)
  other arithmetic  18.1 us (10%)
  local copies, waits for them, and re-layouts  8.62 us (5%)
    ppermute x12, waiting for transfers between devices, from_partner(): return lax.ppermute(value, axis, pairs)  76.3 us
    ppermute x12, starting transfers between devices, from_partner(): return lax.ppermute(value, axis, pairs)  35.9 us
    dot_general x1, matrix products, near_terms(): jnp.einsum('thv,shv->hts', gradient_per_head, value_per_head, preferred_e...  7.44 us
    dot_general x1, matrix products, on_device(): lax.dot_general(out_grad, out_weight, (((1,), (1,)), ((), ())), preferred...  5.94 us
    dot_general x1, matrix products, near_terms(): jnp.einsum('thk,shk->hts', query_per_head, key_per_head, preferred_elemen...  5.91 us
    unnamed x43, local copies, waits for them, and re-layouts  5.7 us
    all_to_all x1, starting transfers between devices, sent_and_summed(): lax.all_to_all(pieces, axis, split_axis=0, concat_axis=0, tiled=True)  4.48 us
    add x5, other arithmetic, exchange_levels(): query_group = query_group + other_query  4.31 us
  transfers between devices with their start and end apart: 13, of which 6 were waited for; matrix products, arithmetic and copies ran while one was open for 33% of the time, Pallas kernels for 0%

commit v1 on v0

v1 whole, which is shorter than its diff:
```python
import functools

import jax
import jax.numpy as jnp
from jax import lax
from jax.experimental import pallas as pl
from jax.experimental.pallas import tpu as pltpu
from jax.sharding import PartitionSpec as P


F32 = jnp.float32
BF16 = jnp.bfloat16
CONTRACT_LAST = (((1,), (1,)), ((), ()))
CONTRACT_FIRST = (((0,), (0,)), ((), ()))
PLAIN = (((1,), (0,)), ((), ()))
TILE = 256
SMALL = 8 * 2**20
LARGE = 24 * 2**20


def dot(left, right, dims=PLAIN):
    return lax.dot_general(left, right, dims, preferred_element_type=F32)


def vmem(shape=None, index_map=None):
    if shape is None:
        return pl.BlockSpec(memory_space=pltpu.VMEM)
    return pl.BlockSpec(shape, index_map)


def hbm():
    return pl.BlockSpec(memory_space=pltpu.HBM)


def in_hbm(*arrays):
    return [pltpu.with_memory_space_constraint(array, pltpu.HBM) for array in arrays]


def column_of(gain_ref, head):
    row = gain_ref[pl.ds(head, 1)]
    return jnp.transpose(jnp.broadcast_to(row, (8, row.shape[1])), (1, 0))[:, :1]


def smem():
    return pl.BlockSpec(memory_space=pltpu.SMEM)


def cost(flops, moved):
    return pl.CostEstimate(flops=int(flops), bytes_accessed=int(moved), transcendentals=0)


def level_weights_of(level_gain):
    levels = jnp.arange(level_gain.shape[1], dtype=jnp.int32)
    decline = jnp.exp2(-0.5 * (levels - 1).astype(F32))
    factor = jnp.where(levels == 0, F32(1.0), decline)
    return level_gain * factor[None, :]


def key_state_kernel(heads, key_hbm, value_hbm, state_hbm, key_ref, value_ref, state, sems):
    dk, dv = key_ref.shape[1] // heads, value_ref.shape[1] // heads
    loads = []
    for h in range(heads):
        narrow, wide = pl.ds(h * dk, dk), pl.ds(h * dv, dv)
        loads.append(
            (
                pltpu.make_async_copy(key_hbm.at[:, narrow], key_ref.at[:, narrow], sems.at[0, h]),
                pltpu.make_async_copy(value_hbm.at[:, wide], value_ref.at[:, wide], sems.at[1, h]),
            )
        )
    for pair in loads:
        for load in pair:
            load.start()
    stores = []
    for h in range(heads):
        for load in loads[h]:
            load.wait()
        own = pl.ds(h * dk, dk)
        key, value = key_ref[:, h * dk : (h + 1) * dk], value_ref[:, h * dv : (h + 1) * dv]
        state[own] = dot(key, value, CONTRACT_FIRST).astype(BF16)
        stores.append(pltpu.make_async_copy(state.at[own], state_hbm.at[own], sems.at[2, h]))
        stores[-1].start()
    for store in stores:
        store.wait()


def key_state(keys, values, heads):
    rows, dk, dv = keys.shape[0], keys.shape[1] // heads, values.shape[1] // heads
    return pl.pallas_call(
        functools.partial(key_state_kernel, heads),
        in_specs=[hbm(), hbm()],
        out_specs=hbm(),
        out_shape=pltpu.HBM((heads * dk, dv), BF16),
        scratch_shapes=[
            pltpu.VMEM(keys.shape, BF16),
            pltpu.VMEM(values.shape, BF16),
            pltpu.VMEM((heads * dk, dv), BF16),
            pltpu.SemaphoreType.DMA((3, heads)),
        ],
        cost_estimate=cost(2 * rows * dk * dv * heads, 2 * rows * (dk + dv) * heads),
        compiler_params=pltpu.CompilerParams(vmem_limit_bytes=SMALL),
        name="key_state",
    )(*in_hbm(keys, values))


def mix_grad_kernel(
    heads, grad_hbm, weight_hbm, query_hbm, gain_ref, dmix_hbm, state_ref,
    dmix, grad, weight, query, sems,
):
    dk, dv = query.shape[1] // heads, weight.shape[0] // heads
    loads = [
        pltpu.make_async_copy(
            weight_hbm.at[pl.ds(h * dv, dv)], weight.at[pl.ds(h * dv, dv)], sems.at[h]
        )
        for h in range(heads)
    ]
    grad_load = pltpu.make_async_copy(grad_hbm, grad, sems.at[heads])
    query_load = pltpu.make_async_copy(query_hbm, query, sems.at[heads + 1])
    grad_load.start()
    loads[0].start()
    query_load.start()
    for load in loads[1:]:
        load.start()
    grad_load.wait()
    stores = []
    for h in range(heads):
        loads[h].wait()
        own = slice(h * dv, (h + 1) * dv)
        piece = dot(grad[...], weight[own], CONTRACT_LAST).astype(BF16)
        dmix[:, own] = piece
        at = pl.ds(h * dv, dv)
        stores.append(
            pltpu.make_async_copy(dmix.at[:, at], dmix_hbm.at[:, at], sems.at[heads + 2 + h])
        )
        stores[-1].start()
        if h == 0:
            query_load.wait()
        gained = (piece.astype(F32) * column_of(gain_ref, h)).astype(BF16)
        rows = slice(h * dk, (h + 1) * dk)
        state_ref[rows] = dot(query[:, rows], gained, CONTRACT_FIRST).astype(BF16)
    for store in stores:
        store.wait()


def mix_grad(out_grad, out_weight, queries, gain, heads):
    rows, width = out_grad.shape
    dv, dk = out_weight.shape[0] // heads, queries.shape[1] // heads
    return pl.pallas_call(
        functools.partial(mix_grad_kernel, heads),
        in_specs=[hbm(), hbm(), hbm(), vmem()],
        out_specs=[hbm(), vmem()],
        out_shape=[
            pltpu.HBM((rows, heads * dv), BF16),
            jax.ShapeDtypeStruct((heads * dk, dv), BF16),
        ],
        scratch_shapes=[
            pltpu.VMEM((rows, heads * dv), BF16),
            pltpu.VMEM(out_grad.shape, BF16),
            pltpu.VMEM(out_weight.shape, BF16),
            pltpu.VMEM(queries.shape, BF16),
            pltpu.SemaphoreType.DMA((2 * heads + 2,)),
        ],
        cost_estimate=cost(2 * rows * dv * heads * (width + dk), 2 * (rows + dv * heads) * width),
        compiler_params=pltpu.CompilerParams(vmem_limit_bytes=LARGE),
        name="mix_grad",
    )(*in_hbm(out_grad, out_weight, queries), gain)


def scan_pieces(earlier, weight_ref, pieces_ref, write):
    count = pieces_ref.shape[0]
    bits = count.bit_length() - 1
    groups = [[pieces_ref[c].astype(F32) for c in range(count)]]
    for _ in range(bits - 1):
        below = groups[-1]
        groups.append([below[2 * g] + below[2 * g + 1] for g in range(len(below) // 2)])
    carried = [None]
    for bit in reversed(range(bits)):
        weight = weight_ref[0, bit]
        spread = []
        for g, carry in enumerate(carried):
            other = groups[bit][2 * g if earlier else 2 * g + 1] * weight
            total = other if carry is None else carry + other
            spread += [carry, total] if earlier else [total, carry]
        carried = spread
    for c, total in enumerate(carried):
        value = jnp.zeros(pieces_ref.shape[1:], F32) if total is None else total
        write(c, value.astype(BF16))


def scan_past_kernel(weight_ref, pieces_ref, query_ref, joined_ref):
    half = pieces_ref.shape[1]

    def write(c, value):
        joined_ref[c, :half] = value
        joined_ref[c, half:] = query_ref[c]

    scan_pieces(True, weight_ref, pieces_ref, write)


def scan_past(pieces, query_states, weights):
    count, part, width = pieces.shape
    return pl.pallas_call(
        scan_past_kernel,
        in_specs=[smem(), vmem(), vmem()],
        out_specs=vmem(),
        out_shape=jax.ShapeDtypeStruct((count, 2 * part, width), BF16),
        cost_estimate=cost(4 * pieces.size, 8 * pieces.size),
        compiler_params=pltpu.CompilerParams(vmem_limit_bytes=SMALL),
        name="scan_past",
    )(weights, pieces, query_states)


def scan_future_kernel(weight_ref, pieces_ref, sums_ref):
    def write(c, value):
        sums_ref[c] = value

    scan_pieces(False, weight_ref, pieces_ref, write)


def scan_future(joined, weights):
    count, part, width = joined.shape
    part = part // 2
    return pl.pallas_call(
        scan_future_kernel,
        grid=(1,),
        in_specs=[smem(), vmem((count, part, width), lambda i: (0, 1, 0))],
        out_specs=vmem((count, part, width), lambda i: (0, 0, 0)),
        out_shape=jax.ShapeDtypeStruct((count, part, width), BF16),
        cost_estimate=cost(2 * joined.size, 2 * joined.size),
        compiler_params=pltpu.CompilerParams(vmem_limit_bytes=SMALL),
        name="scan_future",
    )(weights, joined)


def near_kernel(
    scale, weight_ref, query_ref, key_ref, value_ref, dmix_ref, gain_ref,
    mix_ref, grad_query_ref, grad_key_ref, grad_value_ref,
):
    head = pl.program_id(0)
    rows = query_ref.shape[0]
    tiles = rows // TILE
    low = TILE.bit_length() - 1
    row = lax.broadcasted_iota(jnp.int32, (TILE, TILE), 0)
    column = lax.broadcasted_iota(jnp.int32, (TILE, TILE), 1)
    apart = row ^ column
    gains = column_of(gain_ref, head)
    table = jnp.full((TILE, TILE), weight_ref[head, 0] * scale, F32)
    for level in range(1, low + 1):
        table = jnp.where(apart >= 2 ** (level - 1), weight_ref[head, level] * scale, table)
    table = jnp.where(column <= row, table, F32(0.0))
    grad_keys = [None] * tiles
    grad_values = [None] * tiles
    for i in range(tiles):
        own = slice(i * TILE, (i + 1) * TILE)
        query, dmix, gain = query_ref[own], dmix_ref[own], gains[own]
        mix = grad_query = None
        for j in range(i + 1):
            other = slice(j * TILE, (j + 1) * TILE)
            key, value = key_ref[other], value_ref[other]
            if i == j:
                pair = gain * table
            else:
                pair = gain * (weight_ref[head, low + (i ^ j).bit_length()] * scale)
            near = (pair * dot(query, key, CONTRACT_LAST)).astype(BF16)
            grad = (pair * dot(dmix, value, CONTRACT_LAST)).astype(BF16)
            terms = (
                dot(near, value),
                dot(grad, key),
                dot(grad, query, CONTRACT_FIRST),
                dot(near, dmix, CONTRACT_FIRST),
            )
            mix = terms[0] if mix is None else mix + terms[0]
            grad_query = terms[1] if grad_query is None else grad_query + terms[1]
            grad_keys[j] = terms[2] if grad_keys[j] is None else grad_keys[j] + terms[2]
            grad_values[j] = terms[3] if grad_values[j] is None else grad_values[j] + terms[3]
        mix_ref[own] = mix.astype(BF16)
        grad_query_ref[own] = grad_query.astype(BF16)
    for j in range(tiles):
        own = slice(j * TILE, (j + 1) * TILE)
        grad_key_ref[own] = grad_keys[j].astype(BF16)
        grad_value_ref[own] = grad_values[j].astype(BF16)


def near_terms(queries, keys, values, dmix, gain, level_weights, scale, heads):
    rows, dk, dv = keys.shape[0], keys.shape[1] // heads, values.shape[1] // heads
    narrow = vmem((rows, dk), lambda h: (0, h))
    wide = vmem((rows, dv), lambda h: (0, h))
    thin, thick = (rows, heads * dk), (rows, heads * dv)
    return pl.pallas_call(
        functools.partial(near_kernel, scale),
        grid=(heads,),
        in_specs=[smem(), narrow, narrow, wide, wide, vmem(gain.shape, lambda h: (0, 0))],
        out_specs=[wide, narrow, narrow, wide],
        out_shape=[pltpu.HBM(shape, BF16) for shape in (thick, thin, thin, thick)],
        cost_estimate=cost(1.5 * rows * rows * heads * 3 * (dk + dv), 8 * rows * heads * (dk + dv)),
        compiler_params=pltpu.CompilerParams(vmem_limit_bytes=LARGE),
        name="near_terms",
    )(level_weights, *in_hbm(queries, keys, values, dmix), gain)


def share_kernel(
    scale, heads, count, index_ref, query_hbm, joined_ref, mix_hbm, gain_ref, weight_hbm, *rest
):
    share_refs, (query, mix, weight, mixture, sems) = rest[: 2 * count], rest[2 * count :]
    rows, dk = query.shape[0], query.shape[1] // heads
    dv = joined_ref.shape[2]
    each = rows // count
    some = joined_ref.shape[0] // heads
    half = weight.shape[1] // 2
    query_load = pltpu.make_async_copy(query_hbm, query, sems.at[0])
    mix_load = pltpu.make_async_copy(mix_hbm, mix, sems.at[1])
    sides = [
        pltpu.make_async_copy(
            weight_hbm.at[:, pl.ds(side * half, half)],
            weight.at[:, pl.ds(side * half, half)],
            sems.at[2 + side],
        )
        for side in range(2)
    ]
    for load in (query_load, mix_load, *sides):
        load.start()
    query_load.wait()
    mix_load.wait()
    for h in range(heads):
        past = joined_ref[h * some : (h + 1) * some, : dk // some].reshape(dk, dv)
        far = dot(query[:, h * dk : (h + 1) * dk], past)
        own = slice(h * dv, (h + 1) * dv)
        piece = (mix[:, own].astype(F32) + (column_of(gain_ref, h) * scale) * far).astype(BF16)
        for c in range(count):
            place = lax.rem(c + count - index_ref[0], count)
            at = pl.ds(pl.multiple_of(place * each, each), each)
            mixture[at, own] = piece[c * each : (c + 1) * each]
    for side in range(2):
        sides[side].wait()
        share = dot(mixture[...], weight[:, side * half : (side + 1) * half]).astype(BF16)
        for step in range(count):
            share_refs[side * count + step][...] = share[step * each : (step + 1) * each]


def shares_of(index, queries, joined, mix, gain, weight, scale, heads, count):
    rows, dk = queries.shape[0], queries.shape[1] // heads
    dv, half = joined.shape[2], weight.shape[1] // 2
    share = jax.ShapeDtypeStruct((rows // count, half), BF16)
    queries, mix, weight = in_hbm(queries, mix, weight)
    shares = pl.pallas_call(
        functools.partial(share_kernel, scale, heads, count),
        in_specs=[smem(), hbm(), vmem(), hbm(), vmem(), hbm()],
        out_specs=[vmem()] * (2 * count),
        out_shape=[share] * (2 * count),
        scratch_shapes=[
            pltpu.VMEM(queries.shape, BF16),
            pltpu.VMEM(mix.shape, BF16),
            pltpu.VMEM(weight.shape, BF16),
            pltpu.VMEM(mix.shape, BF16),
            pltpu.SemaphoreType.DMA((4,)),
        ],
        cost_estimate=cost(2 * rows * dv * heads * (dk + 2 * half), 4 * half * (rows + heads * dv)),
        compiler_params=pltpu.CompilerParams(vmem_limit_bytes=LARGE),
        name="shares",
    )(index, queries, joined, mix, gain, weight)
    return shares[:count], shares[count:]


def add_kernel(left_ref, right_ref, out_ref):
    out_ref[...] = (left_ref[...].astype(F32) + right_ref[...].astype(F32)).astype(BF16)


def added(left, right):
    return pl.pallas_call(
        add_kernel,
        in_specs=[vmem()] * 2,
        out_specs=vmem(),
        out_shape=jax.ShapeDtypeStruct(left.shape, BF16),
        cost_estimate=cost(left.size, 6 * left.size),
        compiler_params=pltpu.CompilerParams(vmem_limit_bytes=SMALL),
        name="added",
    )(left, right)


def total_kernel(*refs):
    *parts, out_ref = refs
    half = parts[0].shape[1]
    for side in range(2):
        a, b, c = (ref[...].astype(F32) for ref in parts[3 * side : 3 * side + 3])
        out_ref[:, side * half : (side + 1) * half] = (a + b + c).astype(BF16)


def total(*parts):
    rows, half = parts[0].shape
    return pl.pallas_call(
        total_kernel,
        in_specs=[vmem()] * 6,
        out_specs=vmem(),
        out_shape=jax.ShapeDtypeStruct((rows, 2 * half), BF16),
        cost_estimate=cost(4 * rows * half, 16 * rows * half),
        compiler_params=pltpu.CompilerParams(vmem_limit_bytes=SMALL),
        name="total",
    )(*parts)


def far_past_kernel(scale, dmix_ref, gain_ref, past_ref, near_ref, grad_ref):
    past = past_ref[...].reshape(near_ref.shape[1], -1)
    far = dot(dmix_ref[...], past, CONTRACT_LAST)
    gain = column_of(gain_ref, pl.program_id(0))
    grad_ref[...] = (near_ref[...].astype(F32) + (gain * scale) * far).astype(BF16)


def far_past(dmix, gain, joined, near, scale, heads):
    rows, dk, dv = near.shape[0], near.shape[1] // heads, dmix.shape[1] // heads
    narrow = vmem((rows, dk), lambda h: (0, h))
    state = vmem((joined.shape[0] // heads, joined.shape[1] // 2, dv), lambda h: (h, 0, 0))
    dmix, near = in_hbm(dmix, near)
    return pl.pallas_call(
        functools.partial(far_past_kernel, scale),
        grid=(heads,),
        in_specs=[
            vmem((rows, dv), lambda h: (0, h)), vmem(gain.shape, lambda h: (0, 0)), state, narrow,
        ],
        out_specs=narrow,
        out_shape=pltpu.HBM(near.shape, BF16),
        cost_estimate=cost(2 * rows * dk * dv * heads, 2 * rows * heads * (2 * dk + dv)),
        compiler_params=pltpu.CompilerParams(vmem_limit_bytes=SMALL),
        name="far_past",
    )(dmix, gain, joined, near)


def far_future_kernel(
    scale, heads, key_hbm, value_hbm, future_ref, near_key_hbm, near_value_hbm,
    grad_key_hbm, grad_value_hbm, key, value, near_key, near_value, grad_key, grad_value, sems,
):
    dk, dv = key.shape[1] // heads, value.shape[1] // heads
    some = future_ref.shape[0] // heads
    loads, stores = [], []
    for h in range(heads):
        thin, thick = pl.ds(h * dk, dk), pl.ds(h * dv, dv)
        for n, (source, target, at) in enumerate(
            (
                (value_hbm, value, thick),
                (near_key_hbm, near_key, thin),
                (key_hbm, key, thin),
                (near_value_hbm, near_value, thick),
            )
        ):
            loads.append(pltpu.make_async_copy(source.at[:, at], target.at[:, at], sems.at[n, h]))
    for load in loads:
        load.start()
    for h in range(heads):
        thin, thick = pl.ds(h * dk, dk), pl.ds(h * dv, dv)
        narrow, wide = slice(h * dk, (h + 1) * dk), slice(h * dv, (h + 1) * dv)
        future = future_ref[h * some : (h + 1) * some].reshape(dk, dv)
        for load in loads[4 * h : 4 * h + 2]:
            load.wait()
        far_key = dot(value[:, wide], future, CONTRACT_LAST)
        grad_key[:, narrow] = (near_key[:, narrow].astype(F32) + scale * far_key).astype(BF16)
        stores.append(
            pltpu.make_async_copy(grad_key.at[:, thin], grad_key_hbm.at[:, thin], sems.at[4, h])
        )
        stores[-1].start()
        for load in loads[4 * h + 2 : 4 * h + 4]:
            load.wait()
        far_value = dot(key[:, narrow], future)
        grad_value[:, wide] = (near_value[:, wide].astype(F32) + scale * far_value).astype(BF16)
        stores.append(
            pltpu.make_async_copy(grad_value.at[:, thick], grad_value_hbm.at[:, thick], sems.at[5, h])
        )
        stores[-1].start()
    for store in stores:
        store.wait()


def far_future(keys, values, future, near_keys, near_values, scale, heads):
    rows, dk, dv = keys.shape[0], keys.shape[1] // heads, values.shape[1] // heads
    thin, thick = keys.shape, values.shape
    keys, values, near_keys, near_values = in_hbm(keys, values, near_keys, near_values)
    return pl.pallas_call(
        functools.partial(far_future_kernel, scale, heads),
        in_specs=[hbm(), hbm(), vmem(), hbm(), hbm()],
        out_specs=[hbm()] * 2,
        out_shape=[pltpu.HBM(thin, BF16), pltpu.HBM(thick, BF16)],
        scratch_shapes=[
            pltpu.VMEM(shape, BF16) for shape in (thin, thick, thin, thick, thin, thick)
        ]
        + [pltpu.SemaphoreType.DMA((6, heads))],
        cost_estimate=cost(4 * rows * dk * dv * heads, 6 * rows * heads * (dk + dv)),
        compiler_params=pltpu.CompilerParams(vmem_limit_bytes=LARGE),
        name="far_future",
    )(keys, values, future, near_keys, near_values)


def in_pieces(states, axis):
    count = lax.axis_size(axis)
    return states.reshape(count, states.shape[0] // count, states.shape[1])


def swapped(pieces, axis):
    return lax.all_to_all(pieces, axis, split_axis=0, concat_axis=0, tiled=True)


def turned(value, axis, step):
    count = lax.axis_size(axis)
    return lax.ppermute(value, axis, [(i, (i + step) % count) for i in range(count)])


def summed_shares(left, right, axis):
    left_far = turned(left[2], axis, 1)
    right_far = turned(right[2], axis, -1)
    right_on = turned(right[1], axis, 1)
    left_back = turned(left[3], axis, -1)
    left_on = turned(added(left[1], left_far), axis, 1)
    right_back = turned(added(right[3], right_far), axis, -1)
    return total(left[0], left_on, left_back, right[0], right_on, right_back)


def on_device(
    query_vectors, key_vectors, value_vectors, query_gain, level_gain, out_weight, out_grad
):
    heads, rows = query_gain.shape
    dk = query_vectors.shape[1] // heads
    scale = dk ** (-0.5)
    seq_count = lax.axis_size("seq")
    bits = seq_count.bit_length() - 1
    shift_bits = rows.bit_length() - 1
    level_weights = level_weights_of(level_gain)
    gain = query_gain
    head = lax.axis_index("seq") // (seq_count // heads)
    scan_weights = lax.dynamic_slice(level_weights, (head, shift_bits + 1), (1, bits))

    key_states = key_state(key_vectors, value_vectors, heads)
    key_pieces = swapped(in_pieces(key_states, "seq"), "seq")
    dmix, query_states = mix_grad(out_grad, out_weight, query_vectors, gain, heads)
    past_pieces = scan_past(key_pieces, in_pieces(query_states, "seq"), scan_weights)
    joined = swapped(past_pieces, "seq")
    mix, near_queries, near_keys, near_values = near_terms(
        query_vectors, key_vectors, value_vectors, dmix, gain, level_weights, scale, heads
    )
    index = lax.axis_index("head").reshape(1)
    left, right = shares_of(
        index, query_vectors, joined, mix, gain, out_weight, scale, heads,
        lax.axis_size("head"),
    )
    layer_out = summed_shares(left, right, "head")
    grad_queries = far_past(dmix, gain, joined, near_queries, scale, heads)
    future_pieces = scan_future(joined, scan_weights)
    future = swapped(future_pieces, "seq")
    grad_keys, grad_values = far_future(
        key_vectors, value_vectors, future, near_keys, near_values, scale, heads
    )
    return (layer_out, grad_queries, grad_keys, grad_values)


def solution(mesh):
    return jax.shard_map(
        on_device,
        mesh=mesh,
        in_specs=(
            P("seq", "head"),
            P("seq", "head"),
            P("seq", "head"),
            P("head", "seq"),
            P("head", None),
            P("head", None),
            P("seq", None),
        ),
        out_specs=(P(("seq", "head"), None), P("seq", "head"), P("seq", "head"), P("seq", "head")),
        check_vma=False,
    )
```

time: 187 us -> 92.4 us (0.49)
  waiting for transfers between devices: 76.3 us -> 17.2 us
  matrix products: 41.7 us -> 0 us
  Pallas kernels: 0 us -> 37.8 us
  other arithmetic: 18.1 us -> 0.7 us
  local copies, waits for them, and re-layouts: 8.62 us -> 0.78 us
  starting transfers between devices: 40.4 us -> 34.4 us
    ppermute x12 -> x6, waiting for transfers between devices: 76.3 us -> 0.02 us  [turned(): lax.ppermute(value, axis, [(i, (i + step) % count) for i in range(count)])]
    dot_general x14 -> x0, matrix products: 41.7 us -> none  [the longest x1 7.44 us: near_terms(): jnp.einsum('thv,shv->hts', gradient_per_head, value_per_head, preferred_e...]
    pallas_call x0 -> x11, Pallas kernels: none -> 37.8 us  [the longest x1 9.23 us: mix_grad(): pl.pallas_call(functools.partial(mix_grad_kernel, heads), in_specs=[hbm()...]
    ppermute x12 -> x6, starting transfers between devices: 35.9 us -> 7.36 us  [turned(): lax.ppermute(value, axis, [(i, (i + step) % count) for i in range(count)])]
    all_to_all x1 -> x3, starting transfers between devices: 4.48 us -> 27.1 us  [swapped(): return lax.all_to_all(pieces, axis, split_axis=0, concat_axis=0, tiled=True)]
    all_to_all x1 -> x3, waiting for transfers between devices: 0.01 us -> 17.2 us  [swapped(): return lax.all_to_all(pieces, axis, split_axis=0, concat_axis=0, tiled=True)]
    reduce_sum x2 -> x0, other arithmetic: 6.21 us -> none  [the longest x1 3.22 us: bit_length(): return jnp.sum((numbers[..., None] >= powers).astype(jnp.int32), axis=-1)]
    add x10 -> x0, other arithmetic: 5.86 us -> none  [the longest x5 4.31 us: exchange_levels(): query_group = query_group + other_query]
  transfers between devices with their start and end apart: 13 -> 9, of which waited for: 6 -> 3; matrix products, arithmetic and copies ran while one was open for 33% -> 1% of each run, Pallas kernels for 0% -> 28%
where the time goes in v1:
time: 92.4 us; the launch traced here: 91.7 us
  Pallas kernels  37.8 us (41%)
  starting transfers between devices  34.4 us (37%)
  waiting for transfers between devices  17.2 us (19%)
    all_to_all x3, starting transfers between devices, swapped(): return lax.all_to_all(pieces, axis, split_axis=0, concat_axis=0, tiled=True)  27.1 us
    all_to_all x3, waiting for transfers between devices, swapped(): return lax.all_to_all(pieces, axis, split_axis=0, concat_axis=0, tiled=True)  17.2 us
    pallas_call x1, Pallas kernels, mix_grad(): pl.pallas_call(functools.partial(mix_grad_kernel, heads), in_specs=[hbm()...  9.23 us
    ppermute x6, starting transfers between devices, turned(): lax.ppermute(value, axis, [(i, (i + step) % count) for i in range(count)])  7.36 us
    pallas_call x1, Pallas kernels, near_terms(): pl.pallas_call(functools.partial(near_kernel, scale), grid=(heads,), in_s...  7.34 us
    pallas_call x1, Pallas kernels, shares_of(): pl.pallas_call(functools.partial(share_kernel, scale, heads, count), in_s...  6.49 us
    pallas_call x1, Pallas kernels, far_future(): pl.pallas_call(functools.partial(far_future_kernel, scale, heads), in_spe...  4.13 us
    pallas_call x1, Pallas kernels, far_past(): pl.pallas_call(functools.partial(far_past_kernel, scale), grid=(heads,),...  3.9 us
  transfers between devices with their start and end apart: 9, of which 3 were waited for; matrix products, arithmetic and copies ran while one was open for 1% of the time, Pallas kernels for 28%

profile of v1, /device:TPU:1, one launch (start us, length us, event | category | flops | bytes accessed | tf_op | source)
XLA Modules:
  0.0 91.7 jit_solution(7688798672040381424)
XLA Ops:
  0.6 2.7 %key_state.1 = bf16[512,256]{1,0:T(8,128)(2,1)} custom-call(bf16[512,512]{1,0:T(8,128)(2,1)} %key_hbm.3, bf16[512,1024]{1,0:T(8,128)(2,1)} %value_hbm.3), custom_call_target="tpu_custom_call" | custom-call | flops 134217728 | bytes 1572864 | tf_op jit(solution)/shard_map/key_state/pallas_call | solution.py:88
  3.4 13.0 %all-to-all-start = ((bf16[64,8,256]{2,1,0:T(8,128)(2,1)}), bf16[64,8,256]{2,1,0:T(8,128)(2,1)S(1)}, u32[]{:S(2)}, u32[]{:S(2)}) async-start(bf16[64,8,256]{2,1,0:T(8,128)(2,1)} %bitcast.4), calls=%async_computation | async-start | bytes 524288 | tf_op jit(solution)/shard_map/all_to_all | solution.py:495
  16.4 0.7 broadcast_multiply_fusion.weight_ref
  17.1 0.1 constant_dynamic-slice_fusion.weight_ref
  17.2 0.7 copy-done
  17.9 9.2 %mix_grad.1 = (bf16[512,1024]{1,0:T(8,128)(2,1)}, bf16[512,256]{1,0:T(8,128)(2,1)S(1)}) custom-call(bf16[512,2304]{1,0:T(8,128)(2,1)} %grad_hbm.1, bf16[1024,2304]{1,0:T(8,128)(2,1)} %weight_hbm.3, bf16[512,512]{1,0:T(8,128)(2,1)} %query_hbm.3, f32[4,512]{1,0:T(4,128)S(1)} %copy-done), custom_call_target="tpu_custom_call" | custom-call | flops 2550136832 | bytes 7077888 | tf_op jit(solution)/shard_map/mix_grad/pallas_call | solution.py:147
  27.1 2.3 %all-to-all-done.pieces_ref = bf16[64,8,256]{2,1,0:T(8,128)(2,1)S(1)} async-done(((bf16[64,8,256]{2,1,0:T(8,128)(2,1)}), bf16[64,8,256]{2,1,0:T(8,128)(2,1)S(1)}, u32[]{:S(2)}, u32[]{:S(2)}) %all-to-all-start) | async-done | bytes 262176 | tf_op jit(solution)/shard_map/all_to_all | solution.py:495
  29.4 1.4 %scan_past.1 = bf16[64,16,256]{2,1,0:T(8,128)(2,1)} custom-call(f32[1,6]{1,0:T(1,128)S(1)} %constant_dynamic-slice_fusion.weight_ref, bf16[64,8,256]{2,1,0:T(8,128)(2,1)S(1)} %all-to-all-done.pieces_ref, bf16[64,8,256]{2,1,0:T(8,128)(2,1)S(1)} %bitcast.3), custom_call_target="tpu_custom_call" | custom-call | flops 524288 | bytes 1048576 | tf_op jit(solution)/shard_map/scan_past/pallas_call | solution.py:201
  30.8 8.0 %all-to-all-start.1 = ((bf16[64,16,256]{2,1,0:T(8,128)(2,1)}), bf16[64,16,256]{2,1,0:T(8,128)(2,1)S(1)}, u32[]{:S(2)}, u32[]{:S(2)}) async-start(bf16[64,16,256]{2,1,0:T(8,128)(2,1)} %scan_past.1), calls=%async_computation.1 | async-start | bytes 1048576 | tf_op jit(solution)/shard_map/all_to_all | solution.py:495
  38.8 7.3 %near_terms.1 = (bf16[512,1024]{1,0:T(8,128)(2,1)}, bf16[512,512]{1,0:T(8,128)(2,1)}, bf16[512,512]{1,0:T(8,128)(2,1)}, bf16[512,1024]{1,0:T(8,128)(2,1)}) custom-call(f32[4,21]{1,0:T(4,128)S(1)} %broadcast_multiply_fusion.weight_ref, bf16[512,512]{1,0:T(8,128)(2,1)} %query_hbm.3, bf16[512,512]{1,0:T(8,128)(2,1)} %key_hbm.3, bf16[512,1024]{1,0:T(8,128)(2,1)} %value_hbm.3, ...), custom_call_target="tpu_custom_call" | custom-call | flops 1811939328 | bytes 6291456 | tf_op jit(solution)/shard_map/near_terms/pallas_call | solution.py:288
  46.2 10.3 %all-to-all-done.1.joined_ref.past_ref.pieces_ref = bf16[64,16,256]{2,1,0:T(8,128)(2,1)S(1)} async-done(((bf16[64,16,256]{2,1,0:T(8,128)(2,1)}), bf16[64,16,256]{2,1,0:T(8,128)(2,1)S(1)}, u32[]{:S(2)}, u32[]{:S(2)}) %all-to-all-start.1) | async-done | bytes 524320 | tf_op jit(solution)/shard_map/all_to_all | solution.py:495
  56.5 6.5 %shares.1 = (bf16[128,1152]{1,0:T(8,128)(2,1)S(1)}, bf16[128,1152]{1,0:T(8,128)(2,1)S(1)}, bf16[128,1152]{1,0:T(8,128)(2,1)S(1)}, bf16[128,1152]{1,0:T(8,128)(2,...) custom-call(s32[1]{0:T(128)} %bitcast.index_ref, ...), custom_call_target="tpu_custom_call" | custom-call | flops 2550136832 | bytes 7077888 | tf_op jit(solution)/shard_map/shares/pallas_call | solution.py:344
  63.0 1.4 %collective-permute-start = (bf16[128,1152]{1,0:T(8,128)(2,1)S(1)}, bf16[128,1152]{1,0:T(8,128)(2,1)S(1)}, u32[]{:S(2)}, u32[]{:S(2)}) collective-permute-start(bf16[128,1152]{1,0:T(8,128)(2,1)S(1)} %get-tuple-element.25), channel_id=1, source_target_pairs={{0,1},{1,2},{2,3},{3,0},{4,5},{5,6},{6,7},{7,4},{8,9},{9,10},{10,1... | collective-permute-start | bytes 884744 | tf_op jit(solution)/shard_map/ppermute | solution.py:500
  64.4 1.5 %collective-permute-start.4 = (bf16[128,1152]{1,0:T(8,128)(2,1)}, bf16[128,1152]{1,0:T(8,128)(2,1)S(1)}, u32[]{:S(2)}, u32[]{:S(2)}) collective-permute-start(bf16[128,1152]{1,0:T(8,128)(2,1)} %get-tuple-element.30), channel_id=1, source_target_pairs={{0,3},{1,0},{2,1},{3,2},{4,7},{5,4},{6,5},{7,6},{8,11},{9,8},{10,9... | collective-permute-start | bytes 884744 | tf_op jit(solution)/shard_map/ppermute | solution.py:500
  65.9 1.3 %scan_future.1 = bf16[64,8,256]{2,1,0:T(8,128)(2,1)} custom-call(f32[1,6]{1,0:T(1,128)S(1)} %constant_dynamic-slice_fusion.weight_ref, bf16[64,16,256]{2,1,0:T(8,128)(2,1)S(1)} %all-to-all-done.1.joined_ref.past_ref.pieces_ref), custom_call_target="tpu_custom_call" | custom-call | flops 524288 | bytes 524288 | tf_op jit(solution)/shard_map/scan_future/pallas_call | solution.py:222
  67.3 6.1 %all-to-all-start.2 = ((bf16[64,8,256]{2,1,0:T(8,128)(2,1)}), bf16[64,8,256]{2,1,0:T(8,128)(2,1)S(1)}, u32[]{:S(2)}, u32[]{:S(2)}) async-start(bf16[64,8,256]{2,1,0:T(8,128)(2,1)} %scan_future.1), calls=%async_computation.2 | async-start | bytes 524288 | tf_op jit(solution)/shard_map/all_to_all | solution.py:495
  73.4 1.6 %collective-permute-start.2 = (bf16[128,1152]{1,0:T(8,128)(2,1)}, bf16[128,1152]{1,0:T(8,128)(2,1)S(1)}, u32[]{:S(2)}, u32[]{:S(2)}) collective-permute-start(bf16[128,1152]{1,0:T(8,128)(2,1)} %get-tuple-element.26), channel_id=1, source_target_pairs={{0,3},{1,0},{2,1},{3,2},{4,7},{5,4},{6,5},{7,6},{8,11},{9,8},{10,9... | collective-permute-start | bytes 884744 | tf_op jit(solution)/shard_map/ppermute | solution.py:500
  75.0 0.1 collective-permute-start.1
  75.2 0.1 added.3
  75.2 2.8 %collective-permute-start.5 = (bf16[128,1152]{1,0:T(8,128)(2,1)S(1)}, bf16[128,1152]{1,0:T(8,128)(2,1)S(1)}, u32[]{:S(2)}, u32[]{:S(2)}) collective-permute-start(bf16[128,1152]{1,0:T(8,128)(2,1)S(1)} %added.3), channel_id=1, source_target_pairs={{0,3},{1,0},{2,1},{3,2},{4,7},{5,4},{6,5},{7,6},{8,11},{9,8},{10,9... | collective-permute-start | bytes 884744 | tf_op jit(solution)/shard_map/ppermute | solution.py:500
  78.0 3.9 %far_past.1 = bf16[512,512]{1,0:T(8,128)(2,1)} custom-call(bf16[512,1024]{1,0:T(8,128)(2,1)} %get-tuple-element.21.dmix_ref, f32[4,512]{1,0:T(4,128)S(1)} %copy-done.1, bf16[64,16,256]{2,1,0:T(8,128)(2,1)S(1)} %all-to-all-done.1.joined_ref.past_ref.pieces_ref, bf16[512,512]{1,0:T(8,128)(2,1)} %get-tuple-element.31.near_ref), custom_call_target="tpu_custom_call" | custom-call | flops 134217728 | bytes 2097152 | tf_op jit(solution)/shard_map/far_past/pallas_call | solution.py:412
  81.9 4.6 %all-to-all-done.2.future_ref = bf16[64,8,256]{2,1,0:T(8,128)(2,1)S(1)} async-done(((bf16[64,8,256]{2,1,0:T(8,128)(2,1)}), bf16[64,8,256]{2,1,0:T(8,128)(2,1)S(1)}, u32[]{:S(2)}, u32[]{:S(2)}) %all-to-all-start.2) | async-done | bytes 262176 | tf_op jit(solution)/shard_map/all_to_all | solution.py:495
  86.4 4.1 %far_future.1 = (bf16[512,512]{1,0:T(8,128)(2,1)}, bf16[512,1024]{1,0:T(8,128)(2,1)}) custom-call(bf16[512,512]{1,0:T(8,128)(2,1)} %key_hbm.3, bf16[512,1024]{1,0:T(8,128)(2,1)} %value_hbm.3, bf16[64,8,256]{2,1,0:T(8,128)(2,1)S(1)} %all-to-all-done.2.future_ref, bf16[512,512]{1,0:T(8,128)(2,1)} %get-tuple-element.32.near_key_hbm, ...), custom_call_target="tpu_custom_call" | custom-call | flops 268435456 | bytes 4718592 | tf_op jit(solution)/shard_map/far_future/pallas_call | solution.py:474
  90.6 1.0 %total.1 = bf16[128,2304]{1,0:T(8,128)(2,1)} custom-call(bf16[128,1152]{1,0:T(8,128)(2,1)S(1)} %get-tuple-element.23.refs_0_, bf16[128,1152]{1,0:T(8,128)(2,1)S(1)} %collective-permute-done.1.refs_1_, bf16[128,1152]{1,0:T(8,128)(2,1)S(1)} %collective-permute-done.2.refs_2_, bf16[128,1152]{1,0:T(8,128)(2,1)S(1)} %get-tuple-element.27.refs_3_, ...), custom_call_target="tpu_custom_call" | custom-call | flops 589824 | bytes 2359296 | tf_op jit(solution)/shard_map/total/pallas_call | solution.py:389
  (12 shorter events, 0.1 us)
Async XLA Ops:
  3.4 26.1 %all-to-all-start = ((bf16[64,8,256]{2,1,0:T(8,128)(2,1)}), bf16[64,8,256]{2,1,0:T(8,128)(2,1)S(1)}, u32[]{:S(2)}, u32[]{:S(2)}) async-start(bf16[64,8,256]{2,1,0:T(8,128)(2,1)} %bitcast.4), calls=%async_computation | async-start | bytes 524288 | tf_op jit(solution)/shard_map/all_to_all | solution.py:495
  17.2 0.7 copy-start
  17.9 21.0 %copy-start.1 = (f32[4,512]{1,0:T(4,128)S(1)}, f32[4,512]{1,0:T(4,128)}, u32[]{:S(2)}) copy-start(f32[4,512]{1,0:T(4,128)} %gain_ref.7) | copy-start | bytes 24580
  30.8 25.7 %all-to-all-start.1 = ((bf16[64,16,256]{2,1,0:T(8,128)(2,1)}), bf16[64,16,256]{2,1,0:T(8,128)(2,1)S(1)}, u32[]{:S(2)}, u32[]{:S(2)}) async-start(bf16[64,16,256]{2,1,0:T(8,128)(2,1)} %scan_past.1), calls=%async_computation.1 | async-start | bytes 1048576 | tf_op jit(solution)/shard_map/all_to_all | solution.py:495
  63.0 12.0 %collective-permute-start = (bf16[128,1152]{1,0:T(8,128)(2,1)S(1)}, bf16[128,1152]{1,0:T(8,128)(2,1)S(1)}, u32[]{:S(2)}, u32[]{:S(2)}) collective-permute-start(bf16[128,1152]{1,0:T(8,128)(2,1)S(1)} %get-tuple-element.25), channel_id=1, source_target_pairs={{0,1},{1,2},{2,3},{3,0},{4,5},{5,6},{6,7},{7,4},{8,9},{9,10},{10,1... | collective-permute-start | bytes 884744 | tf_op jit(solution)/shard_map/ppermute | solution.py:500
  64.4 10.8 %collective-permute-start.4 = (bf16[128,1152]{1,0:T(8,128)(2,1)}, bf16[128,1152]{1,0:T(8,128)(2,1)S(1)}, u32[]{:S(2)}, u32[]{:S(2)}) collective-permute-start(bf16[128,1152]{1,0:T(8,128)(2,1)} %get-tuple-element.30), channel_id=1, source_target_pairs={{0,3},{1,0},{2,1},{3,2},{4,7},{5,4},{6,5},{7,6},{8,11},{9,8},{10,9... | collective-permute-start | bytes 884744 | tf_op jit(solution)/shard_map/ppermute | solution.py:500
  67.3 19.2 %all-to-all-start.2 = ((bf16[64,8,256]{2,1,0:T(8,128)(2,1)}), bf16[64,8,256]{2,1,0:T(8,128)(2,1)S(1)}, u32[]{:S(2)}, u32[]{:S(2)}) async-start(bf16[64,8,256]{2,1,0:T(8,128)(2,1)} %scan_future.1), calls=%async_computation.2 | async-start | bytes 524288 | tf_op jit(solution)/shard_map/all_to_all | solution.py:495
  73.4 17.2 %collective-permute-start.2 = (bf16[128,1152]{1,0:T(8,128)(2,1)}, bf16[128,1152]{1,0:T(8,128)(2,1)S(1)}, u32[]{:S(2)}, u32[]{:S(2)}) collective-permute-start(bf16[128,1152]{1,0:T(8,128)(2,1)} %get-tuple-element.26), channel_id=1, source_target_pairs={{0,3},{1,0},{2,1},{3,2},{4,7},{5,4},{6,5},{7,6},{8,11},{9,8},{10,9... | collective-permute-start | bytes 884744 | tf_op jit(solution)/shard_map/ppermute | solution.py:500
  75.0 15.6 %collective-permute-start.3 = (bf16[128,1152]{1,0:T(8,128)(2,1)}, bf16[128,1152]{1,0:T(8,128)(2,1)S(1)}, u32[]{:S(2)}, u32[]{:S(2)}) collective-permute-start(bf16[128,1152]{1,0:T(8,128)(2,1)} %get-tuple-element.28), channel_id=1, source_target_pairs={{0,1},{1,2},{2,3},{3,0},{4,5},{5,6},{6,7},{7,4},{8,9},{9,10},{10,1... | collective-permute-start | bytes 884744 | tf_op jit(solution)/shard_map/ppermute | solution.py:500
  75.0 15.6 %collective-permute-start.1 = (bf16[128,1152]{1,0:T(8,128)(2,1)S(1)}, bf16[128,1152]{1,0:T(8,128)(2,1)S(1)}, u32[]{:S(2)}, u32[]{:S(2)}) collective-permute-start(bf16[128,1152]{1,0:T(8,128)(2,1)S(1)} %added.2), channel_id=1, source_target_pairs={{0,1},{1,2},{2,3},{3,0},{4,5},{5,6},{6,7},{7,4},{8,9},{9,10},{10,1... | collective-permute-start | bytes 884744 | tf_op jit(solution)/shard_map/ppermute | solution.py:500
  75.2 15.4 %collective-permute-start.5 = (bf16[128,1152]{1,0:T(8,128)(2,1)S(1)}, bf16[128,1152]{1,0:T(8,128)(2,1)S(1)}, u32[]{:S(2)}, u32[]{:S(2)}) collective-permute-start(bf16[128,1152]{1,0:T(8,128)(2,1)S(1)} %added.3), channel_id=1, source_target_pairs={{0,3},{1,0},{2,1},{3,2},{4,7},{5,4},{6,5},{7,6},{8,11},{9,8},{10,9... | collective-permute-start | bytes 884744 | tf_op jit(solution)/shard_map/ppermute | solution.py:500

commit v2 on v1

--- a/solution.py
+++ b/solution.py
@@ -107,36 +107,35 @@
     dmix, grad, weight, query, sems,
 ):
     dk, dv = query.shape[1] // heads, weight.shape[0] // heads
+    pair = 2 * dv
+
+    def started(number, source, target):
+        copy = pltpu.make_async_copy(source, target, sems.at[number])
+        copy.start()
+        return copy
+
+    grad_load = started(0, grad_hbm, grad)
     loads = [
-        pltpu.make_async_copy(
-            weight_hbm.at[pl.ds(h * dv, dv)], weight.at[pl.ds(h * dv, dv)], sems.at[h]
-        )
-        for h in range(heads)
+        started(1 + n, weight_hbm.at[pl.ds(n * pair, pair)], weight.at[pl.ds(n * pair, pair)])
+        for n in range(heads // 2)
     ]
-    grad_load = pltpu.make_async_copy(grad_hbm, grad, sems.at[heads])
-    query_load = pltpu.make_async_copy(query_hbm, query, sems.at[heads + 1])
-    grad_load.start()
-    loads[0].start()
-    query_load.start()
-    for load in loads[1:]:
-        load.start()
+    query_load = started(1 + heads, query_hbm, query)
     grad_load.wait()
     stores = []
-    for h in range(heads):
-        loads[h].wait()
-        own = slice(h * dv, (h + 1) * dv)
-        piece = dot(grad[...], weight[own], CONTRACT_LAST).astype(BF16)
-        dmix[:, own] = piece
-        at = pl.ds(h * dv, dv)
-        stores.append(
-            pltpu.make_async_copy(dmix.at[:, at], dmix_hbm.at[:, at], sems.at[heads + 2 + h])
-        )
-        stores[-1].start()
-        if h == 0:
+    for n in range(heads // 2):
+        loads[n].wait()
+        both = slice(n * pair, (n + 1) * pair)
+        piece = dot(grad[...], weight[both], CONTRACT_LAST).astype(BF16)
+        dmix[:, both] = piece
+        at = pl.ds(n * pair, pair)
+        stores.append(started(2 + heads + n, dmix.at[:, at], dmix_hbm.at[:, at]))
+        if n == 0:
             query_load.wait()
-        gained = (piece.astype(F32) * column_of(gain_ref, h)).astype(BF16)
-        rows = slice(h * dk, (h + 1) * dk)
-        state_ref[rows] = dot(query[:, rows], gained, CONTRACT_FIRST).astype(BF16)
+        for h in (2 * n, 2 * n + 1):
+            own = piece[:, (h - 2 * n) * dv : (h - 2 * n + 1) * dv].astype(F32)
+            gained = (own * column_of(gain_ref, h)).astype(BF16)
+            rows = slice(h * dk, (h + 1) * dk)
+            state_ref[rows] = dot(query[:, rows], gained, CONTRACT_FIRST).astype(BF16)
     for store in stores:
         store.wait()
 
@@ -397,26 +396,45 @@
     )(*parts)
 
 
-def far_past_kernel(scale, dmix_ref, gain_ref, past_ref, near_ref, grad_ref):
-    past = past_ref[...].reshape(near_ref.shape[1], -1)
-    far = dot(dmix_ref[...], past, CONTRACT_LAST)
-    gain = column_of(gain_ref, pl.program_id(0))
-    grad_ref[...] = (near_ref[...].astype(F32) + (gain * scale) * far).astype(BF16)
+def far_past_kernel(
+    scale, heads, dmix_hbm, gain_ref, joined_ref, near_hbm, grad_hbm, dmix, near, grad, sems
+):
+    dk, dv = near.shape[1] // heads, dmix.shape[1] // heads
+    some = joined_ref.shape[0] // heads
+    loads, stores = [], []
+    for h in range(heads):
+        for n, (source, target, size) in enumerate(((dmix_hbm, dmix, dv), (near_hbm, near, dk))):
+            at = pl.ds(h * size, size)
+            loads.append(pltpu.make_async_copy(source.at[:, at], target.at[:, at], sems.at[n, h]))
+            loads[-1].start()
+    for h in range(heads):
+        past = joined_ref[h * some : (h + 1) * some, : dk // some].reshape(dk, dv)
+        for load in loads[2 * h : 2 * h + 2]:
+            load.wait()
+        far = dot(dmix[:, h * dv : (h + 1) * dv], past, CONTRACT_LAST)
+        own, at = slice(h * dk, (h + 1) * dk), pl.ds(h * dk, dk)
+        total = near[:, own].astype(F32) + (column_of(gain_ref, h) * scale) * far
+        grad[:, own] = total.astype(BF16)
+        stores.append(pltpu.make_async_copy(grad.at[:, at], grad_hbm.at[:, at], sems.at[2, h]))
+        stores[-1].start()
+    for store in stores:
+        store.wait()
 
 
 def far_past(dmix, gain, joined, near, scale, heads):
     rows, dk, dv = near.shape[0], near.shape[1] // heads, dmix.shape[1] // heads
-    narrow = vmem((rows, dk), lambda h: (0, h))
-    state = vmem((joined.shape[0] // heads, joined.shape[1] // 2, dv), lambda h: (h, 0, 0))
     dmix, near = in_hbm(dmix, near)
     return pl.pallas_call(
-        functools.partial(far_past_kernel, scale),
-        grid=(heads,),
-        in_specs=[
-            vmem((rows, dv), lambda h: (0, h)), vmem(gain.shape, lambda h: (0, 0)), state, narrow,
+        functools.partial(far_past_kernel, scale, heads),
+        in_specs=[hbm(), vmem(), vmem(), hbm()],
+        out_specs=hbm(),
+        out_shape=pltpu.HBM(near.shape, BF16),
+        scratch_shapes=[
+            pltpu.VMEM(dmix.shape, BF16),
+            pltpu.VMEM(near.shape, BF16),
+            pltpu.VMEM(near.shape, BF16),
+            pltpu.SemaphoreType.DMA((3, heads)),
         ],
-        out_specs=narrow,
-        out_shape=pltpu.HBM(near.shape, BF16),
         cost_estimate=cost(2 * rows * dk * dv * heads, 2 * rows * heads * (2 * dk + dv)),
         compiler_params=pltpu.CompilerParams(vmem_limit_bytes=SMALL),
         name="far_past",
@@ -503,8 +521,8 @@
 def summed_shares(left, right, axis):
     left_far = turned(left[2], axis, 1)
     right_far = turned(right[2], axis, -1)
+    left_back = turned(left[3], axis, -1)
     right_on = turned(right[1], axis, 1)
-    left_back = turned(left[3], axis, -1)
     left_on = turned(added(left[1], left_far), axis, 1)
     right_back = turned(added(right[3], right_far), axis, -1)
     return total(left[0], left_on, left_back, right[0], right_on, right_back)
@@ -533,9 +551,9 @@
         query_vectors, key_vectors, value_vectors, dmix, gain, level_weights, scale, heads
     )
     index = lax.axis_index("head").reshape(1)
+    head_count = lax.axis_size("head")
     left, right = shares_of(
-        index, query_vectors, joined, mix, gain, out_weight, scale, heads,
-        lax.axis_size("head"),
+        index, query_vectors, joined, mix, gain, out_weight, scale, heads, head_count
     )
     layer_out = summed_shares(left, right, "head")
     grad_queries = far_past(dmix, gain, joined, near_queries, scale, heads)

time: 92.4 us -> 90.1 us (0.975)
  Pallas kernels: 37.8 us -> 34.5 us
  waiting for transfers between devices: 17.2 us -> 20.4 us
  starting transfers between devices: 34.4 us -> 32.2 us
    all_to_all x3, waiting for transfers between devices: 17.2 us -> 20.3 us  [swapped(): return lax.all_to_all(pieces, axis, split_axis=0, concat_axis=0, tiled=True)]
    all_to_all x3, starting transfers between devices: 27.1 us -> 24.7 us  [swapped(): return lax.all_to_all(pieces, axis, split_axis=0, concat_axis=0, tiled=True)]
    pallas_call x1, Pallas kernels: 9.23 us -> 6.85 us  [mix_grad(): pl.pallas_call(functools.partial(mix_grad_kernel, heads), in_specs=[hbm()...]
  transfers between devices with their start and end apart: 9 -> 9, of which waited for: 3 -> 4; matrix products, arithmetic and copies ran while one was open for 1% -> 1% of each run, Pallas kernels for 28% -> 26%
where the time goes in v2:
time: 90.1 us; the launch traced here: 89.4 us
  Pallas kernels  34.5 us (38%)
  starting transfers between devices  32.2 us (36%)
  waiting for transfers between devices  20.4 us (23%)
    all_to_all x3, starting transfers between devices, swapped(): return lax.all_to_all(pieces, axis, split_axis=0, concat_axis=0, tiled=True)  24.7 us
    all_to_all x3, waiting for transfers between devices, swapped(): return lax.all_to_all(pieces, axis, split_axis=0, concat_axis=0, tiled=True)  20.3 us
    ppermute x6, starting transfers between devices, turned(): lax.ppermute(value, axis, [(i, (i + step) % count) for i in range(count)])  7.54 us
    pallas_call x1, Pallas kernels, near_terms(): pl.pallas_call(functools.partial(near_kernel, scale), grid=(heads,), in_s...  7.34 us
    pallas_call x1, Pallas kernels, mix_grad(): pl.pallas_call(functools.partial(mix_grad_kernel, heads), in_specs=[hbm()...  6.85 us
    pallas_call x1, Pallas kernels, shares_of(): pl.pallas_call(functools.partial(share_kernel, scale, heads, count), in_s...  6.49 us
    pallas_call x1, Pallas kernels, far_future(): pl.pallas_call(functools.partial(far_future_kernel, scale, heads), in_spe...  4.13 us
    pallas_call x1, Pallas kernels, far_past(): pl.pallas_call(functools.partial(far_past_kernel, scale, heads), in_specs...  3.02 us
  transfers between devices with their start and end apart: 9, of which 4 were waited for; matrix products, arithmetic and copies ran while one was open for 1% of the time, Pallas kernels for 26%

profile of v2, /device:TPU:1, one launch (start us, length us, event | category | flops | bytes accessed | tf_op | source)
XLA Modules:
  0.0 89.4 jit_solution(51283709815554733)
XLA Ops:
  0.6 2.7 %key_state.1 = bf16[512,256]{1,0:T(8,128)(2,1)} custom-call(bf16[512,512]{1,0:T(8,128)(2,1)} %key_hbm.3, bf16[512,1024]{1,0:T(8,128)(2,1)} %value_hbm.3), custom_call_target="tpu_custom_call" | custom-call | flops 134217728 | bytes 1572864 | tf_op jit(solution)/shard_map/key_state/pallas_call | solution.py:88
  3.4 13.0 %all-to-all-start = ((bf16[64,8,256]{2,1,0:T(8,128)(2,1)}), bf16[64,8,256]{2,1,0:T(8,128)(2,1)S(1)}, u32[]{:S(2)}, u32[]{:S(2)}) async-start(bf16[64,8,256]{2,1,0:T(8,128)(2,1)} %bitcast.4), calls=%async_computation | async-start | bytes 524288 | tf_op jit(solution)/shard_map/all_to_all | solution.py:513
  16.4 0.7 broadcast_multiply_fusion.weight_ref
  17.1 0.1 constant_dynamic-slice_fusion.weight_ref
  17.2 0.7 copy-done
  17.9 6.9 %mix_grad.1 = (bf16[512,1024]{1,0:T(8,128)(2,1)}, bf16[512,256]{1,0:T(8,128)(2,1)S(1)}) custom-call(bf16[512,2304]{1,0:T(8,128)(2,1)} %grad_hbm.1, bf16[1024,2304]{1,0:T(8,128)(2,1)} %weight_hbm.3, bf16[512,512]{1,0:T(8,128)(2,1)} %query_hbm.3, f32[4,512]{1,0:T(4,128)S(1)} %copy-done), custom_call_target="tpu_custom_call" | custom-call | flops 2550136832 | bytes 7077888 | tf_op jit(solution)/shard_map/mix_grad/pallas_call | solution.py:146
  24.7 4.7 %all-to-all-done.pieces_ref = bf16[64,8,256]{2,1,0:T(8,128)(2,1)S(1)} async-done(((bf16[64,8,256]{2,1,0:T(8,128)(2,1)}), bf16[64,8,256]{2,1,0:T(8,128)(2,1)S(1)}, u32[]{:S(2)}, u32[]{:S(2)}) %all-to-all-start) | async-done | bytes 262176 | tf_op jit(solution)/shard_map/all_to_all | solution.py:513
  29.4 1.4 %scan_past.1 = bf16[64,16,256]{2,1,0:T(8,128)(2,1)} custom-call(f32[1,6]{1,0:T(1,128)S(1)} %constant_dynamic-slice_fusion.weight_ref, bf16[64,8,256]{2,1,0:T(8,128)(2,1)S(1)} %all-to-all-done.pieces_ref, bf16[64,8,256]{2,1,0:T(8,128)(2,1)S(1)} %bitcast.3), custom_call_target="tpu_custom_call" | custom-call | flops 524288 | bytes 1048576 | tf_op jit(solution)/shard_map/scan_past/pallas_call | solution.py:200
  30.8 5.6 %all-to-all-start.1 = ((bf16[64,16,256]{2,1,0:T(8,128)(2,1)}), bf16[64,16,256]{2,1,0:T(8,128)(2,1)S(1)}, u32[]{:S(2)}, u32[]{:S(2)}) async-start(bf16[64,16,256]{2,1,0:T(8,128)(2,1)} %scan_past.1), calls=%async_computation.1 | async-start | bytes 1048576 | tf_op jit(solution)/shard_map/all_to_all | solution.py:513
  36.5 7.3 %near_terms.1 = (bf16[512,1024]{1,0:T(8,128)(2,1)}, bf16[512,512]{1,0:T(8,128)(2,1)}, bf16[512,512]{1,0:T(8,128)(2,1)}, bf16[512,1024]{1,0:T(8,128)(2,1)}) custom-call(f32[4,21]{1,0:T(4,128)S(1)} %broadcast_multiply_fusion.weight_ref, bf16[512,512]{1,0:T(8,128)(2,1)} %query_hbm.3, bf16[512,512]{1,0:T(8,128)(2,1)} %key_hbm.3, bf16[512,1024]{1,0:T(8,128)(2,1)} %value_hbm.3, ...), custom_call_target="tpu_custom_call" | custom-call | flops 1811939328 | bytes 6291456 | tf_op jit(solution)/shard_map/near_terms/pallas_call | solution.py:287
  43.8 10.3 %all-to-all-done.1.joined_ref.pieces_ref = bf16[64,16,256]{2,1,0:T(8,128)(2,1)S(1)} async-done(((bf16[64,16,256]{2,1,0:T(8,128)(2,1)}), bf16[64,16,256]{2,1,0:T(8,128)(2,1)S(1)}, u32[]{:S(2)}, u32[]{:S(2)}) %all-to-all-start.1) | async-done | bytes 524320 | tf_op jit(solution)/shard_map/all_to_all | solution.py:513
  54.1 6.5 %shares.1 = (bf16[128,1152]{1,0:T(8,128)(2,1)S(1)}, bf16[128,1152]{1,0:T(8,128)(2,1)S(1)}, bf16[128,1152]{1,0:T(8,128)(2,1)S(1)}, bf16[128,1152]{1,0:T(8,128)(2,...) custom-call(s32[1]{0:T(128)} %bitcast.index_ref, ...), custom_call_target="tpu_custom_call" | custom-call | flops 2550136832 | bytes 7077888 | tf_op jit(solution)/shard_map/shares/pallas_call | solution.py:343
  60.6 1.4 %collective-permute-start = (bf16[128,1152]{1,0:T(8,128)(2,1)S(1)}, bf16[128,1152]{1,0:T(8,128)(2,1)S(1)}, u32[]{:S(2)}, u32[]{:S(2)}) collective-permute-start(bf16[128,1152]{1,0:T(8,128)(2,1)S(1)} %get-tuple-element.25), channel_id=1, source_target_pairs={{0,1},{1,2},{2,3},{3,0},{4,5},{5,6},{6,7},{7,4},{8,9},{9,10},{10,1... | collective-permute-start | bytes 884744 | tf_op jit(solution)/shard_map/ppermute | solution.py:518
  62.0 1.5 %collective-permute-start.4 = (bf16[128,1152]{1,0:T(8,128)(2,1)}, bf16[128,1152]{1,0:T(8,128)(2,1)S(1)}, u32[]{:S(2)}, u32[]{:S(2)}) collective-permute-start(bf16[128,1152]{1,0:T(8,128)(2,1)} %get-tuple-element.30), channel_id=1, source_target_pairs={{0,3},{1,0},{2,1},{3,2},{4,7},{5,4},{6,5},{7,6},{8,11},{9,8},{10,9... | collective-permute-start | bytes 884744 | tf_op jit(solution)/shard_map/ppermute | solution.py:518
  63.5 1.3 %scan_future.1 = bf16[64,8,256]{2,1,0:T(8,128)(2,1)} custom-call(f32[1,6]{1,0:T(1,128)S(1)} %constant_dynamic-slice_fusion.weight_ref, bf16[64,16,256]{2,1,0:T(8,128)(2,1)S(1)} %all-to-all-done.1.joined_ref.pieces_ref), custom_call_target="tpu_custom_call" | custom-call | flops 524288 | bytes 524288 | tf_op jit(solution)/shard_map/scan_future/pallas_call | solution.py:221
  64.9 6.1 %all-to-all-start.2 = ((bf16[64,8,256]{2,1,0:T(8,128)(2,1)}), bf16[64,8,256]{2,1,0:T(8,128)(2,1)S(1)}, u32[]{:S(2)}, u32[]{:S(2)}) async-start(bf16[64,8,256]{2,1,0:T(8,128)(2,1)} %scan_future.1), calls=%async_computation.2 | async-start | bytes 524288 | tf_op jit(solution)/shard_map/all_to_all | solution.py:513
  71.0 1.8 %collective-permute-start.2 = (bf16[128,1152]{1,0:T(8,128)(2,1)}, bf16[128,1152]{1,0:T(8,128)(2,1)S(1)}, u32[]{:S(2)}, u32[]{:S(2)}) collective-permute-start(bf16[128,1152]{1,0:T(8,128)(2,1)} %get-tuple-element.26), channel_id=1, source_target_pairs={{0,3},{1,0},{2,1},{3,2},{4,7},{5,4},{6,5},{7,6},{8,11},{9,8},{10,9... | collective-permute-start | bytes 884744 | tf_op jit(solution)/shard_map/ppermute | solution.py:518
  72.9 0.1 collective-permute-start.1
  73.0 2.8 %collective-permute-start.5 = (bf16[128,1152]{1,0:T(8,128)(2,1)S(1)}, bf16[128,1152]{1,0:T(8,128)(2,1)S(1)}, u32[]{:S(2)}, u32[]{:S(2)}) collective-permute-start(bf16[128,1152]{1,0:T(8,128)(2,1)S(1)} %added.3), channel_id=1, source_target_pairs={{0,3},{1,0},{2,1},{3,2},{4,7},{5,4},{6,5},{7,6},{8,11},{9,8},{10,9... | collective-permute-start | bytes 884744 | tf_op jit(solution)/shard_map/ppermute | solution.py:518
  75.8 3.0 %far_past.1 = bf16[512,512]{1,0:T(8,128)(2,1)} custom-call(bf16[512,1024]{1,0:T(8,128)(2,1)} %get-tuple-element.21.dmix_ref.dmix_hbm, f32[4,512]{1,0:T(4,128)S(1)} %copy-done.1, bf16[64,16,256]{2,1,0:T(8,128)(2,1)S(1)} %all-to-all-done.1.joined_ref.pieces_ref, bf16[512,512]{1,0:T(8,128)(2,1)} %get-tuple-element.31.near_hbm), custom_call_target="tpu_custom_call" | custom-call | flops 134217728 | bytes 2097152 | tf_op jit(solution)/shard_map/far_past/pallas_call | solution.py:427
  78.8 5.2 %all-to-all-done.2.future_ref = bf16[64,8,256]{2,1,0:T(8,128)(2,1)S(1)} async-done(((bf16[64,8,256]{2,1,0:T(8,128)(2,1)}), bf16[64,8,256]{2,1,0:T(8,128)(2,1)S(1)}, u32[]{:S(2)}, u32[]{:S(2)}) %all-to-all-start.2) | async-done | bytes 262176 | tf_op jit(solution)/shard_map/all_to_all | solution.py:513
  84.1 4.1 %far_future.1 = (bf16[512,512]{1,0:T(8,128)(2,1)}, bf16[512,1024]{1,0:T(8,128)(2,1)}) custom-call(bf16[512,512]{1,0:T(8,128)(2,1)} %key_hbm.3, bf16[512,1024]{1,0:T(8,128)(2,1)} %value_hbm.3, bf16[64,8,256]{2,1,0:T(8,128)(2,1)S(1)} %all-to-all-done.2.future_ref, bf16[512,512]{1,0:T(8,128)(2,1)} %get-tuple-element.32.near_key_hbm, ...), custom_call_target="tpu_custom_call" | custom-call | flops 268435456 | bytes 4718592 | tf_op jit(solution)/shard_map/far_future/pallas_call | solution.py:492
  88.2 0.1 collective-permute-done.1.refs_1_
  88.3 1.0 %total.1 = bf16[128,2304]{1,0:T(8,128)(2,1)} custom-call(bf16[128,1152]{1,0:T(8,128)(2,1)S(1)} %get-tuple-element.23.refs_0_, bf16[128,1152]{1,0:T(8,128)(2,1)S(1)} %collective-permute-done.1.refs_1_, bf16[128,1152]{1,0:T(8,128)(2,1)S(1)} %collective-permute-done.2.refs_2_, bf16[128,1152]{1,0:T(8,128)(2,1)S(1)} %get-tuple-element.27.refs_3_, ...), custom_call_target="tpu_custom_call" | custom-call | flops 589824 | bytes 2359296 | tf_op jit(solution)/shard_map/total/pallas_call | solution.py:388
  (12 shorter events, 0.2 us)
Async XLA Ops:
  3.4 26.1 %all-to-all-start = ((bf16[64,8,256]{2,1,0:T(8,128)(2,1)}), bf16[64,8,256]{2,1,0:T(8,128)(2,1)S(1)}, u32[]{:S(2)}, u32[]{:S(2)}) async-start(bf16[64,8,256]{2,1,0:T(8,128)(2,1)} %bitcast.4), calls=%async_computation | async-start | bytes 524288 | tf_op jit(solution)/shard_map/all_to_all | solution.py:513
  17.2 0.7 copy-start
  17.9 18.6 %copy-start.1 = (f32[4,512]{1,0:T(4,128)S(1)}, f32[4,512]{1,0:T(4,128)}, u32[]{:S(2)}) copy-start(f32[4,512]{1,0:T(4,128)} %gain_ref.7) | copy-start | bytes 24580
  30.8 23.3 %all-to-all-start.1 = ((bf16[64,16,256]{2,1,0:T(8,128)(2,1)}), bf16[64,16,256]{2,1,0:T(8,128)(2,1)S(1)}, u32[]{:S(2)}, u32[]{:S(2)}) async-start(bf16[64,16,256]{2,1,0:T(8,128)(2,1)} %scan_past.1), calls=%async_computation.1 | async-start | bytes 1048576 | tf_op jit(solution)/shard_map/all_to_all | solution.py:513
  60.6 12.1 %collective-permute-start = (bf16[128,1152]{1,0:T(8,128)(2,1)S(1)}, bf16[128,1152]{1,0:T(8,128)(2,1)S(1)}, u32[]{:S(2)}, u32[]{:S(2)}) collective-permute-start(bf16[128,1152]{1,0:T(8,128)(2,1)S(1)} %get-tuple-element.25), channel_id=1, source_target_pairs={{0,1},{1,2},{2,3},{3,0},{4,5},{5,6},{6,7},{7,4},{8,9},{9,10},{10,1... | collective-permute-start | bytes 884744 | tf_op jit(solution)/shard_map/ppermute | solution.py:518
  62.0 10.9 %collective-permute-start.4 = (bf16[128,1152]{1,0:T(8,128)(2,1)}, bf16[128,1152]{1,0:T(8,128)(2,1)S(1)}, u32[]{:S(2)}, u32[]{:S(2)}) collective-permute-start(bf16[128,1152]{1,0:T(8,128)(2,1)} %get-tuple-element.30), channel_id=1, source_target_pairs={{0,3},{1,0},{2,1},{3,2},{4,7},{5,4},{6,5},{7,6},{8,11},{9,8},{10,9... | collective-permute-start | bytes 884744 | tf_op jit(solution)/shard_map/ppermute | solution.py:518
  64.9 19.2 %all-to-all-start.2 = ((bf16[64,8,256]{2,1,0:T(8,128)(2,1)}), bf16[64,8,256]{2,1,0:T(8,128)(2,1)S(1)}, u32[]{:S(2)}, u32[]{:S(2)}) async-start(bf16[64,8,256]{2,1,0:T(8,128)(2,1)} %scan_future.1), calls=%async_computation.2 | async-start | bytes 524288 | tf_op jit(solution)/shard_map/all_to_all | solution.py:513
  71.0 17.2 %collective-permute-start.2 = (bf16[128,1152]{1,0:T(8,128)(2,1)}, bf16[128,1152]{1,0:T(8,128)(2,1)S(1)}, u32[]{:S(2)}, u32[]{:S(2)}) collective-permute-start(bf16[128,1152]{1,0:T(8,128)(2,1)} %get-tuple-element.26), channel_id=1, source_target_pairs={{0,3},{1,0},{2,1},{3,2},{4,7},{5,4},{6,5},{7,6},{8,11},{9,8},{10,9... | collective-permute-start | bytes 884744 | tf_op jit(solution)/shard_map/ppermute | solution.py:518
  72.8 15.4 %collective-permute-start.3 = (bf16[128,1152]{1,0:T(8,128)(2,1)}, bf16[128,1152]{1,0:T(8,128)(2,1)S(1)}, u32[]{:S(2)}, u32[]{:S(2)}) collective-permute-start(bf16[128,1152]{1,0:T(8,128)(2,1)} %get-tuple-element.28), channel_id=1, source_target_pairs={{0,1},{1,2},{2,3},{3,0},{4,5},{5,6},{6,7},{7,4},{8,9},{9,10},{10,1... | collective-permute-start | bytes 884744 | tf_op jit(solution)/shard_map/ppermute | solution.py:518
  72.9 15.5 %collective-permute-start.1 = (bf16[128,1152]{1,0:T(8,128)(2,1)S(1)}, bf16[128,1152]{1,0:T(8,128)(2,1)S(1)}, u32[]{:S(2)}, u32[]{:S(2)}) collective-permute-start(bf16[128,1152]{1,0:T(8,128)(2,1)S(1)} %added.2), channel_id=1, source_target_pairs={{0,1},{1,2},{2,3},{3,0},{4,5},{5,6},{6,7},{7,4},{8,9},{9,10},{10,1... | collective-permute-start | bytes 884744 | tf_op jit(solution)/shard_map/ppermute | solution.py:518
  73.0 15.3 %collective-permute-start.5 = (bf16[128,1152]{1,0:T(8,128)(2,1)S(1)}, bf16[128,1152]{1,0:T(8,128)(2,1)S(1)}, u32[]{:S(2)}, u32[]{:S(2)}) collective-permute-start(bf16[128,1152]{1,0:T(8,128)(2,1)S(1)} %added.3), channel_id=1, source_target_pairs={{0,3},{1,0},{2,1},{3,2},{4,7},{5,4},{6,5},{7,6},{8,11},{9,8},{10,9... | collective-permute-start | bytes 884744 | tf_op jit(solution)/shard_map/ppermute | solution.py:518

commit v3 on v2

--- a/solution.py
+++ b/solution.py
@@ -14,6 +14,7 @@
 CONTRACT_FIRST = (((0,), (0,)), ((), ()))
 PLAIN = (((1,), (0,)), ((), ()))
 TILE = 256
+STEP_HEADS = 2
 SMALL = 8 * 2**20
 LARGE = 24 * 2**20
 
@@ -56,55 +57,58 @@
     return level_gain * factor[None, :]
 
 
-def key_state_kernel(heads, key_hbm, value_hbm, state_hbm, key_ref, value_ref, state, sems):
-    dk, dv = key_ref.shape[1] // heads, value_ref.shape[1] // heads
+def key_state_kernel(
+    heads, core_ref, key_hbm, value_hbm, mine_ref, other_ref, key, value, state, sems
+):
+    dk, dv = key.shape[1] // heads, value.shape[1] // heads
     loads = []
     for h in range(heads):
         narrow, wide = pl.ds(h * dk, dk), pl.ds(h * dv, dv)
         loads.append(
             (
-                pltpu.make_async_copy(key_hbm.at[:, narrow], key_ref.at[:, narrow], sems.at[0, h]),
-                pltpu.make_async_copy(value_hbm.at[:, wide], value_ref.at[:, wide], sems.at[1, h]),
+                pltpu.make_async_copy(key_hbm.at[:, narrow], key.at[:, narrow], sems.at[0, h]),
+                pltpu.make_async_copy(value_hbm.at[:, wide], value.at[:, wide], sems.at[1, h]),
             )
         )
     for pair in loads:
         for load in pair:
             load.start()
-    stores = []
     for h in range(heads):
         for load in loads[h]:
             load.wait()
-        own = pl.ds(h * dk, dk)
-        key, value = key_ref[:, h * dk : (h + 1) * dk], value_ref[:, h * dv : (h + 1) * dv]
-        state[own] = dot(key, value, CONTRACT_FIRST).astype(BF16)
-        stores.append(pltpu.make_async_copy(state.at[own], state_hbm.at[own], sems.at[2, h]))
-        stores[-1].start()
-    for store in stores:
-        store.wait()
-
-
-def key_state(keys, values, heads):
+        narrow, wide = slice(h * dk, (h + 1) * dk), slice(h * dv, (h + 1) * dv)
+        state[narrow] = dot(key[:, narrow], value[:, wide], CONTRACT_FIRST).astype(BF16)
+    take_halves(core_ref, state, mine_ref, other_ref)
+
+
+def take_halves(core_ref, state, mine_ref, other_ref):
+    half = mine_ref.shape[0]
+    mine_ref[...] = state[pl.ds(pl.multiple_of(core_ref[0] * half, half), half)]
+    other_ref[...] = state[pl.ds(pl.multiple_of((1 - core_ref[0]) * half, half), half)]
+
+
+def key_state(core, keys, values, heads):
     rows, dk, dv = keys.shape[0], keys.shape[1] // heads, values.shape[1] // heads
     return pl.pallas_call(
         functools.partial(key_state_kernel, heads),
-        in_specs=[hbm(), hbm()],
-        out_specs=hbm(),
-        out_shape=pltpu.HBM((heads * dk, dv), BF16),
+        in_specs=[smem(), hbm(), hbm()],
+        out_specs=[vmem()] * 2,
+        out_shape=[jax.ShapeDtypeStruct((heads * dk // 2, dv), BF16)] * 2,
         scratch_shapes=[
             pltpu.VMEM(keys.shape, BF16),
             pltpu.VMEM(values.shape, BF16),
             pltpu.VMEM((heads * dk, dv), BF16),
-            pltpu.SemaphoreType.DMA((3, heads)),
+            pltpu.SemaphoreType.DMA((2, heads)),
         ],
         cost_estimate=cost(2 * rows * dk * dv * heads, 2 * rows * (dk + dv) * heads),
         compiler_params=pltpu.CompilerParams(vmem_limit_bytes=SMALL),
         name="key_state",
-    )(*in_hbm(keys, values))
+    )(core, *in_hbm(keys, values))
 
 
 def mix_grad_kernel(
-    heads, grad_hbm, weight_hbm, query_hbm, gain_ref, dmix_hbm, state_ref,
-    dmix, grad, weight, query, sems,
+    heads, core_ref, grad_hbm, weight_hbm, query_hbm, gain_ref, dmix_hbm, mine_ref, other_ref,
+    dmix, grad, weight, query, state, sems,
 ):
     dk, dv = query.shape[1] // heads, weight.shape[0] // heads
     pair = 2 * dv
@@ -114,54 +118,76 @@
         copy.start()
         return copy
 
-    grad_load = started(0, grad_hbm, grad)
-    loads = [
-        started(1 + n, weight_hbm.at[pl.ds(n * pair, pair)], weight.at[pl.ds(n * pair, pair)])
-        for n in range(heads // 2)
+    depth = grad.shape[1] // 3
+    firsts = []
+    for n in range(3):
+        at = pl.ds(n * depth, depth)
+        firsts.append(
+            (
+                started(2 * n, grad_hbm.at[:, at], grad.at[:, at]),
+                started(2 * n + 1, weight_hbm.at[pl.ds(0, pair), at], weight.at[pl.ds(0, pair), at]),
+            )
+        )
+    query_load = started(6, query_hbm, query)
+    loads = [None] + [
+        started(6 + n, weight_hbm.at[pl.ds(n * pair, pair)], weight.at[pl.ds(n * pair, pair)])
+        for n in range(1, heads // 2)
     ]
-    query_load = started(1 + heads, query_hbm, query)
-    grad_load.wait()
+    base = 6 + heads // 2
     stores = []
     for n in range(heads // 2):
-        loads[n].wait()
         both = slice(n * pair, (n + 1) * pair)
-        piece = dot(grad[...], weight[both], CONTRACT_LAST).astype(BF16)
+        if n == 0:
+            piece = None
+            for step, copies in enumerate(firsts):
+                for copy in copies:
+                    copy.wait()
+                at = slice(step * depth, (step + 1) * depth)
+                term = dot(grad[:, at], weight[both, at], CONTRACT_LAST)
+                piece = term if piece is None else piece + term
+        else:
+            loads[n].wait()
+            piece = dot(grad[...], weight[both], CONTRACT_LAST)
+        piece = piece.astype(BF16)
         dmix[:, both] = piece
         at = pl.ds(n * pair, pair)
-        stores.append(started(2 + heads + n, dmix.at[:, at], dmix_hbm.at[:, at]))
+        stores.append(started(base + n, dmix.at[:, at], dmix_hbm.at[:, at]))
         if n == 0:
             query_load.wait()
         for h in (2 * n, 2 * n + 1):
             own = piece[:, (h - 2 * n) * dv : (h - 2 * n + 1) * dv].astype(F32)
             gained = (own * column_of(gain_ref, h)).astype(BF16)
             rows = slice(h * dk, (h + 1) * dk)
-            state_ref[rows] = dot(query[:, rows], gained, CONTRACT_FIRST).astype(BF16)
+            state[rows] = dot(query[:, rows], gained, CONTRACT_FIRST).astype(BF16)
+    take_halves(core_ref, state, mine_ref, other_ref)
     for store in stores:
         store.wait()
 
 
-def mix_grad(out_grad, out_weight, queries, gain, heads):
+def mix_grad(core, out_grad, out_weight, queries, gain, heads):
     rows, width = out_grad.shape
     dv, dk = out_weight.shape[0] // heads, queries.shape[1] // heads
     return pl.pallas_call(
         functools.partial(mix_grad_kernel, heads),
-        in_specs=[hbm(), hbm(), hbm(), vmem()],
-        out_specs=[hbm(), vmem()],
+        in_specs=[smem(), hbm(), hbm(), hbm(), vmem()],
+        out_specs=[hbm(), vmem(), vmem()],
         out_shape=[
             pltpu.HBM((rows, heads * dv), BF16),
-            jax.ShapeDtypeStruct((heads * dk, dv), BF16),
+            jax.ShapeDtypeStruct((heads * dk // 2, dv), BF16),
+            jax.ShapeDtypeStruct((heads * dk // 2, dv), BF16),
         ],
         scratch_shapes=[
             pltpu.VMEM((rows, heads * dv), BF16),
             pltpu.VMEM(out_grad.shape, BF16),
             pltpu.VMEM(out_weight.shape, BF16),
             pltpu.VMEM(queries.shape, BF16),
-            pltpu.SemaphoreType.DMA((2 * heads + 2,)),
+            pltpu.VMEM((heads * dk, dv), BF16),
+            pltpu.SemaphoreType.DMA((6 + heads,)),
         ],
         cost_estimate=cost(2 * rows * dv * heads * (width + dk), 2 * (rows + dv * heads) * width),
         compiler_params=pltpu.CompilerParams(vmem_limit_bytes=LARGE),
         name="mix_grad",
-    )(*in_hbm(out_grad, out_weight, queries), gain)
+    )(core, *in_hbm(out_grad, out_weight, queries), gain)
 
 
 def scan_pieces(earlier, weight_ref, pieces_ref, write):
@@ -185,27 +211,84 @@
         write(c, value.astype(BF16))
 
 
-def scan_past_kernel(weight_ref, pieces_ref, query_ref, joined_ref):
-    half = pieces_ref.shape[1]
+def chip_sum_kernel(mine_ref, other_ref, sum_ref):
+    part = sum_ref.shape[1]
+    for c in range(sum_ref.shape[0]):
+        own = slice(c * part, (c + 1) * part)
+        sum_ref[c] = (mine_ref[own].astype(F32) + other_ref[own].astype(F32)).astype(BF16)
+
+
+def chip_sum(mine, other, count):
+    return pl.pallas_call(
+        chip_sum_kernel,
+        in_specs=[vmem()] * 2,
+        out_specs=vmem(),
+        out_shape=jax.ShapeDtypeStruct((count, mine.shape[0] // count, mine.shape[1]), BF16),
+        cost_estimate=cost(mine.size, 6 * mine.size),
+        compiler_params=pltpu.CompilerParams(vmem_limit_bytes=SMALL),
+        name="chip_sum",
+    )(mine, other)
+
+
+def scan_past_kernel(weight_ref, pieces_ref, mine_ref, other_ref, joined_ref):
+    part = pieces_ref.shape[1]
 
     def write(c, value):
-        joined_ref[c, :half] = value
-        joined_ref[c, half:] = query_ref[c]
+        own = slice(c * part, (c + 1) * part)
+        query = mine_ref[own].astype(F32) + other_ref[own].astype(F32)
+        joined_ref[c, :part] = value
+        joined_ref[c, part:] = query.astype(BF16)
 
     scan_pieces(True, weight_ref, pieces_ref, write)
 
 
-def scan_past(pieces, query_states, weights):
+def scan_past(pieces, mine, other, weights):
     count, part, width = pieces.shape
     return pl.pallas_call(
         scan_past_kernel,
-        in_specs=[smem(), vmem(), vmem()],
+        in_specs=[smem()] + [vmem()] * 3,
         out_specs=vmem(),
         out_shape=jax.ShapeDtypeStruct((count, 2 * part, width), BF16),
         cost_estimate=cost(4 * pieces.size, 8 * pieces.size),
         compiler_params=pltpu.CompilerParams(vmem_limit_bytes=SMALL),
         name="scan_past",
-    )(weights, pieces, query_states)
+    )(weights, pieces, mine, other)
+
+
+def parts_kernel(earlier, core_ref, weight_ref, shared_ref, mine_ref, other_ref, own_ref, sent_ref):
+    part = mine_ref.shape[0] // shared_ref.shape[0]
+    heads = weight_ref.shape[0]
+    each = mine_ref.shape[0] // heads
+    upper = core_ref[0] == 1
+    owns = upper if earlier else jnp.logical_not(upper)
+    for h in range(heads):
+        at = slice(h * each, (h + 1) * each)
+        held = slice(h * each // part, (h + 1) * each // part)
+        shared = shared_ref[held, :part].reshape(each, -1).astype(F32)
+        weight = weight_ref[h, 0]
+        with_other = (shared + weight * other_ref[at].astype(F32)).astype(BF16)
+        with_mine = (shared + weight * mine_ref[at].astype(F32)).astype(BF16)
+        plain = shared.astype(BF16)
+        own_ref[at] = jnp.where(owns, with_other, plain)
+        sent_ref[at] = jnp.where(owns, plain, with_mine)
+
+
+def parts_of(core, weights, shared, mine, other, earlier):
+    return pl.pallas_call(
+        functools.partial(parts_kernel, earlier),
+        in_specs=[smem()] * 2 + [vmem()] * 3,
+        out_specs=[vmem()] * 2,
+        out_shape=[jax.ShapeDtypeStruct(mine.shape, BF16)] * 2,
+        cost_estimate=cost(4 * mine.size, 10 * mine.size),
+        compiler_params=pltpu.CompilerParams(vmem_limit_bytes=SMALL),
+        name="past_parts" if earlier else "future_parts",
+    )(core, weights, shared, mine, other)
+
+
+def state_of(core, own_ref, came_ref, h, heads, dk):
+    at = h % (heads // 2)
+    own, came = own_ref[at * dk : (at + 1) * dk], came_ref[at * dk : (at + 1) * dk]
+    return jnp.where(core == h // (heads // 2), own, came)
 
 
 def scan_future_kernel(weight_ref, pieces_ref, sums_ref):
@@ -234,59 +317,71 @@
     scale, weight_ref, query_ref, key_ref, value_ref, dmix_ref, gain_ref,
     mix_ref, grad_query_ref, grad_key_ref, grad_value_ref,
 ):
-    head = pl.program_id(0)
     rows = query_ref.shape[0]
+    heads = gain_ref.shape[0] // pl.num_programs(0)
+    dk, dv = query_ref.shape[1] // heads, value_ref.shape[1] // heads
     tiles = rows // TILE
     low = TILE.bit_length() - 1
     row = lax.broadcasted_iota(jnp.int32, (TILE, TILE), 0)
     column = lax.broadcasted_iota(jnp.int32, (TILE, TILE), 1)
     apart = row ^ column
-    gains = column_of(gain_ref, head)
-    table = jnp.full((TILE, TILE), weight_ref[head, 0] * scale, F32)
-    for level in range(1, low + 1):
-        table = jnp.where(apart >= 2 ** (level - 1), weight_ref[head, level] * scale, table)
-    table = jnp.where(column <= row, table, F32(0.0))
-    grad_keys = [None] * tiles
-    grad_values = [None] * tiles
+    mixes, grad_queries, grad_keys, grad_values = {}, {}, {}, {}
+
+    def add(sums, at, term):
+        sums[at] = sums[at] + term if at in sums else term
+
+    each = range(heads)
+    names = [pl.program_id(0) * heads + h for h in each]
+    gains = [column_of(gain_ref, names[h]) for h in each]
+    tables = []
+    for h in each:
+        table = jnp.full((TILE, TILE), weight_ref[names[h], 0] * scale, F32)
+        for level in range(1, low + 1):
+            table = jnp.where(
+                apart >= 2 ** (level - 1), weight_ref[names[h], level] * scale, table
+            )
+        tables.append(jnp.where(column <= row, table, F32(0.0)))
     for i in range(tiles):
         own = slice(i * TILE, (i + 1) * TILE)
-        query, dmix, gain = query_ref[own], dmix_ref[own], gains[own]
-        mix = grad_query = None
         for j in range(i + 1):
             other = slice(j * TILE, (j + 1) * TILE)
-            key, value = key_ref[other], value_ref[other]
-            if i == j:
-                pair = gain * table
-            else:
-                pair = gain * (weight_ref[head, low + (i ^ j).bit_length()] * scale)
-            near = (pair * dot(query, key, CONTRACT_LAST)).astype(BF16)
-            grad = (pair * dot(dmix, value, CONTRACT_LAST)).astype(BF16)
-            terms = (
-                dot(near, value),
-                dot(grad, key),
-                dot(grad, query, CONTRACT_FIRST),
-                dot(near, dmix, CONTRACT_FIRST),
-            )
-            mix = terms[0] if mix is None else mix + terms[0]
-            grad_query = terms[1] if grad_query is None else grad_query + terms[1]
-            grad_keys[j] = terms[2] if grad_keys[j] is None else grad_keys[j] + terms[2]
-            grad_values[j] = terms[3] if grad_values[j] is None else grad_values[j] + terms[3]
-        mix_ref[own] = mix.astype(BF16)
-        grad_query_ref[own] = grad_query.astype(BF16)
+            thin = [slice(h * dk, (h + 1) * dk) for h in each]
+            wide = [slice(h * dv, (h + 1) * dv) for h in each]
+            scores = [dot(query_ref[own, thin[h]], key_ref[other, thin[h]], CONTRACT_LAST) for h in each]
+            slopes = [dot(dmix_ref[own, wide[h]], value_ref[other, wide[h]], CONTRACT_LAST) for h in each]
+            pairs = [
+                gains[h][own]
+                * (tables[h] if i == j else weight_ref[names[h], low + (i ^ j).bit_length()] * scale)
+                for h in each
+            ]
+            nears = [(pairs[h] * scores[h]).astype(BF16) for h in each]
+            grads = [(pairs[h] * slopes[h]).astype(BF16) for h in each]
+            for h in each:
+                add(mixes, (h, i), dot(nears[h], value_ref[other, wide[h]]))
+            for h in each:
+                add(grad_queries, (h, i), dot(grads[h], key_ref[other, thin[h]]))
+            for h in each:
+                add(grad_values, (h, j), dot(nears[h], dmix_ref[own, wide[h]], CONTRACT_FIRST))
+            for h in each:
+                add(grad_keys, (h, j), dot(grads[h], query_ref[own, thin[h]], CONTRACT_FIRST))
+        for h in each:
+            mix_ref[own, h * dv : (h + 1) * dv] = mixes[h, i].astype(BF16)
+            grad_query_ref[own, h * dk : (h + 1) * dk] = grad_queries[h, i].astype(BF16)
     for j in range(tiles):
         own = slice(j * TILE, (j + 1) * TILE)
-        grad_key_ref[own] = grad_keys[j].astype(BF16)
-        grad_value_ref[own] = grad_values[j].astype(BF16)
+        for h in each:
+            grad_key_ref[own, h * dk : (h + 1) * dk] = grad_keys[h, j].astype(BF16)
+            grad_value_ref[own, h * dv : (h + 1) * dv] = grad_values[h, j].astype(BF16)
 
 
 def near_terms(queries, keys, values, dmix, gain, level_weights, scale, heads):
     rows, dk, dv = keys.shape[0], keys.shape[1] // heads, values.shape[1] // heads
-    narrow = vmem((rows, dk), lambda h: (0, h))
-    wide = vmem((rows, dv), lambda h: (0, h))
+    narrow = vmem((rows, STEP_HEADS * dk), lambda h: (0, h))
+    wide = vmem((rows, STEP_HEADS * dv), lambda h: (0, h))
     thin, thick = (rows, heads * dk), (rows, heads * dv)
     return pl.pallas_call(
         functools.partial(near_kernel, scale),
-        grid=(heads,),
+        grid=(heads // STEP_HEADS,),
         in_specs=[smem(), narrow, narrow, wide, wide, vmem(gain.shape, lambda h: (0, 0))],
         out_specs=[wide, narrow, narrow, wide],
         out_shape=[pltpu.HBM(shape, BF16) for shape in (thick, thin, thin, thick)],
@@ -297,13 +392,12 @@
 
 
 def share_kernel(
-    scale, heads, count, index_ref, query_hbm, joined_ref, mix_hbm, gain_ref, weight_hbm, *rest
+    scale, heads, count, index_ref, query_hbm, own_ref, came_ref, mix_hbm, gain_ref, weight_hbm, *rest
 ):
     share_refs, (query, mix, weight, mixture, sems) = rest[: 2 * count], rest[2 * count :]
     rows, dk = query.shape[0], query.shape[1] // heads
-    dv = joined_ref.shape[2]
+    dv = own_ref.shape[1]
     each = rows // count
-    some = joined_ref.shape[0] // heads
     half = weight.shape[1] // 2
     query_load = pltpu.make_async_copy(query_hbm, query, sems.at[0])
     mix_load = pltpu.make_async_copy(mix_hbm, mix, sems.at[1])
@@ -320,7 +414,7 @@
     query_load.wait()
     mix_load.wait()
     for h in range(heads):
-        past = joined_ref[h * some : (h + 1) * some, : dk // some].reshape(dk, dv)
+        past = state_of(index_ref[1], own_ref, came_ref, h, heads, dk)
         far = dot(query[:, h * dk : (h + 1) * dk], past)
         own = slice(h * dv, (h + 1) * dv)
         piece = (mix[:, own].astype(F32) + (column_of(gain_ref, h) * scale) * far).astype(BF16)
@@ -335,14 +429,14 @@
             share_refs[side * count + step][...] = share[step * each : (step + 1) * each]
 
 
-def shares_of(index, queries, joined, mix, gain, weight, scale, heads, count):
+def shares_of(index, queries, own, came, mix, gain, weight, scale, heads, count):
     rows, dk = queries.shape[0], queries.shape[1] // heads
-    dv, half = joined.shape[2], weight.shape[1] // 2
+    dv, half = own.shape[1], weight.shape[1] // 2
     share = jax.ShapeDtypeStruct((rows // count, half), BF16)
     queries, mix, weight = in_hbm(queries, mix, weight)
     shares = pl.pallas_call(
         functools.partial(share_kernel, scale, heads, count),
-        in_specs=[smem(), hbm(), vmem(), hbm(), vmem(), hbm()],
+        in_specs=[smem(), hbm(), vmem(), vmem(), hbm(), vmem(), hbm()],
         out_specs=[vmem()] * (2 * count),
         out_shape=[share] * (2 * count),
         scratch_shapes=[
@@ -355,7 +449,7 @@
         cost_estimate=cost(2 * rows * dv * heads * (dk + 2 * half), 4 * half * (rows + heads * dv)),
         compiler_params=pltpu.CompilerParams(vmem_limit_bytes=LARGE),
         name="shares",
-    )(index, queries, joined, mix, gain, weight)
+    )(index, queries, own, came, mix, gain, weight)
     return shares[:count], shares[count:]
 
 
@@ -397,10 +491,10 @@
 
 
 def far_past_kernel(
-    scale, heads, dmix_hbm, gain_ref, joined_ref, near_hbm, grad_hbm, dmix, near, grad, sems
+    scale, heads, core_ref, dmix_hbm, gain_ref, own_ref, came_ref, near_hbm, grad_hbm,
+    dmix, near, grad, sems,
 ):
     dk, dv = near.shape[1] // heads, dmix.shape[1] // heads
-    some = joined_ref.shape[0] // heads
     loads, stores = [], []
     for h in range(heads):
         for n, (source, target, size) in enumerate(((dmix_hbm, dmix, dv), (near_hbm, near, dk))):
@@ -408,7 +502,7 @@
             loads.append(pltpu.make_async_copy(source.at[:, at], target.at[:, at], sems.at[n, h]))
             loads[-1].start()
     for h in range(heads):
-        past = joined_ref[h * some : (h + 1) * some, : dk // some].reshape(dk, dv)
+        past = state_of(core_ref[0], own_ref, came_ref, h, heads, dk)
         for load in loads[2 * h : 2 * h + 2]:
             load.wait()
         far = dot(dmix[:, h * dv : (h + 1) * dv], past, CONTRACT_LAST)
@@ -421,12 +515,12 @@
         store.wait()
 
 
-def far_past(dmix, gain, joined, near, scale, heads):
+def far_past(core, dmix, gain, own, came, near, scale, heads):
     rows, dk, dv = near.shape[0], near.shape[1] // heads, dmix.shape[1] // heads
     dmix, near = in_hbm(dmix, near)
     return pl.pallas_call(
         functools.partial(far_past_kernel, scale, heads),
-        in_specs=[hbm(), vmem(), vmem(), hbm()],
+        in_specs=[smem(), hbm(), vmem(), vmem(), vmem(), hbm()],
         out_specs=hbm(),
         out_shape=pltpu.HBM(near.shape, BF16),
         scratch_shapes=[
@@ -438,15 +532,14 @@
         cost_estimate=cost(2 * rows * dk * dv * heads, 2 * rows * heads * (2 * dk + dv)),
         compiler_params=pltpu.CompilerParams(vmem_limit_bytes=SMALL),
         name="far_past",
-    )(dmix, gain, joined, near)
+    )(core, dmix, gain, own, came, near)
 
 
 def far_future_kernel(
-    scale, heads, key_hbm, value_hbm, future_ref, near_key_hbm, near_value_hbm,
+    scale, heads, core_ref, key_hbm, value_hbm, own_ref, came_ref, near_key_hbm, near_value_hbm,
     grad_key_hbm, grad_value_hbm, key, value, near_key, near_value, grad_key, grad_value, sems,
 ):
     dk, dv = key.shape[1] // heads, value.shape[1] // heads
-    some = future_ref.shape[0] // heads
     loads, stores = [], []
     for h in range(heads):
         thin, thick = pl.ds(h * dk, dk), pl.ds(h * dv, dv)
@@ -464,7 +557,7 @@
     for h in range(heads):
         thin, thick = pl.ds(h * dk, dk), pl.ds(h * dv, dv)
         narrow, wide = slice(h * dk, (h + 1) * dk), slice(h * dv, (h + 1) * dv)
-        future = future_ref[h * some : (h + 1) * some].reshape(dk, dv)
+        future = state_of(core_ref[0], own_ref, came_ref, h, heads, dk)
         for load in loads[4 * h : 4 * h + 2]:
             load.wait()
         far_key = dot(value[:, wide], future, CONTRACT_LAST)
@@ -485,13 +578,13 @@
         store.wait()
 
 
-def far_future(keys, values, future, near_keys, near_values, scale, heads):
+def far_future(core, keys, values, own, came, near_keys, near_values, scale, heads):
     rows, dk, dv = keys.shape[0], keys.shape[1] // heads, values.shape[1] // heads
     thin, thick = keys.shape, values.shape
     keys, values, near_keys, near_values = in_hbm(keys, values, near_keys, near_values)
     return pl.pallas_call(
         functools.partial(far_future_kernel, scale, heads),
-        in_specs=[hbm(), hbm(), vmem(), hbm(), hbm()],
+        in_specs=[smem(), hbm(), hbm(), vmem(), vmem(), hbm(), hbm()],
         out_specs=[hbm()] * 2,
         out_shape=[pltpu.HBM(thin, BF16), pltpu.HBM(thick, BF16)],
         scratch_shapes=[
@@ -501,16 +594,17 @@
         cost_estimate=cost(4 * rows * dk * dv * heads, 6 * rows * heads * (dk + dv)),
         compiler_params=pltpu.CompilerParams(vmem_limit_bytes=LARGE),
         name="far_future",
-    )(keys, values, future, near_keys, near_values)
-
-
-def in_pieces(states, axis):
-    count = lax.axis_size(axis)
-    return states.reshape(count, states.shape[0] // count, states.shape[1])
-
-
-def swapped(pieces, axis):
-    return lax.all_to_all(pieces, axis, split_axis=0, concat_axis=0, tiled=True)
+    )(core, keys, values, own, came, near_keys, near_values)
+
+
+def swapped(pieces, axis, groups):
+    return lax.all_to_all(
+        pieces, axis, split_axis=0, concat_axis=0, tiled=True, axis_index_groups=groups
+    )
+
+
+def from_sibling(value, axis):
+    return lax.ppermute(value, axis, [(i, i ^ 1) for i in range(lax.axis_size(axis))])
 
 
 def turned(value, axis, step):
@@ -539,28 +633,42 @@
     shift_bits = rows.bit_length() - 1
     level_weights = level_weights_of(level_gain)
     gain = query_gain
-    head = lax.axis_index("seq") // (seq_count // heads)
-    scan_weights = lax.dynamic_slice(level_weights, (head, shift_bits + 1), (1, bits))
-
-    key_states = key_state(key_vectors, value_vectors, heads)
-    key_pieces = swapped(in_pieces(key_states, "seq"), "seq")
-    dmix, query_states = mix_grad(out_grad, out_weight, query_vectors, gain, heads)
-    past_pieces = scan_past(key_pieces, in_pieces(query_states, "seq"), scan_weights)
-    joined = swapped(past_pieces, "seq")
+    chips = seq_count // 2
+    groups = [[2 * chip + core for chip in range(chips)] for core in range(2)]
+    chip, core = lax.axis_index("seq") // 2, lax.axis_index("seq") % 2
+    head = core * (heads // 2) + chip * (heads // 2) // chips
+    scan_weights = lax.dynamic_slice(level_weights, (head, shift_bits + 2), (1, bits - 1))
+    pair_weights = lax.dynamic_slice(
+        level_weights, (core * (heads // 2), shift_bits + 1), (heads // 2, 1)
+    )
+    index = jnp.stack([lax.axis_index("head"), core])
+    core = core.reshape(1)
+
+    key_mine, key_sent = key_state(core, key_vectors, value_vectors, heads)
+    key_other = from_sibling(key_sent, "seq")
+    key_pieces = swapped(chip_sum(key_mine, key_other, chips), "seq", groups)
+    dmix, query_mine, query_sent = mix_grad(core, out_grad, out_weight, query_vectors, gain, heads)
+    query_other = from_sibling(query_sent, "seq")
+    past_pieces = scan_past(key_pieces, query_mine, query_other, scan_weights)
+    joined = swapped(past_pieces, "seq", groups)
     mix, near_queries, near_keys, near_values = near_terms(
         query_vectors, key_vectors, value_vectors, dmix, gain, level_weights, scale, heads
     )
-    index = lax.axis_index("head").reshape(1)
-    head_count = lax.axis_size("head")
+    past_own, past_sent = parts_of(core, pair_weights, joined, key_mine, key_other, True)
+    past_came = from_sibling(past_sent, "seq")
     left, right = shares_of(
-        index, query_vectors, joined, mix, gain, out_weight, scale, heads, head_count
+        index, query_vectors, past_own, past_came, mix, gain, out_weight, scale, heads,
+        lax.axis_size("head"),
     )
     layer_out = summed_shares(left, right, "head")
-    grad_queries = far_past(dmix, gain, joined, near_queries, scale, heads)
+    grad_queries = far_past(core, dmix, gain, past_own, past_came, near_queries, scale, heads)
     future_pieces = scan_future(joined, scan_weights)
-    future = swapped(future_pieces, "seq")
+    future = swapped(future_pieces, "seq", groups)
+    future_own, future_sent = parts_of(core, pair_weights, future, query_mine, query_other, False)
+    future_came = from_sibling(future_sent, "seq")
     grad_keys, grad_values = far_future(
-        key_vectors, value_vectors, future, near_keys, near_values, scale, heads
+        core, key_vectors, value_vectors, future_own, future_came, near_keys, near_values,
+        scale, heads,
     )
     return (layer_out, grad_queries, grad_keys, grad_values)
 

time: 90.1 us -> 94.5 us (1.049)
  waiting for transfers between devices: 20.4 us -> 24.8 us
  starting transfers between devices: 32.2 us -> 33.4 us
    ppermute x0 -> x4, starting transfers between devices: none -> 8.7 us  [from_sibling(): lax.ppermute(value, axis, [(i, i ^ 1) for i in range(lax.axis_size(axis))])]
    all_to_all x3, starting transfers between devices: 24.7 us -> 17.1 us  [swapped(): lax.all_to_all(pieces, axis, split_axis=0, concat_axis=0, tiled=True, axi...]
    all_to_all x3, waiting for transfers between devices: 20.3 us -> 24.5 us  [swapped(): lax.all_to_all(pieces, axis, split_axis=0, concat_axis=0, tiled=True, axi...]
    pallas_call x4 -> x7, Pallas kernels: 18.3 us -> 17.5 us  [the longest x1 6.43 us: mix_grad(): pl.pallas_call(functools.partial(mix_grad_kernel, heads), in_specs=[smem(...]
  transfers between devices with their start and end apart: 9 -> 13, of which waited for: 4 -> 4; matrix products, arithmetic and copies ran while one was open for 1% -> 0% of each run, Pallas kernels for 26% -> 23%
where the time goes in v3:
time: 94.5 us; the launch traced here: 94.1 us
  Pallas kernels  34.1 us (36%)
  starting transfers between devices  33.4 us (35%)
  waiting for transfers between devices  24.8 us (26%)
    all_to_all x3, waiting for transfers between devices, swapped(): lax.all_to_all(pieces, axis, split_axis=0, concat_axis=0, tiled=True, axi...  24.5 us
    all_to_all x3, starting transfers between devices, swapped(): lax.all_to_all(pieces, axis, split_axis=0, concat_axis=0, tiled=True, axi...  17.1 us
    ppermute x4, starting transfers between devices, from_sibling(): lax.ppermute(value, axis, [(i, i ^ 1) for i in range(lax.axis_size(axis))])  8.7 us
    ppermute x6, starting transfers between devices, turned(): lax.ppermute(value, axis, [(i, (i + step) % count) for i in range(count)])  7.69 us
    pallas_call x1, Pallas kernels, shares_of(): pl.pallas_call(functools.partial(share_kernel, scale, heads, count), in_s...  7.04 us
    pallas_call x1, Pallas kernels, mix_grad(): pl.pallas_call(functools.partial(mix_grad_kernel, heads), in_specs=[smem(...  6.43 us
    pallas_call x1, Pallas kernels, near_terms(): pl.pallas_call(functools.partial(near_kernel, scale), grid=(heads // STEP...  5.65 us
    pallas_call x1, Pallas kernels, far_future(): pl.pallas_call(functools.partial(far_future_kernel, scale, heads), in_spe...  4.15 us
  transfers between devices with their start and end apart: 13, of which 4 were waited for; matrix products, arithmetic and copies ran while one was open for 0% of the time, Pallas kernels for 23%

profile of v3, /device:TPU:1, one launch (start us, length us, event | category | flops | bytes accessed | tf_op | source)
XLA Modules:
  0.0 94.1 jit_solution(14081926513829624065)
XLA Ops:
  0.6 2.1 %key_state.1 = (bf16[256,256]{1,0:T(8,128)(2,1)S(1)}, bf16[256,256]{1,0:T(8,128)(2,1)S(1)}) custom-call(s32[1]{0:T(128)} %bitcast.1.core_ref, bf16[512,512]{1,0:T(8,128)(2,1)} %key_hbm.3, bf16[512,1024]{1,0:T(8,128)(2,1)} %value_hbm.3), custom_call_target="tpu_custom_call" | custom-call | flops 134217728 | bytes 1572864 | tf_op jit(solution)/shard_map/key_state/pallas_call | solution.py:92
  2.7 3.3 %collective-permute-start = (bf16[256,256]{1,0:T(8,128)(2,1)S(1)}, bf16[256,256]{1,0:T(8,128)(2,1)S(1)}, u32[]{:S(2)}, u32[]{:S(2)}) collective-permute-start(bf16[256,256]{1,0:T(8,128)(2,1)S(1)} %get-tuple-element.28), channel_id=1, source_target_pairs={{0,4},{4,0},{8,12},{12,8},{16,20},{20,16},{24,28},{28,24},{32,36},... | collective-permute-start | bytes 393224 | tf_op jit(solution)/shard_map/ppermute | solution.py:607
  6.0 0.7 copy-done
  6.7 6.4 %mix_grad.1 = (bf16[512,1024]{1,0:T(8,128)(2,1)}, bf16[256,256]{1,0:T(8,128)(2,1)S(1)}, bf16[256,256]{1,0:T(8,128)(2,1)S(1)}) custom-call(s32[1]{0:T(128)} %bitcast.1.core_ref, bf16[512,2304]{1,0:T(8,128)(2,1)} %grad_hbm.1, bf16[1024,2304]{1,0:T(8,128)(2,1)} %weight_hbm.3, bf16[512,512]{1,0:T(8,128)(2,1)} %query_hbm.3, f32[4,512]{1,0:T(4,128)S(1)} %copy-done), custom_call_target="tpu_custom_call" | custom-call | flops 2550136832 | bytes 7077888 | tf_op jit(solution)/shard_map/mix_grad/pallas_call | solution.py:170
  13.3 0.7 chip_sum.1
  14.0 9.3 %all-to-all-start = ((bf16[32,8,256]{2,1,0:T(8,128)(2,1)}), bf16[32,8,256]{2,1,0:T(8,128)(2,1)S(1)}, u32[]{:S(2)}, u32[]{:S(2)}) async-start(bf16[32,8,256]{2,1,0:T(8,128)(2,1)} %chip_sum.1), calls=%async_computation | async-start | bytes 262144 | tf_op jit(solution)/shard_map/all_to_all | solution.py:601
  23.5 9.2 %all-to-all-done.pieces_ref = bf16[32,8,256]{2,1,0:T(8,128)(2,1)S(1)} async-done(((bf16[32,8,256]{2,1,0:T(8,128)(2,1)}), bf16[32,8,256]{2,1,0:T(8,128)(2,1)S(1)}, u32[]{:S(2)}, u32[]{:S(2)}) %all-to-all-start) | async-done | bytes 131104 | tf_op jit(solution)/shard_map/all_to_all | solution.py:601
  32.7 1.3 %scan_past.1 = bf16[32,16,256]{2,1,0:T(8,128)(2,1)} custom-call(f32[1,5]{1,0:T(1,128)S(1)} %constant_dynamic-slice_fusion.weight_ref, bf16[32,8,256]{2,1,0:T(8,128)(2,1)S(1)} %all-to-all-done.pieces_ref, bf16[256,256]{1,0:T(8,128)(2,1)S(1)} %get-tuple-element.29.mine_ref, bf16[256,256]{1,0:T(8,128)(2,1)S(1)} %collective-permute-done.1.other_ref), custom_call_target="tpu_custom_call" | custom-call | flops 262144 | bytes 524288 | tf_op jit(solution)/shard_map/scan_past/pallas_call | solution.py:247
  34.0 3.9 %all-to-all-start.1 = ((bf16[32,16,256]{2,1,0:T(8,128)(2,1)}), bf16[32,16,256]{2,1,0:T(8,128)(2,1)S(1)}, u32[]{:S(2)}, u32[]{:S(2)}) async-start(bf16[32,16,256]{2,1,0:T(8,128)(2,1)} %scan_past.1), calls=%async_computation.1 | async-start | bytes 524288 | tf_op jit(solution)/shard_map/all_to_all | solution.py:601
  37.9 10.5 %all-to-all-done.1.shared_ref.pieces_ref = bf16[32,16,256]{2,1,0:T(8,128)(2,1)S(1)} async-done(((bf16[32,16,256]{2,1,0:T(8,128)(2,1)}), bf16[32,16,256]{2,1,0:T(8,128)(2,1)S(1)}, u32[]{:S(2)}, u32[]{:S(2)}) %all-to-all-start.1) | async-done | bytes 262176 | tf_op jit(solution)/shard_map/all_to_all | solution.py:601
  49.1 3.6 %collective-permute-start.2 = (bf16[256,256]{1,0:T(8,128)(2,1)S(1)}, bf16[256,256]{1,0:T(8,128)(2,1)S(1)}, u32[]{:S(2)}, u32[]{:S(2)}) collective-permute-start(bf16[256,256]{1,0:T(8,128)(2,1)S(1)} %get-tuple-element.32), channel_id=1, source_target_pairs={{0,4},{4,0},{8,12},{12,8},{16,20},{20,16},{24,28},{28,24},{32,36},... | collective-permute-start | bytes 393224 | tf_op jit(solution)/shard_map/ppermute | solution.py:607
  52.7 5.6 %near_terms.1 = (bf16[512,1024]{1,0:T(8,128)(2,1)}, bf16[512,512]{1,0:T(8,128)(2,1)}, bf16[512,512]{1,0:T(8,128)(2,1)}, bf16[512,1024]{1,0:T(8,128)(2,1)}) custom-call(f32[4,21]{1,0:T(4,128)S(1)} %broadcast_multiply_fusion.weight_ref, bf16[512,512]{1,0:T(8,128)(2,1)} %query_hbm.3, bf16[512,512]{1,0:T(8,128)(2,1)} %key_hbm.3, bf16[512,1024]{1,0:T(8,128)(2,1)} %value_hbm.3, ...), custom_call_target="tpu_custom_call" | custom-call | flops 1811939328 | bytes 6291456 | tf_op jit(solution)/shard_map/near_terms/pallas_call | solution.py:382
  58.4 7.0 %shares.1 = (bf16[128,1152]{1,0:T(8,128)(2,1)S(1)}, bf16[128,1152]{1,0:T(8,128)(2,1)S(1)}, bf16[128,1152]{1,0:T(8,128)(2,1)S(1)}, bf16[128,1152]{1,0:T(8,128)(2,...) custom-call(s32[2]{0:T(128)S(1)} %pad_add_fusion.index_ref, ...), custom_call_target="tpu_custom_call" | custom-call | flops 2550136832 | bytes 7077888 | tf_op jit(solution)/shard_map/shares/pallas_call | solution.py:437
  65.4 1.4 %collective-permute-start.3 = (bf16[128,1152]{1,0:T(8,128)(2,1)S(1)}, bf16[128,1152]{1,0:T(8,128)(2,1)S(1)}, u32[]{:S(2)}, u32[]{:S(2)}) collective-permute-start(bf16[128,1152]{1,0:T(8,128)(2,1)S(1)} %get-tuple-element.37), channel_id=1, source_target_pairs={{0,1},{1,2},{2,3},{3,0},{4,5},{5,6},{6,7},{7,4},{8,9},{9,10},{10,1... | collective-permute-start | bytes 884744 | tf_op jit(solution)/shard_map/ppermute | solution.py:612
  66.8 1.7 %collective-permute-start.7 = (bf16[128,1152]{1,0:T(8,128)(2,1)}, bf16[128,1152]{1,0:T(8,128)(2,1)S(1)}, u32[]{:S(2)}, u32[]{:S(2)}) collective-permute-start(bf16[128,1152]{1,0:T(8,128)(2,1)} %get-tuple-element.42), channel_id=1, source_target_pairs={{0,3},{1,0},{2,1},{3,2},{4,7},{5,4},{6,5},{7,6},{8,11},{9,8},{10,9... | collective-permute-start | bytes 884744 | tf_op jit(solution)/shard_map/ppermute | solution.py:612
  68.5 1.2 %scan_future.1 = bf16[32,8,256]{2,1,0:T(8,128)(2,1)} custom-call(f32[1,5]{1,0:T(1,128)S(1)} %constant_dynamic-slice_fusion.weight_ref, bf16[32,16,256]{2,1,0:T(8,128)(2,1)S(1)} %all-to-all-done.1.shared_ref.pieces_ref), custom_call_target="tpu_custom_call" | custom-call | flops 262144 | bytes 262144 | tf_op jit(solution)/shard_map/scan_future/pallas_call | solution.py:304
  69.8 3.9 %all-to-all-start.2 = ((bf16[32,8,256]{2,1,0:T(8,128)(2,1)}), bf16[32,8,256]{2,1,0:T(8,128)(2,1)S(1)}, u32[]{:S(2)}, u32[]{:S(2)}) async-start(bf16[32,8,256]{2,1,0:T(8,128)(2,1)} %scan_future.1), calls=%async_computation.2 | async-start | bytes 262144 | tf_op jit(solution)/shard_map/all_to_all | solution.py:601
  73.6 1.3 %collective-permute-start.5 = (bf16[128,1152]{1,0:T(8,128)(2,1)}, bf16[128,1152]{1,0:T(8,128)(2,1)S(1)}, u32[]{:S(2)}, u32[]{:S(2)}) collective-permute-start(bf16[128,1152]{1,0:T(8,128)(2,1)} %get-tuple-element.38), channel_id=1, source_target_pairs={{0,3},{1,0},{2,1},{3,2},{4,7},{5,4},{6,5},{7,6},{8,11},{9,8},{10,9... | collective-permute-start | bytes 884744 | tf_op jit(solution)/shard_map/ppermute | solution.py:612
  75.7 3.0 %collective-permute-start.8 = (bf16[128,1152]{1,0:T(8,128)(2,1)S(1)}, bf16[128,1152]{1,0:T(8,128)(2,1)S(1)}, u32[]{:S(2)}, u32[]{:S(2)}) collective-permute-start(bf16[128,1152]{1,0:T(8,128)(2,1)S(1)} %added.3), channel_id=1, source_target_pairs={{0,3},{1,0},{2,1},{3,2},{4,7},{5,4},{6,5},{7,6},{8,11},{9,8},{10,9... | collective-permute-start | bytes 884744 | tf_op jit(solution)/shard_map/ppermute | solution.py:612
  78.6 4.8 %all-to-all-done.2.shared_ref = bf16[32,8,256]{2,1,0:T(8,128)(2,1)S(1)} async-done(((bf16[32,8,256]{2,1,0:T(8,128)(2,1)}), bf16[32,8,256]{2,1,0:T(8,128)(2,1)S(1)}, u32[]{:S(2)}, u32[]{:S(2)}) %all-to-all-start.2) | async-done | bytes 131104 | tf_op jit(solution)/shard_map/all_to_all | solution.py:601
  84.1 1.7 %collective-permute-start.9 = (bf16[256,256]{1,0:T(8,128)(2,1)S(1)}, bf16[256,256]{1,0:T(8,128)(2,1)S(1)}, u32[]{:S(2)}, u32[]{:S(2)}) collective-permute-start(bf16[256,256]{1,0:T(8,128)(2,1)S(1)} %get-tuple-element.45), channel_id=1, source_target_pairs={{0,4},{4,0},{8,12},{12,8},{16,20},{20,16},{24,28},{28,24},{32,36},... | collective-permute-start | bytes 393224 | tf_op jit(solution)/shard_map/ppermute | solution.py:607
  85.9 3.0 %far_past.1 = bf16[512,512]{1,0:T(8,128)(2,1)} custom-call(s32[1]{0:T(128)} %bitcast.1.core_ref, bf16[512,1024]{1,0:T(8,128)(2,1)} %get-tuple-element.33.dmix_ref.dmix_hbm, f32[4,512]{1,0:T(4,128)S(1)} %copy-done.1, bf16[256,256]{1,0:T(8,128)(2,1)S(1)} %get-tuple-element.31.own_ref, bf16[256,256]{1,0:T(8,128)(2,1)S(1)} %collective-permute-done.2.came_ref, ...), custom_call_target="tpu_custom_call" | custom-call | flops 134217728 | bytes 2097152 | tf_op jit(solution)/shard_map/far_past/pallas_call | solution.py:521
  88.9 4.1 %far_future.1 = (bf16[512,512]{1,0:T(8,128)(2,1)}, bf16[512,1024]{1,0:T(8,128)(2,1)}) custom-call(s32[1]{0:T(128)} %bitcast.1.core_ref, bf16[512,512]{1,0:T(8,128)(2,1)} %key_hbm.3, bf16[512,1024]{1,0:T(8,128)(2,1)} %value_hbm.3, bf16[256,256]{1,0:T(8,128)(2,1)S(1)} %get-tuple-element.44.own_ref, bf16[256,256]{1,0:T(8,128)(2,1)S(1)} %collective-permute-done.9.came_ref, ...), custom_call_target="tpu_custom_call" | custom-call | flops 268435456 | bytes 4718592 | tf_op jit(solution)/shard_map/far_future/pallas_call | solution.py:585
  93.1 1.0 %total.1 = bf16[128,2304]{1,0:T(8,128)(2,1)} custom-call(bf16[128,1152]{1,0:T(8,128)(2,1)S(1)} %get-tuple-element.35.refs_0_, bf16[128,1152]{1,0:T(8,128)(2,1)S(1)} %collective-permute-done.4.refs_1_, bf16[128,1152]{1,0:T(8,128)(2,1)S(1)} %collective-permute-done.5.refs_2_, bf16[128,1152]{1,0:T(8,128)(2,1)S(1)} %get-tuple-element.39.refs_3_, ...), custom_call_target="tpu_custom_call" | custom-call | flops 589824 | bytes 2359296 | tf_op jit(solution)/shard_map/total/pallas_call | solution.py:482
  (27 shorter events, 2.4 us)
Async XLA Ops:
  2.7 10.5 %collective-permute-start = (bf16[256,256]{1,0:T(8,128)(2,1)S(1)}, bf16[256,256]{1,0:T(8,128)(2,1)S(1)}, u32[]{:S(2)}, u32[]{:S(2)}) collective-permute-start(bf16[256,256]{1,0:T(8,128)(2,1)S(1)} %get-tuple-element.28), channel_id=1, source_target_pairs={{0,4},{4,0},{8,12},{12,8},{16,20},{20,16},{24,28},{28,24},{32,36},... | collective-permute-start | bytes 393224 | tf_op jit(solution)/shard_map/ppermute | solution.py:607
  6.0 0.7 copy-start
  6.7 16.6 %copy-start.2 = (f32[4,21]{1,0:T(4,128)S(1)}, f32[4,21]{1,0:T(4,128)}, u32[]{:S(2)}) copy-start(f32[4,21]{1,0:T(4,128)} %param.11) | copy-start | bytes 1012
  6.7 46.0 %copy-start.1 = (f32[4,512]{1,0:T(4,128)S(1)}, f32[4,512]{1,0:T(4,128)}, u32[]{:S(2)}) copy-start(f32[4,512]{1,0:T(4,128)} %gain_ref.7) | copy-start | bytes 24580
  13.2 10.3 %collective-permute-start.1 = (bf16[256,256]{1,0:T(8,128)(2,1)S(1)}, bf16[256,256]{1,0:T(8,128)(2,1)S(1)}, u32[]{:S(2)}, u32[]{:S(2)}) collective-permute-start(bf16[256,256]{1,0:T(8,128)(2,1)S(1)} %get-tuple-element.30), channel_id=1, source_target_pairs={{0,4},{4,0},{8,12},{12,8},{16,20},{20,16},{24,28},{28,24},{32,36},... | collective-permute-start | bytes 393224 | tf_op jit(solution)/shard_map/ppermute | solution.py:607
  14.0 18.7 %all-to-all-start = ((bf16[32,8,256]{2,1,0:T(8,128)(2,1)}), bf16[32,8,256]{2,1,0:T(8,128)(2,1)S(1)}, u32[]{:S(2)}, u32[]{:S(2)}) async-start(bf16[32,8,256]{2,1,0:T(8,128)(2,1)} %chip_sum.1), calls=%async_computation | async-start | bytes 262144 | tf_op jit(solution)/shard_map/all_to_all | solution.py:601
  34.0 14.5 %all-to-all-start.1 = ((bf16[32,16,256]{2,1,0:T(8,128)(2,1)}), bf16[32,16,256]{2,1,0:T(8,128)(2,1)S(1)}, u32[]{:S(2)}, u32[]{:S(2)}) async-start(bf16[32,16,256]{2,1,0:T(8,128)(2,1)} %scan_past.1), calls=%async_computation.1 | async-start | bytes 524288 | tf_op jit(solution)/shard_map/all_to_all | solution.py:601
  49.1 9.3 %collective-permute-start.2 = (bf16[256,256]{1,0:T(8,128)(2,1)S(1)}, bf16[256,256]{1,0:T(8,128)(2,1)S(1)}, u32[]{:S(2)}, u32[]{:S(2)}) collective-permute-start(bf16[256,256]{1,0:T(8,128)(2,1)S(1)} %get-tuple-element.32), channel_id=1, source_target_pairs={{0,4},{4,0},{8,12},{12,8},{16,20},{20,16},{24,28},{28,24},{32,36},... | collective-permute-start | bytes 393224 | tf_op jit(solution)/shard_map/ppermute | solution.py:607
  65.4 10.0 %collective-permute-start.3 = (bf16[128,1152]{1,0:T(8,128)(2,1)S(1)}, bf16[128,1152]{1,0:T(8,128)(2,1)S(1)}, u32[]{:S(2)}, u32[]{:S(2)}) collective-permute-start(bf16[128,1152]{1,0:T(8,128)(2,1)S(1)} %get-tuple-element.37), channel_id=1, source_target_pairs={{0,1},{1,2},{2,3},{3,0},{4,5},{5,6},{6,7},{7,4},{8,9},{9,10},{10,1... | collective-permute-start | bytes 884744 | tf_op jit(solution)/shard_map/ppermute | solution.py:612
  66.8 8.8 %collective-permute-start.7 = (bf16[128,1152]{1,0:T(8,128)(2,1)}, bf16[128,1152]{1,0:T(8,128)(2,1)S(1)}, u32[]{:S(2)}, u32[]{:S(2)}) collective-permute-start(bf16[128,1152]{1,0:T(8,128)(2,1)} %get-tuple-element.42), channel_id=1, source_target_pairs={{0,3},{1,0},{2,1},{3,2},{4,7},{5,4},{6,5},{7,6},{8,11},{9,8},{10,9... | collective-permute-start | bytes 884744 | tf_op jit(solution)/shard_map/ppermute | solution.py:612
  69.8 13.7 %all-to-all-start.2 = ((bf16[32,8,256]{2,1,0:T(8,128)(2,1)}), bf16[32,8,256]{2,1,0:T(8,128)(2,1)S(1)}, u32[]{:S(2)}, u32[]{:S(2)}) async-start(bf16[32,8,256]{2,1,0:T(8,128)(2,1)} %scan_future.1), calls=%async_computation.2 | async-start | bytes 262144 | tf_op jit(solution)/shard_map/all_to_all | solution.py:601
  73.6 19.4 %collective-permute-start.5 = (bf16[128,1152]{1,0:T(8,128)(2,1)}, bf16[128,1152]{1,0:T(8,128)(2,1)S(1)}, u32[]{:S(2)}, u32[]{:S(2)}) collective-permute-start(bf16[128,1152]{1,0:T(8,128)(2,1)} %get-tuple-element.38), channel_id=1, source_target_pairs={{0,3},{1,0},{2,1},{3,2},{4,7},{5,4},{6,5},{7,6},{8,11},{9,8},{10,9... | collective-permute-start | bytes 884744 | tf_op jit(solution)/shard_map/ppermute | solution.py:612
  74.9 18.2 %collective-permute-start.6 = (bf16[128,1152]{1,0:T(8,128)(2,1)}, bf16[128,1152]{1,0:T(8,128)(2,1)S(1)}, u32[]{:S(2)}, u32[]{:S(2)}) collective-permute-start(bf16[128,1152]{1,0:T(8,128)(2,1)} %get-tuple-element.40), channel_id=1, source_target_pairs={{0,1},{1,2},{2,3},{3,0},{4,5},{5,6},{6,7},{7,4},{8,9},{9,10},{10,1... | collective-permute-start | bytes 884744 | tf_op jit(solution)/shard_map/ppermute | solution.py:612
  75.5 17.6 %collective-permute-start.4 = (bf16[128,1152]{1,0:T(8,128)(2,1)S(1)}, bf16[128,1152]{1,0:T(8,128)(2,1)S(1)}, u32[]{:S(2)}, u32[]{:S(2)}) collective-permute-start(bf16[128,1152]{1,0:T(8,128)(2,1)S(1)} %added.2), channel_id=1, source_target_pairs={{0,1},{1,2},{2,3},{3,0},{4,5},{5,6},{6,7},{7,4},{8,9},{9,10},{10,1... | collective-permute-start | bytes 884744 | tf_op jit(solution)/shard_map/ppermute | solution.py:612
  75.7 17.4 %collective-permute-start.8 = (bf16[128,1152]{1,0:T(8,128)(2,1)S(1)}, bf16[128,1152]{1,0:T(8,128)(2,1)S(1)}, u32[]{:S(2)}, u32[]{:S(2)}) collective-permute-start(bf16[128,1152]{1,0:T(8,128)(2,1)S(1)} %added.3), channel_id=1, source_target_pairs={{0,3},{1,0},{2,1},{3,2},{4,7},{5,4},{6,5},{7,6},{8,11},{9,8},{10,9... | collective-permute-start | bytes 884744 | tf_op jit(solution)/shard_map/ppermute | solution.py:612
  84.1 4.8 %collective-permute-start.9 = (bf16[256,256]{1,0:T(8,128)(2,1)S(1)}, bf16[256,256]{1,0:T(8,128)(2,1)S(1)}, u32[]{:S(2)}, u32[]{:S(2)}) collective-permute-start(bf16[256,256]{1,0:T(8,128)(2,1)S(1)} %get-tuple-element.45), channel_id=1, source_target_pairs={{0,4},{4,0},{8,12},{12,8},{16,20},{20,16},{24,28},{28,24},{32,36},... | collective-permute-start | bytes 393224 | tf_op jit(solution)/shard_map/ppermute | solution.py:607

commit v4 on v3

--- a/solution.py
+++ b/solution.py
@@ -107,8 +107,8 @@
 
 
 def mix_grad_kernel(
-    heads, core_ref, grad_hbm, weight_hbm, query_hbm, gain_ref, dmix_hbm, mine_ref, other_ref,
-    dmix, grad, weight, query, state, sems,
+    heads, core_ref, grad_hbm, weight_hbm, query_hbm, gain_hbm, dmix_hbm, mine_ref, other_ref,
+    dmix, grad, weight, query, state, gain_ref, sems,
 ):
     dk, dv = query.shape[1] // heads, weight.shape[0] // heads
     pair = 2 * dv
@@ -129,6 +129,7 @@
             )
         )
     query_load = started(6, query_hbm, query)
+    gain_load = started(6 + heads, gain_hbm, gain_ref)
     loads = [None] + [
         started(6 + n, weight_hbm.at[pl.ds(n * pair, pair)], weight.at[pl.ds(n * pair, pair)])
         for n in range(1, heads // 2)
@@ -154,6 +155,7 @@
         stores.append(started(base + n, dmix.at[:, at], dmix_hbm.at[:, at]))
         if n == 0:
             query_load.wait()
+            gain_load.wait()
         for h in (2 * n, 2 * n + 1):
             own = piece[:, (h - 2 * n) * dv : (h - 2 * n + 1) * dv].astype(F32)
             gained = (own * column_of(gain_ref, h)).astype(BF16)
@@ -169,7 +171,7 @@
     dv, dk = out_weight.shape[0] // heads, queries.shape[1] // heads
     return pl.pallas_call(
         functools.partial(mix_grad_kernel, heads),
-        in_specs=[smem(), hbm(), hbm(), hbm(), vmem()],
+        in_specs=[smem(), hbm(), hbm(), hbm(), hbm()],
         out_specs=[hbm(), vmem(), vmem()],
         out_shape=[
             pltpu.HBM((rows, heads * dv), BF16),
@@ -182,12 +184,13 @@
             pltpu.VMEM(out_weight.shape, BF16),
             pltpu.VMEM(queries.shape, BF16),
             pltpu.VMEM((heads * dk, dv), BF16),
-            pltpu.SemaphoreType.DMA((6 + heads,)),
+            pltpu.VMEM(gain.shape, F32),
+            pltpu.SemaphoreType.DMA((7 + heads,)),
         ],
         cost_estimate=cost(2 * rows * dv * heads * (width + dk), 2 * (rows + dv * heads) * width),
         compiler_params=pltpu.CompilerParams(vmem_limit_bytes=LARGE),
         name="mix_grad",
-    )(core, *in_hbm(out_grad, out_weight, queries), gain)
+    )(core, *in_hbm(out_grad, out_weight, queries, gain))
 
 
 def scan_pieces(earlier, weight_ref, pieces_ref, write):
@@ -388,7 +391,7 @@
         cost_estimate=cost(1.5 * rows * rows * heads * 3 * (dk + dv), 8 * rows * heads * (dk + dv)),
         compiler_params=pltpu.CompilerParams(vmem_limit_bytes=LARGE),
         name="near_terms",
-    )(level_weights, *in_hbm(queries, keys, values, dmix), gain)
+    )(level_weights, *in_hbm(queries, keys, values, dmix, gain))
 
 
 def share_kernel(

time: 94.5 us -> 93.9 us (level)
  transfers between devices with their start and end apart: 13 -> 13, of which waited for: 4 -> 4; matrix products, arithmetic and copies ran while one was open for 0% -> 0% of each run, Pallas kernels for 23% -> 24%
where the time goes in v4:
time: 93.9 us; the launch traced here: 93.6 us
  Pallas kernels  34.2 us (36%)
  starting transfers between devices  33.5 us (36%)
  waiting for transfers between devices  24.8 us (26%)
    all_to_all x3, waiting for transfers between devices, swapped(): lax.all_to_all(pieces, axis, split_axis=0, concat_axis=0, tiled=True, axi...  24.6 us
    all_to_all x3, starting transfers between devices, swapped(): lax.all_to_all(pieces, axis, split_axis=0, concat_axis=0, tiled=True, axi...  17.1 us
    ppermute x4, starting transfers between devices, from_sibling(): lax.ppermute(value, axis, [(i, i ^ 1) for i in range(lax.axis_size(axis))])  8.71 us
    ppermute x6, starting transfers between devices, turned(): lax.ppermute(value, axis, [(i, (i + step) % count) for i in range(count)])  7.69 us
    pallas_call x1, Pallas kernels, shares_of(): pl.pallas_call(functools.partial(share_kernel, scale, heads, count), in_s...  7.04 us
    pallas_call x1, Pallas kernels, mix_grad(): pl.pallas_call(functools.partial(mix_grad_kernel, heads), in_specs=[smem(...  6.41 us
    pallas_call x1, Pallas kernels, near_terms(): pl.pallas_call(functools.partial(near_kernel, scale), grid=(heads // STEP...  5.76 us
    pallas_call x1, Pallas kernels, far_future(): pl.pallas_call(functools.partial(far_future_kernel, scale, heads), in_spe...  4.15 us
  transfers between devices with their start and end apart: 13, of which 4 were waited for; matrix products, arithmetic and copies ran while one was open for 0% of the time, Pallas kernels for 24%

profile of v4, /device:TPU:1, one launch (start us, length us, event | category | flops | bytes accessed | tf_op | source)
XLA Modules:
  0.0 93.6 jit_solution(4801277091446296305)
XLA Ops:
  0.6 2.1 %key_state.1 = (bf16[256,256]{1,0:T(8,128)(2,1)S(1)}, bf16[256,256]{1,0:T(8,128)(2,1)S(1)}) custom-call(s32[1]{0:T(128)} %bitcast.1.core_ref, bf16[512,512]{1,0:T(8,128)(2,1)} %key_hbm.3, bf16[512,1024]{1,0:T(8,128)(2,1)} %value_hbm.3), custom_call_target="tpu_custom_call" | custom-call | flops 134217728 | bytes 1572864 | tf_op jit(solution)/shard_map/key_state/pallas_call | solution.py:92
  2.7 3.3 %collective-permute-start = (bf16[256,256]{1,0:T(8,128)(2,1)S(1)}, bf16[256,256]{1,0:T(8,128)(2,1)S(1)}, u32[]{:S(2)}, u32[]{:S(2)}) collective-permute-start(bf16[256,256]{1,0:T(8,128)(2,1)S(1)} %get-tuple-element.28), channel_id=1, source_target_pairs={{0,4},{4,0},{8,12},{12,8},{16,20},{20,16},{24,28},{28,24},{32,36},... | collective-permute-start | bytes 393224 | tf_op jit(solution)/shard_map/ppermute | solution.py:610
  6.0 6.4 %mix_grad.1 = (bf16[512,1024]{1,0:T(8,128)(2,1)}, bf16[256,256]{1,0:T(8,128)(2,1)S(1)}, bf16[256,256]{1,0:T(8,128)(2,1)S(1)}) custom-call(s32[1]{0:T(128)} %bitcast.1.core_ref, bf16[512,2304]{1,0:T(8,128)(2,1)} %grad_hbm.1, bf16[1024,2304]{1,0:T(8,128)(2,1)} %weight_hbm.3, bf16[512,512]{1,0:T(8,128)(2,1)} %query_hbm.3, f32[4,512]{1,0:T(4,128)} %gain_ref.5), custom_call_target="tpu_custom_call" | custom-call | flops 2550136832 | bytes 7077888 | tf_op jit(solution)/shard_map/mix_grad/pallas_call | solution.py:172
  12.6 0.7 chip_sum.1
  13.3 9.3 %all-to-all-start = ((bf16[32,8,256]{2,1,0:T(8,128)(2,1)}), bf16[32,8,256]{2,1,0:T(8,128)(2,1)S(1)}, u32[]{:S(2)}, u32[]{:S(2)}) async-start(bf16[32,8,256]{2,1,0:T(8,128)(2,1)} %chip_sum.1), calls=%async_computation | async-start | bytes 262144 | tf_op jit(solution)/shard_map/all_to_all | solution.py:604
  22.8 9.2 %all-to-all-done.pieces_ref = bf16[32,8,256]{2,1,0:T(8,128)(2,1)S(1)} async-done(((bf16[32,8,256]{2,1,0:T(8,128)(2,1)}), bf16[32,8,256]{2,1,0:T(8,128)(2,1)S(1)}, u32[]{:S(2)}, u32[]{:S(2)}) %all-to-all-start) | async-done | bytes 131104 | tf_op jit(solution)/shard_map/all_to_all | solution.py:604
  32.0 1.3 %scan_past.1 = bf16[32,16,256]{2,1,0:T(8,128)(2,1)} custom-call(f32[1,5]{1,0:T(1,128)S(1)} %constant_dynamic-slice_fusion.weight_ref, bf16[32,8,256]{2,1,0:T(8,128)(2,1)S(1)} %all-to-all-done.pieces_ref, bf16[256,256]{1,0:T(8,128)(2,1)S(1)} %get-tuple-element.29.mine_ref, bf16[256,256]{1,0:T(8,128)(2,1)S(1)} %collective-permute-done.1.other_ref), custom_call_target="tpu_custom_call" | custom-call | flops 262144 | bytes 524288 | tf_op jit(solution)/shard_map/scan_past/pallas_call | solution.py:250
  33.3 3.9 %all-to-all-start.1 = ((bf16[32,16,256]{2,1,0:T(8,128)(2,1)}), bf16[32,16,256]{2,1,0:T(8,128)(2,1)S(1)}, u32[]{:S(2)}, u32[]{:S(2)}) async-start(bf16[32,16,256]{2,1,0:T(8,128)(2,1)} %scan_past.1), calls=%async_computation.1 | async-start | bytes 524288 | tf_op jit(solution)/shard_map/all_to_all | solution.py:604
  37.2 10.5 %all-to-all-done.1.shared_ref.pieces_ref = bf16[32,16,256]{2,1,0:T(8,128)(2,1)S(1)} async-done(((bf16[32,16,256]{2,1,0:T(8,128)(2,1)}), bf16[32,16,256]{2,1,0:T(8,128)(2,1)S(1)}, u32[]{:S(2)}, u32[]{:S(2)}) %all-to-all-start.1) | async-done | bytes 262176 | tf_op jit(solution)/shard_map/all_to_all | solution.py:604
  47.7 0.6 past_parts.1
  48.4 3.6 %collective-permute-start.2 = (bf16[256,256]{1,0:T(8,128)(2,1)S(1)}, bf16[256,256]{1,0:T(8,128)(2,1)S(1)}, u32[]{:S(2)}, u32[]{:S(2)}) collective-permute-start(bf16[256,256]{1,0:T(8,128)(2,1)S(1)} %get-tuple-element.32), channel_id=1, source_target_pairs={{0,4},{4,0},{8,12},{12,8},{16,20},{20,16},{24,28},{28,24},{32,36},... | collective-permute-start | bytes 393224 | tf_op jit(solution)/shard_map/ppermute | solution.py:610
  52.0 5.8 %near_terms.1 = (bf16[512,1024]{1,0:T(8,128)(2,1)}, bf16[512,512]{1,0:T(8,128)(2,1)}, bf16[512,512]{1,0:T(8,128)(2,1)}, bf16[512,1024]{1,0:T(8,128)(2,1)}) custom-call(f32[4,21]{1,0:T(4,128)S(1)} %broadcast_multiply_fusion.weight_ref, bf16[512,512]{1,0:T(8,128)(2,1)} %query_hbm.3, bf16[512,512]{1,0:T(8,128)(2,1)} %key_hbm.3, bf16[512,1024]{1,0:T(8,128)(2,1)} %value_hbm.3, ...), custom_call_target="tpu_custom_call" | custom-call | flops 1811939328 | bytes 6291456 | tf_op jit(solution)/shard_map/near_terms/pallas_call | solution.py:385
  57.8 7.0 %shares.1 = (bf16[128,1152]{1,0:T(8,128)(2,1)S(1)}, bf16[128,1152]{1,0:T(8,128)(2,1)S(1)}, bf16[128,1152]{1,0:T(8,128)(2,1)S(1)}, bf16[128,1152]{1,0:T(8,128)(2,...) custom-call(s32[2]{0:T(128)S(1)} %pad_add_fusion.index_ref, ...), custom_call_target="tpu_custom_call" | custom-call | flops 2550136832 | bytes 7077888 | tf_op jit(solution)/shard_map/shares/pallas_call | solution.py:440
  64.9 1.4 %collective-permute-start.3 = (bf16[128,1152]{1,0:T(8,128)(2,1)S(1)}, bf16[128,1152]{1,0:T(8,128)(2,1)S(1)}, u32[]{:S(2)}, u32[]{:S(2)}) collective-permute-start(bf16[128,1152]{1,0:T(8,128)(2,1)S(1)} %get-tuple-element.37), channel_id=1, source_target_pairs={{0,1},{1,2},{2,3},{3,0},{4,5},{5,6},{6,7},{7,4},{8,9},{9,10},{10,1... | collective-permute-start | bytes 884744 | tf_op jit(solution)/shard_map/ppermute | solution.py:615
  66.2 1.7 %collective-permute-start.7 = (bf16[128,1152]{1,0:T(8,128)(2,1)}, bf16[128,1152]{1,0:T(8,128)(2,1)S(1)}, u32[]{:S(2)}, u32[]{:S(2)}) collective-permute-start(bf16[128,1152]{1,0:T(8,128)(2,1)} %get-tuple-element.42), channel_id=1, source_target_pairs={{0,3},{1,0},{2,1},{3,2},{4,7},{5,4},{6,5},{7,6},{8,11},{9,8},{10,9... | collective-permute-start | bytes 884744 | tf_op jit(solution)/shard_map/ppermute | solution.py:615
  67.9 1.2 %scan_future.1 = bf16[32,8,256]{2,1,0:T(8,128)(2,1)} custom-call(f32[1,5]{1,0:T(1,128)S(1)} %constant_dynamic-slice_fusion.weight_ref, bf16[32,16,256]{2,1,0:T(8,128)(2,1)S(1)} %all-to-all-done.1.shared_ref.pieces_ref), custom_call_target="tpu_custom_call" | custom-call | flops 262144 | bytes 262144 | tf_op jit(solution)/shard_map/scan_future/pallas_call | solution.py:307
  69.2 3.9 %all-to-all-start.2 = ((bf16[32,8,256]{2,1,0:T(8,128)(2,1)}), bf16[32,8,256]{2,1,0:T(8,128)(2,1)S(1)}, u32[]{:S(2)}, u32[]{:S(2)}) async-start(bf16[32,8,256]{2,1,0:T(8,128)(2,1)} %scan_future.1), calls=%async_computation.2 | async-start | bytes 262144 | tf_op jit(solution)/shard_map/all_to_all | solution.py:604
  73.1 1.3 %collective-permute-start.5 = (bf16[128,1152]{1,0:T(8,128)(2,1)}, bf16[128,1152]{1,0:T(8,128)(2,1)S(1)}, u32[]{:S(2)}, u32[]{:S(2)}) collective-permute-start(bf16[128,1152]{1,0:T(8,128)(2,1)} %get-tuple-element.38), channel_id=1, source_target_pairs={{0,3},{1,0},{2,1},{3,2},{4,7},{5,4},{6,5},{7,6},{8,11},{9,8},{10,9... | collective-permute-start | bytes 884744 | tf_op jit(solution)/shard_map/ppermute | solution.py:615
  75.1 3.0 %collective-permute-start.8 = (bf16[128,1152]{1,0:T(8,128)(2,1)S(1)}, bf16[128,1152]{1,0:T(8,128)(2,1)S(1)}, u32[]{:S(2)}, u32[]{:S(2)}) collective-permute-start(bf16[128,1152]{1,0:T(8,128)(2,1)S(1)} %added.3), channel_id=1, source_target_pairs={{0,3},{1,0},{2,1},{3,2},{4,7},{5,4},{6,5},{7,6},{8,11},{9,8},{10,9... | collective-permute-start | bytes 884744 | tf_op jit(solution)/shard_map/ppermute | solution.py:615
  78.0 4.9 %all-to-all-done.2.shared_ref = bf16[32,8,256]{2,1,0:T(8,128)(2,1)S(1)} async-done(((bf16[32,8,256]{2,1,0:T(8,128)(2,1)}), bf16[32,8,256]{2,1,0:T(8,128)(2,1)S(1)}, u32[]{:S(2)}, u32[]{:S(2)}) %all-to-all-start.2) | async-done | bytes 131104 | tf_op jit(solution)/shard_map/all_to_all | solution.py:604
  83.6 1.7 %collective-permute-start.9 = (bf16[256,256]{1,0:T(8,128)(2,1)S(1)}, bf16[256,256]{1,0:T(8,128)(2,1)S(1)}, u32[]{:S(2)}, u32[]{:S(2)}) collective-permute-start(bf16[256,256]{1,0:T(8,128)(2,1)S(1)} %get-tuple-element.45), channel_id=1, source_target_pairs={{0,4},{4,0},{8,12},{12,8},{16,20},{20,16},{24,28},{28,24},{32,36},... | collective-permute-start | bytes 393224 | tf_op jit(solution)/shard_map/ppermute | solution.py:610
  85.3 3.0 %far_past.1 = bf16[512,512]{1,0:T(8,128)(2,1)} custom-call(s32[1]{0:T(128)} %bitcast.1.core_ref, bf16[512,1024]{1,0:T(8,128)(2,1)} %get-tuple-element.33.dmix_ref.dmix_hbm, f32[4,512]{1,0:T(4,128)S(1)} %copy-done, bf16[256,256]{1,0:T(8,128)(2,1)S(1)} %get-tuple-element.31.own_ref, bf16[256,256]{1,0:T(8,128)(2,1)S(1)} %collective-permute-done.2.came_ref, ...), custom_call_target="tpu_custom_call" | custom-call | flops 134217728 | bytes 2097152 | tf_op jit(solution)/shard_map/far_past/pallas_call | solution.py:524
  88.3 4.1 %far_future.1 = (bf16[512,512]{1,0:T(8,128)(2,1)}, bf16[512,1024]{1,0:T(8,128)(2,1)}) custom-call(s32[1]{0:T(128)} %bitcast.1.core_ref, bf16[512,512]{1,0:T(8,128)(2,1)} %key_hbm.3, bf16[512,1024]{1,0:T(8,128)(2,1)} %value_hbm.3, bf16[256,256]{1,0:T(8,128)(2,1)S(1)} %get-tuple-element.44.own_ref, bf16[256,256]{1,0:T(8,128)(2,1)S(1)} %collective-permute-done.9.came_ref, ...), custom_call_target="tpu_custom_call" | custom-call | flops 268435456 | bytes 4718592 | tf_op jit(solution)/shard_map/far_future/pallas_call | solution.py:588
  92.5 1.0 %total.1 = bf16[128,2304]{1,0:T(8,128)(2,1)} custom-call(bf16[128,1152]{1,0:T(8,128)(2,1)S(1)} %get-tuple-element.35.refs_0_, bf16[128,1152]{1,0:T(8,128)(2,1)S(1)} %collective-permute-done.4.refs_1_, bf16[128,1152]{1,0:T(8,128)(2,1)S(1)} %collective-permute-done.5.refs_2_, bf16[128,1152]{1,0:T(8,128)(2,1)S(1)} %get-tuple-element.39.refs_3_, ...), custom_call_target="tpu_custom_call" | custom-call | flops 589824 | bytes 2359296 | tf_op jit(solution)/shard_map/total/pallas_call | solution.py:485
  (25 shorter events, 1.7 us)
Async XLA Ops:
  2.7 19.9 %copy-start.1 = (f32[4,21]{1,0:T(4,128)S(1)}, f32[4,21]{1,0:T(4,128)}, u32[]{:S(2)}) copy-start(f32[4,21]{1,0:T(4,128)} %param.11) | copy-start | bytes 1012
  2.7 9.8 %collective-permute-start = (bf16[256,256]{1,0:T(8,128)(2,1)S(1)}, bf16[256,256]{1,0:T(8,128)(2,1)S(1)}, u32[]{:S(2)}, u32[]{:S(2)}) collective-permute-start(bf16[256,256]{1,0:T(8,128)(2,1)S(1)} %get-tuple-element.28), channel_id=1, source_target_pairs={{0,4},{4,0},{8,12},{12,8},{16,20},{20,16},{24,28},{28,24},{32,36},... | collective-permute-start | bytes 393224 | tf_op jit(solution)/shard_map/ppermute | solution.py:610
  12.5 45.4 %copy-start = (f32[4,512]{1,0:T(4,128)S(1)}, f32[4,512]{1,0:T(4,128)}, u32[]{:S(2)}) copy-start(f32[4,512]{1,0:T(4,128)} %gain_ref.5) | copy-start | bytes 24580
  12.5 10.3 %collective-permute-start.1 = (bf16[256,256]{1,0:T(8,128)(2,1)S(1)}, bf16[256,256]{1,0:T(8,128)(2,1)S(1)}, u32[]{:S(2)}, u32[]{:S(2)}) collective-permute-start(bf16[256,256]{1,0:T(8,128)(2,1)S(1)} %get-tuple-element.30), channel_id=1, source_target_pairs={{0,4},{4,0},{8,12},{12,8},{16,20},{20,16},{24,28},{28,24},{32,36},... | collective-permute-start | bytes 393224 | tf_op jit(solution)/shard_map/ppermute | solution.py:610
  13.3 18.7 %all-to-all-start = ((bf16[32,8,256]{2,1,0:T(8,128)(2,1)}), bf16[32,8,256]{2,1,0:T(8,128)(2,1)S(1)}, u32[]{:S(2)}, u32[]{:S(2)}) async-start(bf16[32,8,256]{2,1,0:T(8,128)(2,1)} %chip_sum.1), calls=%async_computation | async-start | bytes 262144 | tf_op jit(solution)/shard_map/all_to_all | solution.py:604
  33.3 14.5 %all-to-all-start.1 = ((bf16[32,16,256]{2,1,0:T(8,128)(2,1)}), bf16[32,16,256]{2,1,0:T(8,128)(2,1)S(1)}, u32[]{:S(2)}, u32[]{:S(2)}) async-start(bf16[32,16,256]{2,1,0:T(8,128)(2,1)} %scan_past.1), calls=%async_computation.1 | async-start | bytes 524288 | tf_op jit(solution)/shard_map/all_to_all | solution.py:604
  48.4 9.4 %collective-permute-start.2 = (bf16[256,256]{1,0:T(8,128)(2,1)S(1)}, bf16[256,256]{1,0:T(8,128)(2,1)S(1)}, u32[]{:S(2)}, u32[]{:S(2)}) collective-permute-start(bf16[256,256]{1,0:T(8,128)(2,1)S(1)} %get-tuple-element.32), channel_id=1, source_target_pairs={{0,4},{4,0},{8,12},{12,8},{16,20},{20,16},{24,28},{28,24},{32,36},... | collective-permute-start | bytes 393224 | tf_op jit(solution)/shard_map/ppermute | solution.py:610
  64.9 9.9 %collective-permute-start.3 = (bf16[128,1152]{1,0:T(8,128)(2,1)S(1)}, bf16[128,1152]{1,0:T(8,128)(2,1)S(1)}, u32[]{:S(2)}, u32[]{:S(2)}) collective-permute-start(bf16[128,1152]{1,0:T(8,128)(2,1)S(1)} %get-tuple-element.37), channel_id=1, source_target_pairs={{0,1},{1,2},{2,3},{3,0},{4,5},{5,6},{6,7},{7,4},{8,9},{9,10},{10,1... | collective-permute-start | bytes 884744 | tf_op jit(solution)/shard_map/ppermute | solution.py:615
  66.2 8.7 %collective-permute-start.7 = (bf16[128,1152]{1,0:T(8,128)(2,1)}, bf16[128,1152]{1,0:T(8,128)(2,1)S(1)}, u32[]{:S(2)}, u32[]{:S(2)}) collective-permute-start(bf16[128,1152]{1,0:T(8,128)(2,1)} %get-tuple-element.42), channel_id=1, source_target_pairs={{0,3},{1,0},{2,1},{3,2},{4,7},{5,4},{6,5},{7,6},{8,11},{9,8},{10,9... | collective-permute-start | bytes 884744 | tf_op jit(solution)/shard_map/ppermute | solution.py:615
  69.2 13.7 %all-to-all-start.2 = ((bf16[32,8,256]{2,1,0:T(8,128)(2,1)}), bf16[32,8,256]{2,1,0:T(8,128)(2,1)S(1)}, u32[]{:S(2)}, u32[]{:S(2)}) async-start(bf16[32,8,256]{2,1,0:T(8,128)(2,1)} %scan_future.1), calls=%async_computation.2 | async-start | bytes 262144 | tf_op jit(solution)/shard_map/all_to_all | solution.py:604
  73.1 19.4 %collective-permute-start.5 = (bf16[128,1152]{1,0:T(8,128)(2,1)}, bf16[128,1152]{1,0:T(8,128)(2,1)S(1)}, u32[]{:S(2)}, u32[]{:S(2)}) collective-permute-start(bf16[128,1152]{1,0:T(8,128)(2,1)} %get-tuple-element.38), channel_id=1, source_target_pairs={{0,3},{1,0},{2,1},{3,2},{4,7},{5,4},{6,5},{7,6},{8,11},{9,8},{10,9... | collective-permute-start | bytes 884744 | tf_op jit(solution)/shard_map/ppermute | solution.py:615
  74.3 18.2 %collective-permute-start.6 = (bf16[128,1152]{1,0:T(8,128)(2,1)}, bf16[128,1152]{1,0:T(8,128)(2,1)S(1)}, u32[]{:S(2)}, u32[]{:S(2)}) collective-permute-start(bf16[128,1152]{1,0:T(8,128)(2,1)} %get-tuple-element.40), channel_id=1, source_target_pairs={{0,1},{1,2},{2,3},{3,0},{4,5},{5,6},{6,7},{7,4},{8,9},{9,10},{10,1... | collective-permute-start | bytes 884744 | tf_op jit(solution)/shard_map/ppermute | solution.py:615
  74.9 17.6 %collective-permute-start.4 = (bf16[128,1152]{1,0:T(8,128)(2,1)S(1)}, bf16[128,1152]{1,0:T(8,128)(2,1)S(1)}, u32[]{:S(2)}, u32[]{:S(2)}) collective-permute-start(bf16[128,1152]{1,0:T(8,128)(2,1)S(1)} %added.2), channel_id=1, source_target_pairs={{0,1},{1,2},{2,3},{3,0},{4,5},{5,6},{6,7},{7,4},{8,9},{9,10},{10,1... | collective-permute-start | bytes 884744 | tf_op jit(solution)/shard_map/ppermute | solution.py:615
  75.1 17.5 %collective-permute-start.8 = (bf16[128,1152]{1,0:T(8,128)(2,1)S(1)}, bf16[128,1152]{1,0:T(8,128)(2,1)S(1)}, u32[]{:S(2)}, u32[]{:S(2)}) collective-permute-start(bf16[128,1152]{1,0:T(8,128)(2,1)S(1)} %added.3), channel_id=1, source_target_pairs={{0,3},{1,0},{2,1},{3,2},{4,7},{5,4},{6,5},{7,6},{8,11},{9,8},{10,9... | collective-permute-start | bytes 884744 | tf_op jit(solution)/shard_map/ppermute | solution.py:615
  83.6 4.8 %collective-permute-start.9 = (bf16[256,256]{1,0:T(8,128)(2,1)S(1)}, bf16[256,256]{1,0:T(8,128)(2,1)S(1)}, u32[]{:S(2)}, u32[]{:S(2)}) collective-permute-start(bf16[256,256]{1,0:T(8,128)(2,1)S(1)} %get-tuple-element.45), channel_id=1, source_target_pairs={{0,4},{4,0},{8,12},{12,8},{16,20},{20,16},{24,28},{28,24},{32,36},... | collective-permute-start | bytes 393224 | tf_op jit(solution)/shard_map/ppermute | solution.py:610

commit v5 on v4

--- a/solution.py
+++ b/solution.py
@@ -402,15 +402,17 @@
     dv = own_ref.shape[1]
     each = rows // count
     half = weight.shape[1] // 2
+    cut = -(-half // TILE) * TILE
+    spans = ((0, cut), (cut, 2 * half))
     query_load = pltpu.make_async_copy(query_hbm, query, sems.at[0])
     mix_load = pltpu.make_async_copy(mix_hbm, mix, sems.at[1])
     sides = [
         pltpu.make_async_copy(
-            weight_hbm.at[:, pl.ds(side * half, half)],
-            weight.at[:, pl.ds(side * half, half)],
+            weight_hbm.at[:, pl.ds(start, stop - start)],
+            weight.at[:, pl.ds(start, stop - start)],
             sems.at[2 + side],
         )
-        for side in range(2)
+        for side, (start, stop) in enumerate(spans)
     ]
     for load in (query_load, mix_load, *sides):
         load.start()
@@ -425,11 +427,16 @@
             place = lax.rem(c + count - index_ref[0], count)
             at = pl.ds(pl.multiple_of(place * each, each), each)
             mixture[at, own] = piece[c * each : (c + 1) * each]
-    for side in range(2):
+    for side, (start, stop) in enumerate(spans):
         sides[side].wait()
-        share = dot(mixture[...], weight[:, side * half : (side + 1) * half]).astype(BF16)
+        share = dot(mixture[...], weight[:, start:stop]).astype(BF16)
         for step in range(count):
-            share_refs[side * count + step][...] = share[step * each : (step + 1) * each]
+            part = share[step * each : (step + 1) * each]
+            if side == 0:
+                share_refs[step][...] = part[:, :half]
+                share_refs[count + step][:, : cut - half] = part[:, half:]
+            else:
+                share_refs[count + step][:, cut - half :] = part
 
 
 def shares_of(index, queries, own, came, mix, gain, weight, scale, heads, count):

time: 93.9 us -> 93.3 us (level)
  no operation moved by 1% of the time
where the time goes in v5:
time: 93.3 us; the launch traced here: 93 us
  Pallas kernels  33.6 us (36%)
  starting transfers between devices  33.4 us (36%)
  waiting for transfers between devices  24.8 us (27%)
    all_to_all x3, waiting for transfers between devices, swapped(): lax.all_to_all(pieces, axis, split_axis=0, concat_axis=0, tiled=True, axi...  24.6 us
    all_to_all x3, starting transfers between devices, swapped(): lax.all_to_all(pieces, axis, split_axis=0, concat_axis=0, tiled=True, axi...  17.2 us
    ppermute x4, starting transfers between devices, from_sibling(): lax.ppermute(value, axis, [(i, i ^ 1) for i in range(lax.axis_size(axis))])  8.92 us
    ppermute x6, starting transfers between devices, turned(): lax.ppermute(value, axis, [(i, (i + step) % count) for i in range(count)])  7.26 us
    pallas_call x1, Pallas kernels, shares_of(): pl.pallas_call(functools.partial(share_kernel, scale, heads, count), in_s...  6.46 us
    pallas_call x1, Pallas kernels, mix_grad(): pl.pallas_call(functools.partial(mix_grad_kernel, heads), in_specs=[smem(...  6.41 us
    pallas_call x1, Pallas kernels, near_terms(): pl.pallas_call(functools.partial(near_kernel, scale), grid=(heads // STEP...  5.76 us
    pallas_call x1, Pallas kernels, far_future(): pl.pallas_call(functools.partial(far_future_kernel, scale, heads), in_spe...  4.15 us
  transfers between devices with their start and end apart: 13, of which 4 were waited for; matrix products, arithmetic and copies ran while one was open for 0% of the time, Pallas kernels for 24%

profile of v5, /device:TPU:1, one launch (start us, length us, event | category | flops | bytes accessed | tf_op | source)
XLA Modules:
  0.0 93.0 jit_solution(11178256539679079993)
XLA Ops:
  0.6 2.1 %key_state.1 = (bf16[256,256]{1,0:T(8,128)(2,1)S(1)}, bf16[256,256]{1,0:T(8,128)(2,1)S(1)}) custom-call(s32[1]{0:T(128)} %bitcast.1.core_ref, bf16[512,512]{1,0:T(8,128)(2,1)} %key_hbm.3, bf16[512,1024]{1,0:T(8,128)(2,1)} %value_hbm.3), custom_call_target="tpu_custom_call" | custom-call | flops 134217728 | bytes 1572864 | tf_op jit(solution)/shard_map/key_state/pallas_call | solution.py:92
  2.7 3.3 %collective-permute-start = (bf16[256,256]{1,0:T(8,128)(2,1)S(1)}, bf16[256,256]{1,0:T(8,128)(2,1)S(1)}, u32[]{:S(2)}, u32[]{:S(2)}) collective-permute-start(bf16[256,256]{1,0:T(8,128)(2,1)S(1)} %get-tuple-element.28), channel_id=1, source_target_pairs={{0,4},{4,0},{8,12},{12,8},{16,20},{20,16},{24,28},{28,24},{32,36},... | collective-permute-start | bytes 393224 | tf_op jit(solution)/shard_map/ppermute | solution.py:617
  6.0 6.4 %mix_grad.1 = (bf16[512,1024]{1,0:T(8,128)(2,1)}, bf16[256,256]{1,0:T(8,128)(2,1)S(1)}, bf16[256,256]{1,0:T(8,128)(2,1)S(1)}) custom-call(s32[1]{0:T(128)} %bitcast.1.core_ref, bf16[512,2304]{1,0:T(8,128)(2,1)} %grad_hbm.1, bf16[1024,2304]{1,0:T(8,128)(2,1)} %weight_hbm.3, bf16[512,512]{1,0:T(8,128)(2,1)} %query_hbm.3, f32[4,512]{1,0:T(4,128)} %gain_ref.5), custom_call_target="tpu_custom_call" | custom-call | flops 2550136832 | bytes 7077888 | tf_op jit(solution)/shard_map/mix_grad/pallas_call | solution.py:172
  12.6 0.7 chip_sum.1
  13.3 9.3 %all-to-all-start = ((bf16[32,8,256]{2,1,0:T(8,128)(2,1)}), bf16[32,8,256]{2,1,0:T(8,128)(2,1)S(1)}, u32[]{:S(2)}, u32[]{:S(2)}) async-start(bf16[32,8,256]{2,1,0:T(8,128)(2,1)} %chip_sum.1), calls=%async_computation | async-start | bytes 262144 | tf_op jit(solution)/shard_map/all_to_all | solution.py:611
  22.8 9.2 %all-to-all-done.pieces_ref = bf16[32,8,256]{2,1,0:T(8,128)(2,1)S(1)} async-done(((bf16[32,8,256]{2,1,0:T(8,128)(2,1)}), bf16[32,8,256]{2,1,0:T(8,128)(2,1)S(1)}, u32[]{:S(2)}, u32[]{:S(2)}) %all-to-all-start) | async-done | bytes 131104 | tf_op jit(solution)/shard_map/all_to_all | solution.py:611
  32.0 1.3 %scan_past.1 = bf16[32,16,256]{2,1,0:T(8,128)(2,1)} custom-call(f32[1,5]{1,0:T(1,128)S(1)} %constant_dynamic-slice_fusion.weight_ref, bf16[32,8,256]{2,1,0:T(8,128)(2,1)S(1)} %all-to-all-done.pieces_ref, bf16[256,256]{1,0:T(8,128)(2,1)S(1)} %get-tuple-element.29.mine_ref, bf16[256,256]{1,0:T(8,128)(2,1)S(1)} %collective-permute-done.1.other_ref), custom_call_target="tpu_custom_call" | custom-call | flops 262144 | bytes 524288 | tf_op jit(solution)/shard_map/scan_past/pallas_call | solution.py:250
  33.3 3.9 %all-to-all-start.1 = ((bf16[32,16,256]{2,1,0:T(8,128)(2,1)}), bf16[32,16,256]{2,1,0:T(8,128)(2,1)S(1)}, u32[]{:S(2)}, u32[]{:S(2)}) async-start(bf16[32,16,256]{2,1,0:T(8,128)(2,1)} %scan_past.1), calls=%async_computation.1 | async-start | bytes 524288 | tf_op jit(solution)/shard_map/all_to_all | solution.py:611
  37.2 10.5 %all-to-all-done.1.shared_ref.pieces_ref = bf16[32,16,256]{2,1,0:T(8,128)(2,1)S(1)} async-done(((bf16[32,16,256]{2,1,0:T(8,128)(2,1)}), bf16[32,16,256]{2,1,0:T(8,128)(2,1)S(1)}, u32[]{:S(2)}, u32[]{:S(2)}) %all-to-all-start.1) | async-done | bytes 262176 | tf_op jit(solution)/shard_map/all_to_all | solution.py:611
  47.7 0.6 past_parts.1
  48.4 3.6 %collective-permute-start.2 = (bf16[256,256]{1,0:T(8,128)(2,1)S(1)}, bf16[256,256]{1,0:T(8,128)(2,1)S(1)}, u32[]{:S(2)}, u32[]{:S(2)}) collective-permute-start(bf16[256,256]{1,0:T(8,128)(2,1)S(1)} %get-tuple-element.32), channel_id=1, source_target_pairs={{0,4},{4,0},{8,12},{12,8},{16,20},{20,16},{24,28},{28,24},{32,36},... | collective-permute-start | bytes 393224 | tf_op jit(solution)/shard_map/ppermute | solution.py:617
  52.0 5.8 %near_terms.1 = (bf16[512,1024]{1,0:T(8,128)(2,1)}, bf16[512,512]{1,0:T(8,128)(2,1)}, bf16[512,512]{1,0:T(8,128)(2,1)}, bf16[512,1024]{1,0:T(8,128)(2,1)}) custom-call(f32[4,21]{1,0:T(4,128)S(1)} %broadcast_multiply_fusion.weight_ref, bf16[512,512]{1,0:T(8,128)(2,1)} %query_hbm.3, bf16[512,512]{1,0:T(8,128)(2,1)} %key_hbm.3, bf16[512,1024]{1,0:T(8,128)(2,1)} %value_hbm.3, ...), custom_call_target="tpu_custom_call" | custom-call | flops 1811939328 | bytes 6291456 | tf_op jit(solution)/shard_map/near_terms/pallas_call | solution.py:385
  57.8 6.5 %shares.1 = (bf16[128,1152]{1,0:T(8,128)(2,1)S(1)}, bf16[128,1152]{1,0:T(8,128)(2,1)S(1)}, bf16[128,1152]{1,0:T(8,128)(2,1)S(1)}, bf16[128,1152]{1,0:T(8,128)(2,...) custom-call(s32[2]{0:T(128)S(1)} %pad_add_fusion.index_ref, ...), custom_call_target="tpu_custom_call" | custom-call | flops 2550136832 | bytes 7077888 | tf_op jit(solution)/shard_map/shares/pallas_call | solution.py:447
  64.3 1.4 %collective-permute-start.3 = (bf16[128,1152]{1,0:T(8,128)(2,1)S(1)}, bf16[128,1152]{1,0:T(8,128)(2,1)S(1)}, u32[]{:S(2)}, u32[]{:S(2)}) collective-permute-start(bf16[128,1152]{1,0:T(8,128)(2,1)S(1)} %get-tuple-element.37), channel_id=1, source_target_pairs={{0,1},{1,2},{2,3},{3,0},{4,5},{5,6},{6,7},{7,4},{8,9},{9,10},{10,1... | collective-permute-start | bytes 884744 | tf_op jit(solution)/shard_map/ppermute | solution.py:622
  65.7 1.5 %collective-permute-start.7 = (bf16[128,1152]{1,0:T(8,128)(2,1)}, bf16[128,1152]{1,0:T(8,128)(2,1)S(1)}, u32[]{:S(2)}, u32[]{:S(2)}) collective-permute-start(bf16[128,1152]{1,0:T(8,128)(2,1)} %get-tuple-element.42), channel_id=1, source_target_pairs={{0,3},{1,0},{2,1},{3,2},{4,7},{5,4},{6,5},{7,6},{8,11},{9,8},{10,9... | collective-permute-start | bytes 884744 | tf_op jit(solution)/shard_map/ppermute | solution.py:622
  67.2 1.2 %scan_future.1 = bf16[32,8,256]{2,1,0:T(8,128)(2,1)} custom-call(f32[1,5]{1,0:T(1,128)S(1)} %constant_dynamic-slice_fusion.weight_ref, bf16[32,16,256]{2,1,0:T(8,128)(2,1)S(1)} %all-to-all-done.1.shared_ref.pieces_ref), custom_call_target="tpu_custom_call" | custom-call | flops 262144 | bytes 262144 | tf_op jit(solution)/shard_map/scan_future/pallas_call | solution.py:307
  68.4 4.0 %all-to-all-start.2 = ((bf16[32,8,256]{2,1,0:T(8,128)(2,1)}), bf16[32,8,256]{2,1,0:T(8,128)(2,1)S(1)}, u32[]{:S(2)}, u32[]{:S(2)}) async-start(bf16[32,8,256]{2,1,0:T(8,128)(2,1)} %scan_future.1), calls=%async_computation.2 | async-start | bytes 262144 | tf_op jit(solution)/shard_map/all_to_all | solution.py:611
  72.5 1.5 %collective-permute-start.5 = (bf16[128,1152]{1,0:T(8,128)(2,1)}, bf16[128,1152]{1,0:T(8,128)(2,1)S(1)}, u32[]{:S(2)}, u32[]{:S(2)}) collective-permute-start(bf16[128,1152]{1,0:T(8,128)(2,1)} %get-tuple-element.38), channel_id=1, source_target_pairs={{0,3},{1,0},{2,1},{3,2},{4,7},{5,4},{6,5},{7,6},{8,11},{9,8},{10,9... | collective-permute-start | bytes 884744 | tf_op jit(solution)/shard_map/ppermute | solution.py:622
  74.5 2.7 %collective-permute-start.8 = (bf16[128,1152]{1,0:T(8,128)(2,1)S(1)}, bf16[128,1152]{1,0:T(8,128)(2,1)S(1)}, u32[]{:S(2)}, u32[]{:S(2)}) collective-permute-start(bf16[128,1152]{1,0:T(8,128)(2,1)S(1)} %added.3), channel_id=1, source_target_pairs={{0,3},{1,0},{2,1},{3,2},{4,7},{5,4},{6,5},{7,6},{8,11},{9,8},{10,9... | collective-permute-start | bytes 884744 | tf_op jit(solution)/shard_map/ppermute | solution.py:622
  77.2 4.9 %all-to-all-done.2.shared_ref = bf16[32,8,256]{2,1,0:T(8,128)(2,1)S(1)} async-done(((bf16[32,8,256]{2,1,0:T(8,128)(2,1)}), bf16[32,8,256]{2,1,0:T(8,128)(2,1)S(1)}, u32[]{:S(2)}, u32[]{:S(2)}) %all-to-all-start.2) | async-done | bytes 131104 | tf_op jit(solution)/shard_map/all_to_all | solution.py:611
  82.8 1.9 %collective-permute-start.9 = (bf16[256,256]{1,0:T(8,128)(2,1)S(1)}, bf16[256,256]{1,0:T(8,128)(2,1)S(1)}, u32[]{:S(2)}, u32[]{:S(2)}) collective-permute-start(bf16[256,256]{1,0:T(8,128)(2,1)S(1)} %get-tuple-element.45), channel_id=1, source_target_pairs={{0,4},{4,0},{8,12},{12,8},{16,20},{20,16},{24,28},{28,24},{32,36},... | collective-permute-start | bytes 393224 | tf_op jit(solution)/shard_map/ppermute | solution.py:617
  84.7 3.0 %far_past.1 = bf16[512,512]{1,0:T(8,128)(2,1)} custom-call(s32[1]{0:T(128)} %bitcast.1.core_ref, bf16[512,1024]{1,0:T(8,128)(2,1)} %get-tuple-element.33.dmix_ref.dmix_hbm, f32[4,512]{1,0:T(4,128)S(1)} %copy-done, bf16[256,256]{1,0:T(8,128)(2,1)S(1)} %get-tuple-element.31.own_ref, bf16[256,256]{1,0:T(8,128)(2,1)S(1)} %collective-permute-done.2.came_ref, ...), custom_call_target="tpu_custom_call" | custom-call | flops 134217728 | bytes 2097152 | tf_op jit(solution)/shard_map/far_past/pallas_call | solution.py:531
  87.8 4.1 %far_future.1 = (bf16[512,512]{1,0:T(8,128)(2,1)}, bf16[512,1024]{1,0:T(8,128)(2,1)}) custom-call(s32[1]{0:T(128)} %bitcast.1.core_ref, bf16[512,512]{1,0:T(8,128)(2,1)} %key_hbm.3, bf16[512,1024]{1,0:T(8,128)(2,1)} %value_hbm.3, bf16[256,256]{1,0:T(8,128)(2,1)S(1)} %get-tuple-element.44.own_ref, bf16[256,256]{1,0:T(8,128)(2,1)S(1)} %collective-permute-done.9.came_ref, ...), custom_call_target="tpu_custom_call" | custom-call | flops 268435456 | bytes 4718592 | tf_op jit(solution)/shard_map/far_future/pallas_call | solution.py:595
  92.0 1.0 %total.1 = bf16[128,2304]{1,0:T(8,128)(2,1)} custom-call(bf16[128,1152]{1,0:T(8,128)(2,1)S(1)} %get-tuple-element.35.refs_0_, bf16[128,1152]{1,0:T(8,128)(2,1)S(1)} %collective-permute-done.4.refs_1_, bf16[128,1152]{1,0:T(8,128)(2,1)S(1)} %collective-permute-done.5.refs_2_, bf16[128,1152]{1,0:T(8,128)(2,1)S(1)} %get-tuple-element.39.refs_3_, ...), custom_call_target="tpu_custom_call" | custom-call | flops 589824 | bytes 2359296 | tf_op jit(solution)/shard_map/total/pallas_call | solution.py:492
  (25 shorter events, 1.6 us)
Async XLA Ops:
  2.7 19.9 %copy-start.1 = (f32[4,21]{1,0:T(4,128)S(1)}, f32[4,21]{1,0:T(4,128)}, u32[]{:S(2)}) copy-start(f32[4,21]{1,0:T(4,128)} %param.11) | copy-start | bytes 1012
  2.7 9.8 %collective-permute-start = (bf16[256,256]{1,0:T(8,128)(2,1)S(1)}, bf16[256,256]{1,0:T(8,128)(2,1)S(1)}, u32[]{:S(2)}, u32[]{:S(2)}) collective-permute-start(bf16[256,256]{1,0:T(8,128)(2,1)S(1)} %get-tuple-element.28), channel_id=1, source_target_pairs={{0,4},{4,0},{8,12},{12,8},{16,20},{20,16},{24,28},{28,24},{32,36},... | collective-permute-start | bytes 393224 | tf_op jit(solution)/shard_map/ppermute | solution.py:617
  12.5 45.4 %copy-start = (f32[4,512]{1,0:T(4,128)S(1)}, f32[4,512]{1,0:T(4,128)}, u32[]{:S(2)}) copy-start(f32[4,512]{1,0:T(4,128)} %gain_ref.5) | copy-start | bytes 24580
  12.5 10.3 %collective-permute-start.1 = (bf16[256,256]{1,0:T(8,128)(2,1)S(1)}, bf16[256,256]{1,0:T(8,128)(2,1)S(1)}, u32[]{:S(2)}, u32[]{:S(2)}) collective-permute-start(bf16[256,256]{1,0:T(8,128)(2,1)S(1)} %get-tuple-element.30), channel_id=1, source_target_pairs={{0,4},{4,0},{8,12},{12,8},{16,20},{20,16},{24,28},{28,24},{32,36},... | collective-permute-start | bytes 393224 | tf_op jit(solution)/shard_map/ppermute | solution.py:617
  13.3 18.7 %all-to-all-start = ((bf16[32,8,256]{2,1,0:T(8,128)(2,1)}), bf16[32,8,256]{2,1,0:T(8,128)(2,1)S(1)}, u32[]{:S(2)}, u32[]{:S(2)}) async-start(bf16[32,8,256]{2,1,0:T(8,128)(2,1)} %chip_sum.1), calls=%async_computation | async-start | bytes 262144 | tf_op jit(solution)/shard_map/all_to_all | solution.py:611
  33.3 14.5 %all-to-all-start.1 = ((bf16[32,16,256]{2,1,0:T(8,128)(2,1)}), bf16[32,16,256]{2,1,0:T(8,128)(2,1)S(1)}, u32[]{:S(2)}, u32[]{:S(2)}) async-start(bf16[32,16,256]{2,1,0:T(8,128)(2,1)} %scan_past.1), calls=%async_computation.1 | async-start | bytes 524288 | tf_op jit(solution)/shard_map/all_to_all | solution.py:611
  48.4 9.4 %collective-permute-start.2 = (bf16[256,256]{1,0:T(8,128)(2,1)S(1)}, bf16[256,256]{1,0:T(8,128)(2,1)S(1)}, u32[]{:S(2)}, u32[]{:S(2)}) collective-permute-start(bf16[256,256]{1,0:T(8,128)(2,1)S(1)} %get-tuple-element.32), channel_id=1, source_target_pairs={{0,4},{4,0},{8,12},{12,8},{16,20},{20,16},{24,28},{28,24},{32,36},... | collective-permute-start | bytes 393224 | tf_op jit(solution)/shard_map/ppermute | solution.py:617
  64.3 10.0 %collective-permute-start.3 = (bf16[128,1152]{1,0:T(8,128)(2,1)S(1)}, bf16[128,1152]{1,0:T(8,128)(2,1)S(1)}, u32[]{:S(2)}, u32[]{:S(2)}) collective-permute-start(bf16[128,1152]{1,0:T(8,128)(2,1)S(1)} %get-tuple-element.37), channel_id=1, source_target_pairs={{0,1},{1,2},{2,3},{3,0},{4,5},{5,6},{6,7},{7,4},{8,9},{9,10},{10,1... | collective-permute-start | bytes 884744 | tf_op jit(solution)/shard_map/ppermute | solution.py:622
  65.7 8.7 %collective-permute-start.7 = (bf16[128,1152]{1,0:T(8,128)(2,1)}, bf16[128,1152]{1,0:T(8,128)(2,1)S(1)}, u32[]{:S(2)}, u32[]{:S(2)}) collective-permute-start(bf16[128,1152]{1,0:T(8,128)(2,1)} %get-tuple-element.42), channel_id=1, source_target_pairs={{0,3},{1,0},{2,1},{3,2},{4,7},{5,4},{6,5},{7,6},{8,11},{9,8},{10,9... | collective-permute-start | bytes 884744 | tf_op jit(solution)/shard_map/ppermute | solution.py:622
  68.4 13.7 %all-to-all-start.2 = ((bf16[32,8,256]{2,1,0:T(8,128)(2,1)}), bf16[32,8,256]{2,1,0:T(8,128)(2,1)S(1)}, u32[]{:S(2)}, u32[]{:S(2)}) async-start(bf16[32,8,256]{2,1,0:T(8,128)(2,1)} %scan_future.1), calls=%async_computation.2 | async-start | bytes 262144 | tf_op jit(solution)/shard_map/all_to_all | solution.py:611
  72.5 19.4 %collective-permute-start.5 = (bf16[128,1152]{1,0:T(8,128)(2,1)}, bf16[128,1152]{1,0:T(8,128)(2,1)S(1)}, u32[]{:S(2)}, u32[]{:S(2)}) collective-permute-start(bf16[128,1152]{1,0:T(8,128)(2,1)} %get-tuple-element.38), channel_id=1, source_target_pairs={{0,3},{1,0},{2,1},{3,2},{4,7},{5,4},{6,5},{7,6},{8,11},{9,8},{10,9... | collective-permute-start | bytes 884744 | tf_op jit(solution)/shard_map/ppermute | solution.py:622
  73.9 18.0 %collective-permute-start.6 = (bf16[128,1152]{1,0:T(8,128)(2,1)}, bf16[128,1152]{1,0:T(8,128)(2,1)S(1)}, u32[]{:S(2)}, u32[]{:S(2)}) collective-permute-start(bf16[128,1152]{1,0:T(8,128)(2,1)} %get-tuple-element.40), channel_id=1, source_target_pairs={{0,1},{1,2},{2,3},{3,0},{4,5},{5,6},{6,7},{7,4},{8,9},{9,10},{10,1... | collective-permute-start | bytes 884744 | tf_op jit(solution)/shard_map/ppermute | solution.py:622
  74.3 17.6 %collective-permute-start.4 = (bf16[128,1152]{1,0:T(8,128)(2,1)S(1)}, bf16[128,1152]{1,0:T(8,128)(2,1)S(1)}, u32[]{:S(2)}, u32[]{:S(2)}) collective-permute-start(bf16[128,1152]{1,0:T(8,128)(2,1)S(1)} %added.2), channel_id=1, source_target_pairs={{0,1},{1,2},{2,3},{3,0},{4,5},{5,6},{6,7},{7,4},{8,9},{9,10},{10,1... | collective-permute-start | bytes 884744 | tf_op jit(solution)/shard_map/ppermute | solution.py:622
  74.5 17.5 %collective-permute-start.8 = (bf16[128,1152]{1,0:T(8,128)(2,1)S(1)}, bf16[128,1152]{1,0:T(8,128)(2,1)S(1)}, u32[]{:S(2)}, u32[]{:S(2)}) collective-permute-start(bf16[128,1152]{1,0:T(8,128)(2,1)S(1)} %added.3), channel_id=1, source_target_pairs={{0,3},{1,0},{2,1},{3,2},{4,7},{5,4},{6,5},{7,6},{8,11},{9,8},{10,9... | collective-permute-start | bytes 884744 | tf_op jit(solution)/shard_map/ppermute | solution.py:622
  82.8 5.0 %collective-permute-start.9 = (bf16[256,256]{1,0:T(8,128)(2,1)S(1)}, bf16[256,256]{1,0:T(8,128)(2,1)S(1)}, u32[]{:S(2)}, u32[]{:S(2)}) collective-permute-start(bf16[256,256]{1,0:T(8,128)(2,1)S(1)} %get-tuple-element.45), channel_id=1, source_target_pairs={{0,4},{4,0},{8,12},{12,8},{16,20},{20,16},{24,28},{28,24},{32,36},... | collective-permute-start | bytes 393224 | tf_op jit(solution)/shard_map/ppermute | solution.py:617
